TPU v7x, 128 devices: a whole 4x4x4 slice. The times are simulated.
128 devices in a mesh: col: 16 (over y, z_lo, core), row: 8 (over z_hi, x).
Axes of the slice: x: 4, y: 4, z: 4 (z_hi: 2, z_lo: 2; z = z_hi * 2 + z_lo), core: 2. Of those that a mesh axis runs over, the one named last changes fastest.
Arguments:
- valence: float32 [32, 64, 4096], P('row'), may hold values from -6 to 6
- conduction: float32 [64, 64, 4096], P('col'), may hold values from -6 to 6
- valence_energy: float32 [32], P('row'), may hold values from -10 to -0.5
- conduction_energy: float32 [64], P('col'), may hold values from 0.5 to 10
- pair_list: int32 [1024, 2], P(('col', 'row')), may hold values from 0 to 63, as said below
- sphere_index: int32 [16384], replicated, may hold values from 0 to 262143, as said below
Outputs:
- response: float32 [16384, 16384], P('row', 'col')
Inputs may be any that keep to these rules, and one draw needn't show every extreme that they name: `pair_list`: the 8 rows of the device with col index c and row index r (the block of rows that starts at (c * 8 + r) * 8) are distinct pairs, with valence index from r * 4 to (r + 1) * 4 - 1 and conduction index from c * 4 to (c + 1) * 4 - 1. `sphere_index`: distinct flat indices a * 64**2 + b * 64 + c of grid points.
All inputs are finite; a program needn't handle non-finite values.
Results may differ from a plain program's by a relative error of at most 0.004.
Values may be sent and summed in bfloat16 or wider, within the bound.
No kernel may reach another device: no remote copies, remote signals or barrier semaphores. Data moves between devices by JAX's collectives and lax.ppermute only.
A program may use at most 192 MiB of HBM per device.

v0:
```python
import math

import jax
import jax.numpy as jnp
from jax import lax
from jax.sharding import PartitionSpec as P


def dft_tables(grid_edge):
    counter = jnp.arange(grid_edge, dtype=jnp.int32)
    phases = (counter[:, None] * counter[None, :] % grid_edge).astype(jnp.float32) * (
        2.0 * math.pi / grid_edge
    )
    return (jnp.cos(phases), jnp.sin(phases))


def swap_halves(spectrum, half_width):
    return jnp.concatenate([spectrum[..., half_width:], -spectrum[..., :half_width]], axis=-1)


def grid_transform(samples):
    grid_edge = samples.shape[-1]
    cosine, sine_table = dft_tables(grid_edge)
    highest = lax.Precision.HIGHEST
    stacked = jnp.concatenate([cosine, -sine_table], axis=1)
    spectrum = jnp.einsum("pxyz,zk->pxyk", samples, stacked, precision=highest)
    spectrum = jnp.einsum("pxyk,yj->pxjk", spectrum, cosine, precision=highest) + swap_halves(
        jnp.einsum("pxyk,yj->pxjk", spectrum, sine_table, precision=highest), grid_edge
    )
    spectrum = jnp.einsum("pxyk,xj->pjyk", spectrum, cosine, precision=highest) + swap_halves(
        jnp.einsum("pxyk,xj->pjyk", spectrum, sine_table, precision=highest), grid_edge
    )
    return spectrum


def sphere_select(spectrum_rows, sphere_index, grid_edge):
    plane_waves = sphere_index.shape[0]
    block_width = min(2048, plane_waves)
    line_index = (sphere_index // grid_edge).reshape(plane_waves // block_width, block_width)
    point_index = (sphere_index % grid_edge).reshape(plane_waves // block_width, block_width)
    columns = jnp.arange(2 * grid_edge, dtype=jnp.int32)

    def one_block(indices):
        lines, points = indices
        chosen = jnp.take(spectrum_rows, lines, axis=1)
        real_part = jnp.sum(
            jnp.where(columns[None, None, :] == points[None, :, None], chosen, 0.0), axis=2
        )
        imag_part = jnp.sum(
            jnp.where(columns[None, None, :] == points[None, :, None] + grid_edge, chosen, 0.0),
            axis=2,
        )
        return jnp.stack([real_part, imag_part], axis=1)

    selected = lax.map(one_block, (line_index, point_index))
    return selected.transpose(1, 2, 0, 3).reshape(spectrum_rows.shape[0], 2, plane_waves)


def per_device(valence, conduction, valence_energy, conduction_energy, pair_list, sphere_index):
    val_count = valence.shape[0]
    con_count = conduction.shape[0]
    grid_edge = valence.shape[1]
    pair_count = pair_list.shape[0]
    n_row = lax.axis_size("row")
    n_col = lax.axis_size("col")
    total_pairs = pair_count * n_row * n_col
    valence_local = pair_list[:, 0] - lax.axis_index("row") * val_count
    conduction_local = pair_list[:, 1] - lax.axis_index("col") * con_count
    product = jnp.take(valence, valence_local, axis=0) * jnp.take(
        conduction, conduction_local, axis=0
    )
    spectrum = grid_transform(product.reshape(pair_count, grid_edge, grid_edge, grid_edge))
    spectrum_rows = spectrum.reshape(pair_count, grid_edge * grid_edge, 2 * grid_edge)
    density = sphere_select(spectrum_rows, sphere_index, grid_edge) * grid_edge ** (-1.5)
    energy_gap = jnp.take(conduction_energy, conduction_local) - jnp.take(
        valence_energy, valence_local
    )
    weight = -4.0 / (total_pairs * energy_gap)
    weighted = (weight[:, None, None] * density).astype(jnp.bfloat16)
    unweighted = density.astype(jnp.bfloat16)
    group_pairs = lax.all_gather(unweighted, "row", axis=0, tiled=True)
    right_all = lax.all_to_all(group_pairs, "col", split_axis=2, concat_axis=0, tiled=True)
    divided_left = lax.all_to_all(weighted, "row", split_axis=2, concat_axis=0, tiled=True)
    return jnp.einsum(
        "pkg,pkh->gh",
        lax.all_gather(divided_left, "col", axis=0, tiled=True),
        right_all,
        preferred_element_type=jnp.float32,
    )


def solution(mesh):
    return jax.shard_map(
        per_device,
        mesh=mesh,
        in_specs=(
            P("row", None, None),
            P("col", None, None),
            P("row"),
            P("col"),
            P(("col", "row"), None),
            P(),
        ),
        out_specs=P("row", "col"),
        check_vma=False,
    )
```

profile of v0, /device:TPU:0, one launch (start us, length us, event | category | flops | bytes accessed | tf_op | source)
XLA Modules:
  0.0 957.9 jit_solution(873171886327470696)
XLA Ops:
  66.0 22.0 %convolution_bitcast_fusion = f32[8,64,64,128]{3,2,1,0:T(8,128)} fusion(f32[8,64,64,128]{3,2,1,0:T(8,128)} %fusion.17), kind=kOutput, calls=%fused_computation.28 | convolution fusion | flops 3221282816 | bytes 33554432 | tf_op jit(solution)/shard_map/pxyk,yj->pxjk/dot_general | solution.py:28
  87.9 24.4 %fusion.53 = (f32[8,64,64,64]{3,2,1,0:T(8,128)}, f32[8,64,64,64]{3,2,1,0:T(8,128)}) fusion(f32[8,64,64,128]{3,2,1,0:T(8,128)} %convolution_bitcast_fusion), kind=kLoop, calls=%fused_computation.88 | loop fusion | flops 2097152 | bytes 33554432 | tf_op jit(solution)/shard_map/slice | solution.py:18
  112.4 31.4 %maximum_add_fusion = f32[8,64,64,128]{3,2,1,0:T(8,128)} fusion(f32[8,64,64,64]{3,2,1,0:T(8,128)} %get-tuple-element.109, f32[8,64,64,64]{3,2,1,0:T(8,128)} %get-tuple-element.108, f32[8,64,64,128]{3,2,1,0:T(8,128)} %fusion.17), kind=kOutput, calls=%fused_computation.21 | convolution fusion | flops 3229671424 | bytes 50331648 | tf_op jit(solution)/shard_map/pxyk,yj->pxjk/dot_general | solution.py:27
  143.7 33.4 %fusion.9 = f32[8,64,64,128]{3,1,2,0:T(8,128)} fusion(f32[8,64,64,128]{3,2,1,0:T(8,128)} %maximum_add_fusion), kind=kOutput, calls=%fused_computation.27 | convolution fusion | flops 3221282816 | bytes 33554432 | tf_op jit(solution)/shard_map/pxyk,xj->pjyk/dot_general | solution.py:31
  177.2 24.7 %fusion.52 = (f32[8,64,64,64]{3,1,2,0:T(8,128)}, f32[8,64,64,64]{3,1,2,0:T(8,128)}) fusion(f32[8,64,64,128]{3,1,2,0:T(8,128)} %fusion.9), kind=kLoop, calls=%fused_computation.87 | loop fusion | flops 2097152 | bytes 33554432 | tf_op jit(solution)/shard_map/slice | solution.py:18
  201.9 33.7 %maximum_add_fusion.1 = f32[8,64,64,128]{3,1,2,0:T(8,128)} fusion(f32[8,64,64,64]{3,1,2,0:T(8,128)} %get-tuple-element.107, f32[8,64,64,64]{3,1,2,0:T(8,128)} %get-tuple-element.106, f32[8,64,64,128]{3,2,1,0:T(8,128)S(1)} %bitcast.86), kind=kOutput, calls=%fused_computation.22 | convolution fusion | flops 3229671424 | bytes 50331648 | tf_op jit(solution)/shard_map/pxyk,xj->pjyk/dot_general | solution.py:30
  250.8 24.0 %copy.48 = f32[8,4096,128]{2,0,1:T(8,128)} copy(f32[8,4096,128]{2,1,0:T(8,128)S(1)} %bitcast.89) | data formatting | bytes 33554432
  274.9 452.8 %while.12 = (s32[]{:T(128)}, f32[8,8,2,2048]{3,1,2,0:T(8,128)}, s32[8,2048]{1,0:T(8,128)S(1)}, s32[8,2048]{1,0:T(8,128)S(1)}, f32[8,4096,128]{2,0,1:T(8,128)}, /*index=5*/s32[]{:T(128)}) while((s32[]{:T(128)}, f32[8,8,2,2048]{3,1,2,0:T(8,128)}, s32[8,2048]{1,0:T(8,128)S(1)}, s32[8,2048]{1,0:T(8,128)S(1)}, ...), condition=%wide.region_3.5_spmd.clone.clone, body=%wide.region_0.4_spmd.clone.clone.sunk | while | flops 11032578 | bytes 26980940 | solution.py:55
  276.3 21.4 %gather_fusion = f32[2048,8,128]{2,1,0:T(8,128)} fusion(f32[8,4096,128]{2,0,1:T(8,128)} %get-tuple-element.179, s32[2048]{0:T(1024)S(1)} %broadcast_clamp_fusion.2), kind=kCustom, calls=%fused_computation.2.clone.clone.1 | custom fusion | bytes 16785408 | tf_op jit(solution)/shard_map/while/body/eval_jaxpr/jit(_take)/gather | solution.py:45
  297.6 32.6 %select_reduce_fusion.3 = (f32[2048,8]{1,0:T(8,128)S(1)}, f32[2048,8]{1,0:T(8,128)S(1)}) fusion(f32[2048,8,128]{2,1,0:T(8,128)} %gather_fusion, pred[2048]{0:T(1024)(128)(4,1)S(1)} %compare_and_fusion.4, pred[2048,128]{1,0:T(8,128)(4,1)S(1)} %get-tuple-element.159, pred[2048,128]{1,0:T(8,128)(4,1)S(1)} %get-tuple-element.160), kind=kLoop, calls=%fused_computation.7.clone.1 | loop fusion | flops 10452992 | bytes 9046016 | tf_op jit(solution)/shard_map/while/body/eval_jaxpr/reduce_sum | solution.py:46
  332.9 21.4 %gather_fusion = f32[2048,8,128]{2,1,0:T(8,128)} fusion(f32[8,4096,128]{2,0,1:T(8,128)} %get-tuple-element.179, s32[2048]{0:T(1024)S(1)} %broadcast_clamp_fusion.2), kind=kCustom, calls=%fused_computation.2.clone.clone.1 | custom fusion | bytes 16785408 | tf_op jit(solution)/shard_map/while/body/eval_jaxpr/jit(_take)/gather | solution.py:45
  354.2 32.6 %select_reduce_fusion.3 = (f32[2048,8]{1,0:T(8,128)S(1)}, f32[2048,8]{1,0:T(8,128)S(1)}) fusion(f32[2048,8,128]{2,1,0:T(8,128)} %gather_fusion, pred[2048]{0:T(1024)(128)(4,1)S(1)} %compare_and_fusion.4, pred[2048,128]{1,0:T(8,128)(4,1)S(1)} %get-tuple-element.159, pred[2048,128]{1,0:T(8,128)(4,1)S(1)} %get-tuple-element.160), kind=kLoop, calls=%fused_computation.7.clone.1 | loop fusion | flops 10452992 | bytes 9046016 | tf_op jit(solution)/shard_map/while/body/eval_jaxpr/reduce_sum | solution.py:46
  389.4 21.4 %gather_fusion = f32[2048,8,128]{2,1,0:T(8,128)} fusion(f32[8,4096,128]{2,0,1:T(8,128)} %get-tuple-element.179, s32[2048]{0:T(1024)S(1)} %broadcast_clamp_fusion.2), kind=kCustom, calls=%fused_computation.2.clone.clone.1 | custom fusion | bytes 16785408 | tf_op jit(solution)/shard_map/while/body/eval_jaxpr/jit(_take)/gather | solution.py:45
  410.8 32.6 %select_reduce_fusion.3 = (f32[2048,8]{1,0:T(8,128)S(1)}, f32[2048,8]{1,0:T(8,128)S(1)}) fusion(f32[2048,8,128]{2,1,0:T(8,128)} %gather_fusion, pred[2048]{0:T(1024)(128)(4,1)S(1)} %compare_and_fusion.4, pred[2048,128]{1,0:T(8,128)(4,1)S(1)} %get-tuple-element.159, pred[2048,128]{1,0:T(8,128)(4,1)S(1)} %get-tuple-element.160), kind=kLoop, calls=%fused_computation.7.clone.1 | loop fusion | flops 10452992 | bytes 9046016 | tf_op jit(solution)/shard_map/while/body/eval_jaxpr/reduce_sum | solution.py:46
  446.0 21.4 %gather_fusion = f32[2048,8,128]{2,1,0:T(8,128)} fusion(f32[8,4096,128]{2,0,1:T(8,128)} %get-tuple-element.179, s32[2048]{0:T(1024)S(1)} %broadcast_clamp_fusion.2), kind=kCustom, calls=%fused_computation.2.clone.clone.1 | custom fusion | bytes 16785408 | tf_op jit(solution)/shard_map/while/body/eval_jaxpr/jit(_take)/gather | solution.py:45
  467.4 32.6 %select_reduce_fusion.3 = (f32[2048,8]{1,0:T(8,128)S(1)}, f32[2048,8]{1,0:T(8,128)S(1)}) fusion(f32[2048,8,128]{2,1,0:T(8,128)} %gather_fusion, pred[2048]{0:T(1024)(128)(4,1)S(1)} %compare_and_fusion.4, pred[2048,128]{1,0:T(8,128)(4,1)S(1)} %get-tuple-element.159, pred[2048,128]{1,0:T(8,128)(4,1)S(1)} %get-tuple-element.160), kind=kLoop, calls=%fused_computation.7.clone.1 | loop fusion | flops 10452992 | bytes 9046016 | tf_op jit(solution)/shard_map/while/body/eval_jaxpr/reduce_sum | solution.py:46
  502.7 21.4 %gather_fusion = f32[2048,8,128]{2,1,0:T(8,128)} fusion(f32[8,4096,128]{2,0,1:T(8,128)} %get-tuple-element.179, s32[2048]{0:T(1024)S(1)} %broadcast_clamp_fusion.2), kind=kCustom, calls=%fused_computation.2.clone.clone.1 | custom fusion | bytes 16785408 | tf_op jit(solution)/shard_map/while/body/eval_jaxpr/jit(_take)/gather | solution.py:45
  524.0 32.6 %select_reduce_fusion.3 = (f32[2048,8]{1,0:T(8,128)S(1)}, f32[2048,8]{1,0:T(8,128)S(1)}) fusion(f32[2048,8,128]{2,1,0:T(8,128)} %gather_fusion, pred[2048]{0:T(1024)(128)(4,1)S(1)} %compare_and_fusion.4, pred[2048,128]{1,0:T(8,128)(4,1)S(1)} %get-tuple-element.159, pred[2048,128]{1,0:T(8,128)(4,1)S(1)} %get-tuple-element.160), kind=kLoop, calls=%fused_computation.7.clone.1 | loop fusion | flops 10452992 | bytes 9046016 | tf_op jit(solution)/shard_map/while/body/eval_jaxpr/reduce_sum | solution.py:46
  559.3 21.4 %gather_fusion = f32[2048,8,128]{2,1,0:T(8,128)} fusion(f32[8,4096,128]{2,0,1:T(8,128)} %get-tuple-element.179, s32[2048]{0:T(1024)S(1)} %broadcast_clamp_fusion.2), kind=kCustom, calls=%fused_computation.2.clone.clone.1 | custom fusion | bytes 16785408 | tf_op jit(solution)/shard_map/while/body/eval_jaxpr/jit(_take)/gather | solution.py:45
  580.6 32.6 %select_reduce_fusion.3 = (f32[2048,8]{1,0:T(8,128)S(1)}, f32[2048,8]{1,0:T(8,128)S(1)}) fusion(f32[2048,8,128]{2,1,0:T(8,128)} %gather_fusion, pred[2048]{0:T(1024)(128)(4,1)S(1)} %compare_and_fusion.4, pred[2048,128]{1,0:T(8,128)(4,1)S(1)} %get-tuple-element.159, pred[2048,128]{1,0:T(8,128)(4,1)S(1)} %get-tuple-element.160), kind=kLoop, calls=%fused_computation.7.clone.1 | loop fusion | flops 10452992 | bytes 9046016 | tf_op jit(solution)/shard_map/while/body/eval_jaxpr/reduce_sum | solution.py:46
  637.2 32.6 %select_reduce_fusion.3 = (f32[2048,8]{1,0:T(8,128)S(1)}, f32[2048,8]{1,0:T(8,128)S(1)}) fusion(f32[2048,8,128]{2,1,0:T(8,128)} %gather_fusion, pred[2048]{0:T(1024)(128)(4,1)S(1)} %compare_and_fusion.4, pred[2048,128]{1,0:T(8,128)(4,1)S(1)} %get-tuple-element.159, pred[2048,128]{1,0:T(8,128)(4,1)S(1)} %get-tuple-element.160), kind=kLoop, calls=%fused_computation.7.clone.1 | loop fusion | flops 10452992 | bytes 9046016 | tf_op jit(solution)/shard_map/while/body/eval_jaxpr/reduce_sum | solution.py:46
  672.4 21.4 %gather_fusion = f32[2048,8,128]{2,1,0:T(8,128)} fusion(f32[8,4096,128]{2,0,1:T(8,128)} %get-tuple-element.179, s32[2048]{0:T(1024)S(1)} %broadcast_clamp_fusion.2), kind=kCustom, calls=%fused_computation.2.clone.clone.1 | custom fusion | bytes 16785408 | tf_op jit(solution)/shard_map/while/body/eval_jaxpr/jit(_take)/gather | solution.py:45
  693.8 32.6 %select_reduce_fusion.3 = (f32[2048,8]{1,0:T(8,128)S(1)}, f32[2048,8]{1,0:T(8,128)S(1)}) fusion(f32[2048,8,128]{2,1,0:T(8,128)} %gather_fusion, pred[2048]{0:T(1024)(128)(4,1)S(1)} %compare_and_fusion.4, pred[2048,128]{1,0:T(8,128)(4,1)S(1)} %get-tuple-element.159, pred[2048,128]{1,0:T(8,128)(4,1)S(1)} %get-tuple-element.160), kind=kLoop, calls=%fused_computation.7.clone.1 | loop fusion | flops 10452992 | bytes 9046016 | tf_op jit(solution)/shard_map/while/body/eval_jaxpr/reduce_sum | solution.py:46
  838.2 64.3 %all_to_all.37 = bf16[16,2,65536]{2,1,0:T(2,128)(2,1)} all-to-all(bf16[16,2,65536]{2,1,0:T(2,128)(2,1)} %reshape.203), channel_id=1, replica_groups=mesh['col'=16,'row'=8] {'col'}, dimensions={0} | all-to-all | bytes 8388608 | tf_op jit(solution)/shard_map/all_to_all | solution.py:82
  (134 shorter events, 275.3 us)
Async XLA Ops:
  6.5 722.5 %copy-start = (f32[4]{0:T(128)S(1)}, f32[4]{0:T(128)}, u32[]{:S(2)}) copy-start(f32[4]{0:T(128)} %param.15) | copy-start | bytes 52
  6.5 799.7 %all-gather.5.cloned.1.call-start = ((), (), s32[]{:S(2)}) async-start(), calls=%async_computation.3 | async-start | bytes 4718592 | tf_op jit(solution)/shard_map/all_gather | solution.py:81
  7.5 0.6 copy-start.5
  7.5 0.6 copy-start.7
  8.1 13.2 %copy-start.3 = (s32[1024]{0:T(1024)}, s32[1024]{0:T(1024)S(1)}, u32[]{:S(2)}) copy-start(s32[1024]{0:T(1024)S(1)} %get-tuple-element.117) | copy-start | bytes 12292
  8.1 13.2 %copy-start.4 = (s32[1024]{0:T(1024)}, s32[1024]{0:T(1024)S(1)}, u32[]{:S(2)}) copy-start(s32[1024]{0:T(1024)S(1)} %get-tuple-element.116) | copy-start | bytes 12292
  143.7 58.1 %slice-start = ((s8[16777216]{0:T(1024)(128)(4,1)}), s8[4194304]{0:T(1024)(128)(4,1)S(1)}, s32[]{:S(2)}) async-start(s8[16777216]{0:T(1024)(128)(4,1)} %bitcast.85), calls=%async_computation.4 | async-start | bytes 8388608
  143.7 58.1 %slice-start.1 = ((s8[16777216]{0:T(1024)(128)(4,1)}), s8[4194304]{0:T(1024)(128)(4,1)S(1)}, s32[]{:S(2)}) async-start(s8[16777216]{0:T(1024)(128)(4,1)} %bitcast.85), calls=%async_computation.5 | async-start | bytes 8388608
  177.1 24.7 %slice-start.2 = ((s8[16777216]{0:T(1024)(128)(4,1)}), s8[4194304]{0:T(1024)(128)(4,1)S(1)}, s32[]{:S(2)}) async-start(s8[16777216]{0:T(1024)(128)(4,1)} %bitcast.85), calls=%async_computation.6 | async-start | bytes 8388608
  177.1 24.7 %slice-start.3 = ((s8[16777216]{0:T(1024)(128)(4,1)}), s8[4194304]{0:T(1024)(128)(4,1)S(1)}, s32[]{:S(2)}) async-start(s8[16777216]{0:T(1024)(128)(4,1)} %bitcast.85), calls=%async_computation.7 | async-start | bytes 8388608
  250.8 24.0 %copy-start.2 = (s32[16384]{0:T(1024)S(1)}, s32[16384]{0:T(1024)}, u32[]{:S(2)}) copy-start(s32[16384]{0:T(1024)} %param.17) | copy-start | bytes 196612
  274.9 454.9 %copy-start.1 = (f32[4]{0:T(128)S(1)}, f32[4]{0:T(128)}, u32[]{:S(2)}) copy-start(f32[4]{0:T(128)} %param.14) | copy-start | bytes 52
  274.9 455.7 %copy-start.6 = (s32[8]{0:T(128)S(1)}, s32[8]{0:T(128)}, u32[]{:S(2)}) copy-start(s32[8]{0:T(128)} %copy-done.5) | copy-start | bytes 100
  274.9 455.7 %copy-start.8 = (s32[8]{0:T(128)S(1)}, s32[8]{0:T(128)}, u32[]{:S(2)}) copy-start(s32[8]{0:T(128)} %copy-done.7) | copy-start | bytes 100
  731.6 204.7 %all-gather.3.cloned.1.call-start = ((), (), s32[]{:S(2)}) async-start(), calls=%async_computation.2 | async-start | bytes 8912896 | tf_op jit(solution)/shard_map/all_gather | solution.py:86
Sparse Core Ops, SparseCore 0:
  731.7 74.5 all-gather.4
  807.9 91.3 all-gather.2
where the time goes:
time: 968 us; the launch traced here: 958 us
  local copies, waits for them, and re-layouts  365 us (38%)
  other arithmetic  340 us (35%)
  matrix products  154 us (16%)
  blocking collectives  83.7 us (9%)
  between operations  13.8 us (1%)
    reduce_sum x8, other arithmetic, one_block(): jnp.sum(jnp.where(columns[None, None, :] == points[None, :, None], chosen...  261 us
    gather x8, local copies, waits for them, and re-layouts, one_block(): chosen = jnp.take(spectrum_rows, lines, axis=1)  171 us
    unnamed x31, local copies, waits for them, and re-layouts  73.7 us
    all_to_all x1, blocking collectives, per_device(): lax.all_to_all(group_pairs, 'col', split_axis=2, concat_axis=0, tiled=True)  64.3 us
    slice x2, other arithmetic, swap_halves(): spectrum[..., half_width:]  49.1 us
    dot_general x1, matrix products, grid_transform(): jnp.einsum('pxyk,xj->pjyk', spectrum, cosine, precision=highest)  33.7 us
    dot_general x1, matrix products, grid_transform(): jnp.einsum('pxyk,xj->pjyk', spectrum, sine_table, precision=highest)  33.4 us
    dot_general x1, matrix products, grid_transform(): jnp.einsum('pxyk,yj->pxjk', spectrum, cosine, precision=highest)  31.4 us
  transfers between devices with their start and end apart: 2, of which 1 were waited for; matrix products, arithmetic and copies ran while one was open for 12% of the time, Pallas kernels for 0%

commit v1 on v0

v1 whole, which is shorter than its diff:
```python
import math

import jax
import jax.numpy as jnp
import numpy as np
from jax import lax
from jax.experimental import pallas as pl
from jax.experimental.pallas import tpu as pltpu
from jax.sharding import PartitionSpec as P

EDGE = 64
HALF = EDGE // 2
LANES = 128
BF = jnp.bfloat16
F32 = jnp.float32


def two_terms(table):
    high = table.astype(np.float32).astype(BF)
    low = (table - high.astype(np.float64)).astype(BF)
    return np.asarray(high), np.asarray(low)


def x_table():
    x = np.arange(EDGE)
    a = np.arange(HALF)
    angle = 2.0 * np.pi * ((a[:, None] * x[None, :]) % EDGE) / EDGE
    table = np.concatenate([np.cos(angle), -np.sin(angle)], axis=0)
    table[HALF] = 1.0 - 2.0 * (x % 2)
    high, low = two_terms(table)
    return np.concatenate([high, high, low], axis=1)


def z_table():
    z = np.arange(EDGE)
    angle = 2.0 * np.pi * ((z[:, None] * z[None, :]) % EDGE) / EDGE
    cosine, sine = np.cos(angle), np.sin(angle)
    table = np.block([[cosine, -sine], [sine, cosine]]) * EDGE ** (-1.5)
    high, low = two_terms(table)
    return np.block([[high, low], [high, np.zeros_like(low)]]).astype(BF)


def y_table():
    angle = 2.0 * np.pi * np.arange(HALF) / EDGE
    odd = np.arange(LANES)[None, :] >= EDGE
    real = np.where(odd, np.cos(angle)[:, None], 1.0)
    imag = np.where(odd, -np.sin(angle)[:, None], 0.0)
    return np.concatenate([real, imag], axis=0).astype(np.float32)


def small_dft(re, im):
    n = len(re)
    if n == 1:
        return re, im
    even_re, even_im = small_dft(re[0::2], im[0::2])
    odd_re, odd_im = small_dft(re[1::2], im[1::2])
    out_re, out_im = [None] * n, [None] * n
    for k in range(n // 2):
        r, i = odd_re[k], odd_im[k]
        if k == 0:
            pass
        elif 4 * k == n:
            r, i = i, -r
        elif 8 * k == n:
            s = math.sqrt(0.5)
            r, i = (r + i) * s, (i - r) * s
        elif 8 * k == 3 * n:
            s = math.sqrt(0.5)
            r, i = (i - r) * s, (r + i) * -s
        else:
            c, s = math.cos(2 * math.pi * k / n), math.sin(2 * math.pi * k / n)
            r, i = r * c + i * s, i * c - r * s
        out_re[k], out_im[k] = even_re[k] + r, even_im[k] + i
        out_re[k + n // 2], out_im[k + n // 2] = even_re[k] - r, even_im[k] - i
    return out_re, out_im


def split(value):
    high = value.astype(BF)
    return high, (value - high.astype(F32)).astype(BF)


def density_kernel(
    pairs,
    lines,
    valence,
    conduction,
    weight,
    point,
    wave,
    x_factors,
    z_factors,
    y_factors,
    left,
    right,
    staged,
    table,
):
    n_pairs = 8
    wide = 2 * LANES

    def x_stage(chunk, carry):
        lanes = pl.ds(pl.multiple_of(chunk * wide, wide), wide)
        for p in range(n_pairs):
            product = valence[pairs[2 * p], :, lanes] * conduction[pairs[2 * p + 1], :, lanes]
            high, low = split(product)
            spectrum = jnp.dot(
                x_factors[...],
                jnp.concatenate([high, low, high], axis=0),
                preferred_element_type=F32,
            )
            for h in range(2):
                staged[2 * chunk + h, pl.ds(p * EDGE, EDGE), :] = spectrum[:, h * LANES : (h + 1) * LANES]
        return carry

    lax.fori_loop(0, EDGE * EDGE // wide, x_stage, 0)

    first = lax.broadcasted_iota(jnp.int32, (8, LANES), 1) < EDGE

    def yz_stage(a, carry):
        re = [staged[y, pl.ds(a, 8, stride=EDGE), :] for y in range(HALF)]
        im = [staged[y, pl.ds(a + HALF, 8, stride=EDGE), :] for y in range(HALF)]
        re, im = small_dft(re, im)
        lower, upper = [], []
        for b in range(HALF):
            r, i = re[b], im[b]
            if b:
                c = y_factors[pl.ds(b, 8, stride=0), :]
                s = y_factors[pl.ds(b + HALF, 8, stride=0), :]
                r, i = r * c - i * s, r * s + i * c
            even = jnp.where(first, r, pltpu.roll(i, EDGE, 1))
            odd = jnp.where(first, pltpu.roll(r, EDGE, 1), i)
            lower.append(even + odd)
            upper.append(even - odd)
        high, low = split(jnp.concatenate(lower + upper, axis=0))
        out = jnp.dot(
            jnp.concatenate([high, low], axis=1), z_factors[...], preferred_element_type=F32
        )
        out = out[:, :LANES] + out[:, LANES:]
        table[pl.ds(a * EDGE, EDGE)] = out.reshape(EDGE, 8, LANES)
        return carry

    lax.fori_loop(0, HALF, yz_stage, 0)

    lane = lax.broadcasted_iota(jnp.int32, (8, LANES), 1)
    mirror = (lane & EDGE) | ((EDGE - lane) & (EDGE - 1))

    def one_line(b):
        return table[b], jnp.take_along_axis(table[(EDGE - b) & (EDGE - 1)], mirror, axis=1)

    def store_line(b, here, there):
        total, delta = 0.5 * (here + there), 0.5 * (here - there)
        swapped_total, swapped_delta = pltpu.roll(total, EDGE, 1), pltpu.roll(delta, EDGE, 1)
        table[b] = jnp.where(first, total, delta)
        table[HALF * EDGE + b] = jnp.where(first, swapped_total, -swapped_delta)

    for b in range(HALF + 1):
        mine = one_line(b)
        other = (EDGE - b) & (EDGE - 1)
        if other != b:
            theirs = one_line(other)
            store_line(other, *theirs)
        store_line(b, *mine)

    per_row, per_col = left.shape[2] // LANES, right.shape[2] // LANES
    slot = lane & (EDGE - 1)
    w = weight[...]

    def select(q, carry):
        parts = []
        for h in range(2):
            index = point[pl.ds(2 * q + h, 8, stride=0), :]
            c = jnp.where(index >= (HALF + 1) * EDGE * EDGE, EDGE - index, index) & (EDGE - 1)
            take = c + jnp.where(first, h * EDGE, EDGE - h * EDGE)
            picked = jnp.zeros((8, LANES), F32)
            for j in range(EDGE):
                tile = table[lines[q * LANES + h * EDGE + j]]
                picked = jnp.where(slot == j, jnp.take_along_axis(tile, take, axis=1), picked)
            parts.append(picked)
        re = jnp.where(first, parts[0], parts[1])
        im = pltpu.roll(jnp.where(first, parts[1], parts[0]), EDGE, 1)
        index = wave[pl.ds(q, 8, stride=0), :]
        im = jnp.where(index >= (HALF + 1) * EDGE * EDGE, -im, im)
        plain = jnp.concatenate([re, im], axis=0).astype(BF)
        scaled = jnp.concatenate([w * re, w * im], axis=0).astype(BF)
        at = pl.multiple_of((q % per_row) * LANES, LANES)
        left[q // per_row, :, pl.ds(at, LANES)] = scaled
        at = pl.multiple_of((q % per_col) * LANES, LANES)
        right[q // per_col, :, pl.ds(at, LANES)] = plain
        return carry

    lax.fori_loop(0, wave.shape[0], select, 0)


def densities(n_row, n_col, valence, conduction, valence_energy, conduction_energy, pair_list, sphere_index):
    n_pairs, waves = pair_list.shape[0], sphere_index.shape[0]
    total_pairs = n_pairs * n_row * n_col
    v = pair_list[:, 0] - lax.axis_index("row") * valence.shape[0]
    c = pair_list[:, 1] - lax.axis_index("col") * conduction.shape[0]
    v_hot = v[:, None] == jnp.arange(valence.shape[0])[None, :]
    c_hot = c[:, None] == jnp.arange(conduction.shape[0])[None, :]
    gap = jnp.sum(jnp.where(c_hot, conduction_energy[None, :], 0.0), axis=1) - jnp.sum(
        jnp.where(v_hot, valence_energy[None, :], 0.0), axis=1
    )
    weight = jnp.broadcast_to((-4.0 / (total_pairs * gap))[:, None], (n_pairs, LANES))
    mirrored = sphere_index >= (HALF + 1) * EDGE * EDGE
    a, b = sphere_index // (EDGE * EDGE), (sphere_index // EDGE) % EDGE
    a = jnp.where(mirrored, EDGE - a, a)
    b = jnp.where(mirrored, (EDGE - b) % EDGE, b)
    lines = a * EDGE + b
    halves = sphere_index.reshape(-1, EDGE)
    smem = pl.BlockSpec(memory_space=pltpu.SMEM)
    vmem = pl.BlockSpec(memory_space=pltpu.VMEM)
    return pl.pallas_call(
        density_kernel,
        in_specs=[smem, smem] + [vmem] * 8,
        out_specs=[vmem, vmem],
        out_shape=[
            jax.ShapeDtypeStruct((n_row, 2 * n_pairs, waves // n_row), BF),
            jax.ShapeDtypeStruct((n_col, 2 * n_pairs, waves // n_col), BF),
        ],
        scratch_shapes=[
            pltpu.VMEM((HALF, n_pairs * EDGE, LANES), F32),
            pltpu.VMEM(((HALF + 1) * EDGE, 8, LANES), F32),
        ],
        compiler_params=pltpu.CompilerParams(vmem_limit_bytes=48 * 1024 * 1024),
        name="density",
    )(
        jnp.stack([v, c], axis=1).reshape(-1),
        lines,
        valence,
        conduction,
        weight,
        jnp.concatenate([halves, halves], axis=1),
        sphere_index.reshape(-1, LANES),
        jnp.asarray(x_table()),
        jnp.asarray(z_table()),
        jnp.asarray(y_table()),
    )


def per_device(valence, conduction, valence_energy, conduction_energy, pair_list, sphere_index):
    n_row, n_col = lax.axis_size("row"), lax.axis_size("col")
    left, right = densities(
        n_row, n_col, valence, conduction, valence_energy, conduction_energy, pair_list, sphere_index
    )
    left = lax.all_to_all(left, "row", split_axis=0, concat_axis=0, tiled=True)
    right = lax.all_to_all(right, "col", split_axis=0, concat_axis=0, tiled=True)
    left = lax.all_gather(left, "col", axis=0, tiled=False)
    right = lax.all_gather(right, "row", axis=0, tiled=False)
    return jnp.einsum("crkg,rckh->gh", left, right, preferred_element_type=F32)


def solution(mesh):
    return jax.shard_map(
        per_device,
        mesh=mesh,
        in_specs=(
            P("row", None, None),
            P("col", None, None),
            P("row"),
            P("col"),
            P(("col", "row"), None),
            P(),
        ),
        out_specs=P("row", "col"),
        check_vma=False,
    )
```

time: 968 us -> 242 us (0.25)
  local copies, waits for them, and re-layouts: 365 us -> 6.61 us
  other arithmetic: 340 us -> 2.62 us
  matrix products: 154 us -> 14.6 us
  waiting for transfers between devices: 2.04 us -> 103 us
  Pallas kernels: 0 us -> 62.6 us
  blocking collectives: 83.7 us -> 36.8 us
    reduce_sum x8 -> x1, other arithmetic: 261 us -> 0.76 us  [densities(): jnp.sum(jnp.where(v_hot, valence_energy[None, :], 0.0), axis=1)]
    gather x12 -> x0, local copies, waits for them, and re-layouts: 186 us -> none  [the longest x8 171 us: one_block(): chosen = jnp.take(spectrum_rows, lines, axis=1)]
    dot_general x6 -> x1, matrix products: 154 us -> 14.6 us  [per_device(): return jnp.einsum('crkg,rckh->gh', left, right, preferred_element_type=F32)]
    all_gather x2, waiting for transfers between devices: 2.01 us -> 103 us  [the longest x1 51.6 us: per_device(): left = lax.all_gather(left, 'col', axis=0, tiled=False)]
    unnamed x31 -> x10, local copies, waits for them, and re-layouts: 73.7 us -> 5.45 us
    pallas_call x0 -> x1, Pallas kernels: none -> 62.6 us  [densities(): pl.pallas_call(density_kernel, in_specs=[smem, smem] + [vmem] * 8, out_sp...]
    slice x2 -> x0, other arithmetic: 49.1 us -> none  [swap_halves(): spectrum[..., half_width:]]
    all_to_all x2, blocking collectives: 83.7 us -> 36.8 us  [the longest x1 20.1 us: per_device(): left = lax.all_to_all(left, 'row', split_axis=0, concat_axis=0, tiled=True)]
  transfers between devices with their start and end apart: 2 -> 2, of which waited for: 1 -> 2; matrix products, arithmetic and copies ran while one was open for 12% -> 0% of each run, Pallas kernels for 0% -> 0%
where the time goes in v1:
time: 242 us; the launch traced here: 240 us
  waiting for transfers between devices  103 us (43%)
  Pallas kernels  62.6 us (26%)
  blocking collectives  36.8 us (15%)
  matrix products  14.6 us (6%)
  between operations  13.4 us (6%)
  local copies, waits for them, and re-layouts  6.61 us (3%)
  other arithmetic  2.62 us (1%)
    pallas_call x1, Pallas kernels, densities(): pl.pallas_call(density_kernel, in_specs=[smem, smem] + [vmem] * 8, out_sp...  62.6 us
    all_gather x1, waiting for transfers between devices, per_device(): left = lax.all_gather(left, 'col', axis=0, tiled=False)  51.6 us
    all_gather x1, waiting for transfers between devices, per_device(): right = lax.all_gather(right, 'row', axis=0, tiled=False)  51.3 us
    all_to_all x1, blocking collectives, per_device(): left = lax.all_to_all(left, 'row', split_axis=0, concat_axis=0, tiled=True)  20.1 us
    all_to_all x1, blocking collectives, per_device(): lax.all_to_all(right, 'col', split_axis=0, concat_axis=0, tiled=True)  16.8 us
    dot_general x1, matrix products, per_device(): return jnp.einsum('crkg,rckh->gh', left, right, preferred_element_type=F32)  14.6 us
    unnamed x10, local copies, waits for them, and re-layouts  5.45 us
  transfers between devices with their start and end apart: 2, of which 2 were waited for; matrix products, arithmetic and copies ran while one was open for 0% of the time, Pallas kernels for 0%

profile of v1, /device:TPU:0, one launch (start us, length us, event | category | flops | bytes accessed | tf_op | source)
XLA Modules:
  0.0 239.8 jit_solution(8322443532644486917)
XLA Ops:
  6.5 0.0 all-gather.7.cloned.1.call-start
  6.5 1.0 fusion.3.lines
  7.5 0.9 reshape.19
  8.4 0.8 slice_subtract_fusion.1
  9.2 0.1 copy.17
  9.3 0.1 reshape.18.pairs
  9.4 0.1 pad_add_fusion.point
  9.5 0.8 select_reduce_fusion
  10.3 0.1 broadcast_in_dim.33.weight
  10.3 0.0 copy-start
  10.3 2.2 copy-done
  12.5 0.8 copy-done.1
  13.4 0.9 copy-done.2
  14.3 0.8 copy-done.3
  15.0 0.8 copy-done.4
  15.8 62.6 %density.1 = (bf16[8,16,2048]{2,1,0:T(8,128)(2,1)S(1)}, bf16[16,16,1024]{2,1,0:T(8,128)(2,1)S(1)}) custom-call(s32[16]{0:T(128)S(1)} %reshape.18.pairs, s32[16384]{0:T(1024)S(1)} %fusion.3.lines, f32[4,64,4096]{2,1,0:T(8,128)S(1)} %copy-done, f32[4,64,4096]{2,1,0:T(8,128)} %conduction.1, f32[8,128]{1,0:T(8,128)S(1)} %broadcast_in_dim.33.weight, ...), custom_call_target="tpu_custom_call" | custom-call | tf_op jit(solution)/shard_map/density/pallas_call | solution.py:214
  78.4 16.8 %all_to_all.10 = bf16[16,16,1024]{2,1,0:T(8,128)(2,1)} all-to-all(bf16[16,16,1024]{2,1,0:T(8,128)(2,1)S(1)} %get-tuple-element.8), channel_id=1, replica_groups=mesh['col'=16,'row'=8] {'col'}, dimensions={0} | all-to-all | bytes 1048576 | tf_op jit(solution)/shard_map/all_to_all | solution.py:248
  95.2 0.0 all-gather.7.cloned.1.call-update
  95.2 0.0 all-gather.5.cloned.1.call-start
  95.3 20.1 %all_to_all.11 = bf16[8,16,2048]{2,1,0:T(8,128)(2,1)} all-to-all(bf16[8,16,2048]{2,1,0:T(8,128)(2,1)S(1)} %get-tuple-element.7), channel_id=1, replica_groups=mesh['col'=16,'row'=8] {'row'}, dimensions={0} | all-to-all | bytes 1048576 | tf_op jit(solution)/shard_map/all_to_all | solution.py:247
  115.3 0.0 all-gather.5.cloned.1.call-update
  115.3 51.3 %all-gather.7.cloned.1.call-done = bf16[128,16,1024]{2,1,0:T(8,128)(2,1)} async-done(((bf16[16,16,1024]{2,1,0:T(8,128)(2,1)}), bf16[128,16,1024]{2,1,0:T(8,128)(2,1)}) %all-gather.7.cloned.1.call-update) | async-done | bytes 4194320 | tf_op jit(solution)/shard_map/all_gather | solution.py:250
  166.7 51.6 %all-gather.5.cloned.1.call-done = bf16[128,16,2048]{2,1,0:T(8,128)(2,1)} async-done(((bf16[8,16,2048]{2,1,0:T(8,128)(2,1)}), bf16[128,16,2048]{2,1,0:T(8,128)(2,1)}) %all-gather.5.cloned.1.call-update) | async-done | bytes 8388624 | tf_op jit(solution)/shard_map/all_gather | solution.py:249
  218.3 14.6 %convolution_bitcast_fusion = f32[2048,1024]{1,0:T(8,128)} fusion(bf16[16,8,16,2048]{3,2,1,0:T(8,128)(2,1)} %bitcast.13, bf16[8,16,16,1024]{3,2,1,0:T(8,128)(2,1)} %bitcast.14), kind=kOutput, calls=%fused_computation | convolution fusion | flops 8589934592 | bytes 20971520 | tf_op jit(solution)/shard_map/crkg,rckh->gh/dot_general | solution.py:251
  (6 shorter events, 0.0 us)
Async XLA Ops:
  6.5 160.1 %all-gather.7.cloned.1.call-start = ((), (), s32[]{:S(2)}) async-start(), calls=%async_computation.3 | async-start | bytes 4718592 | tf_op jit(solution)/shard_map/all_gather | solution.py:250
  10.3 2.2 copy-start
  12.5 0.8 copy-start.1
  13.4 0.9 copy-start.2
  14.3 0.8 copy-start.3
  15.0 0.8 copy-start.4
  95.2 123.1 %all-gather.5.cloned.1.call-start = ((), (), s32[]{:S(2)}) async-start(), calls=%async_computation.2 | async-start | bytes 8912896 | tf_op jit(solution)/shard_map/all_gather | solution.py:249
Sparse Core Ops, SparseCore 0:
  95.3 71.2 all-gather.6
  168.4 49.8 all-gather.4

commit v2 on v1

--- a/solution.py
+++ b/solution.py
@@ -110,7 +110,7 @@
                 preferred_element_type=F32,
             )
             for h in range(2):
-                staged[2 * chunk + h, pl.ds(p * EDGE, EDGE), :] = spectrum[:, h * LANES : (h + 1) * LANES]
+                staged[2 * chunk + h, pl.ds(p, EDGE, stride=8), :] = spectrum[:, h * LANES : (h + 1) * LANES]
         return carry
 
     lax.fori_loop(0, EDGE * EDGE // wide, x_stage, 0)
@@ -118,8 +118,8 @@
     first = lax.broadcasted_iota(jnp.int32, (8, LANES), 1) < EDGE
 
     def yz_stage(a, carry):
-        re = [staged[y, pl.ds(a, 8, stride=EDGE), :] for y in range(HALF)]
-        im = [staged[y, pl.ds(a + HALF, 8, stride=EDGE), :] for y in range(HALF)]
+        re = [staged[y, pl.ds(pl.multiple_of(a * 8, 8), 8), :] for y in range(HALF)]
+        im = [staged[y, pl.ds(pl.multiple_of((a + HALF) * 8, 8), 8), :] for y in range(HALF)]
         re, im = small_dft(re, im)
         lower, upper = [], []
         for b in range(HALF):
@@ -165,6 +165,7 @@
     per_row, per_col = left.shape[2] // LANES, right.shape[2] // LANES
     slot = lane & (EDGE - 1)
     w = weight[...]
+    bits = [(slot & (1 << i)) != 0 for i in range(6)]
 
     def select(q, carry):
         parts = []
@@ -172,10 +173,15 @@
             index = point[pl.ds(2 * q + h, 8, stride=0), :]
             c = jnp.where(index >= (HALF + 1) * EDGE * EDGE, EDGE - index, index) & (EDGE - 1)
             take = c + jnp.where(first, h * EDGE, EDGE - h * EDGE)
-            picked = jnp.zeros((8, LANES), F32)
-            for j in range(EDGE):
-                tile = table[lines[q * LANES + h * EDGE + j]]
-                picked = jnp.where(slot == j, jnp.take_along_axis(tile, take, axis=1), picked)
+            def merge(level, j):
+                if level < 0:
+                    tile = table[lines[q * LANES + h * EDGE + j]]
+                    return jnp.take_along_axis(tile, take, axis=1)
+                one = merge(level - 1, j)
+                other = merge(level - 1, j + (1 << level))
+                return jnp.where(bits[level], other, one)
+
+            picked = merge(5, 0)
             parts.append(picked)
         re = jnp.where(first, parts[0], parts[1])
         im = pltpu.roll(jnp.where(first, parts[1], parts[0]), EDGE, 1)
@@ -189,7 +195,7 @@
         right[q // per_col, :, pl.ds(at, LANES)] = plain
         return carry
 
-    lax.fori_loop(0, wave.shape[0], select, 0)
+    lax.fori_loop(0, wave.shape[0], select, 0, unroll=4)
 
 
 def densities(n_row, n_col, valence, conduction, valence_energy, conduction_energy, pair_list, sphere_index):
@@ -239,16 +245,109 @@
     )
 
 
+def product_kernel(n_left, n_right, left_slots, right_slots, *refs):
+    left_in, right_in = refs[:n_left], refs[n_left : n_left + n_right]
+    out, left, right, left_sem, right_sem = refs[n_left + n_right :]
+
+    @pl.when(pl.program_id(0) == 0)
+    def _():
+        copies = [
+            pltpu.make_async_copy(piece, right.at[:, right_slots[j]], right_sem.at[j])
+            for j, piece in enumerate(right_in)
+        ] + [
+            pltpu.make_async_copy(piece, left.at[left_slots[i]], left_sem.at[i])
+            for i, piece in enumerate(left_in)
+        ]
+        for copy in copies:
+            copy.start()
+        for copy in copies:
+            copy.wait()
+
+    rows = out.shape[0]
+    at = pl.multiple_of(pl.program_id(0) * rows, rows)
+    depth = left.shape[0] * left.shape[1] * left.shape[2]
+    out[...] = lax.dot_general(
+        left[:, :, :, pl.ds(at, rows)].reshape(depth, rows),
+        right[...].reshape(depth, right.shape[3]),
+        (((0,), (0,)), ((), ())),
+        preferred_element_type=F32,
+    )
+
+
+def product(left, left_slots, right, right_slots):
+    n_left, n_right = len(left), len(right)
+    rows, cols = left[0].shape[2], right[0].shape[2]
+    block = 256
+    smem = pl.BlockSpec(memory_space=pltpu.SMEM)
+    return pl.pallas_call(
+        lambda *refs: product_kernel(n_left, n_right, *refs),
+        grid=(rows // block,),
+        in_specs=[smem, smem] + [pl.BlockSpec(memory_space=pl.ANY)] * (n_left + n_right),
+        out_specs=pl.BlockSpec((block, cols), lambda m: (m, 0)),
+        out_shape=jax.ShapeDtypeStruct((rows, cols), F32),
+        scratch_shapes=[
+            pltpu.VMEM((n_left,) + left[0].shape, BF),
+            pltpu.VMEM((right[0].shape[0], n_right) + right[0].shape[1:], BF),
+            pltpu.SemaphoreType.DMA((n_left,)),
+            pltpu.SemaphoreType.DMA((n_right,)),
+        ],
+        compiler_params=pltpu.CompilerParams(vmem_limit_bytes=40 * 1024 * 1024),
+        name="product",
+    )(left_slots, right_slots, *left, *right)
+
+
+RING = 4
+
+
+def shift(value, axis, step, stride):
+    count = lax.axis_size(axis)
+    block = RING * stride
+
+    def target(i):
+        place = i // stride % RING
+        return i // block * block + (place + step) % RING * stride + i % stride
+
+    return lax.ppermute(value, axis, [(i, target(i)) for i in range(count)])
+
+
+def swap(value, axis, bit):
+    count = lax.axis_size(axis)
+    return lax.ppermute(value, axis, [(i, i ^ bit) for i in range(count)])
+
+
+def ring(value, axis, stride, forward):
+    before = shift(value, axis, 1, stride)
+    after = shift(value, axis, -1, stride)
+    far = shift(before, axis, 1, stride) if forward else shift(after, axis, -1, stride)
+    return [value, before, after, far]
+
+
+def ring_places(index, stride):
+    block = RING * stride
+    place = index // stride % RING
+    base = index - place * stride
+    return [base + (place + step) % RING * stride for step in (0, RING - 1, 1, 2)]
+
+
 def per_device(valence, conduction, valence_energy, conduction_energy, pair_list, sphere_index):
     n_row, n_col = lax.axis_size("row"), lax.axis_size("col")
+    r, c = lax.axis_index("row"), lax.axis_index("col")
     left, right = densities(
         n_row, n_col, valence, conduction, valence_energy, conduction_energy, pair_list, sphere_index
     )
+    right = lax.all_to_all(right, "col", split_axis=0, concat_axis=0, tiled=True)
+    right_far = swap(right, "row", 4)
+    rights = ring(right, "row", 1, True)
     left = lax.all_to_all(left, "row", split_axis=0, concat_axis=0, tiled=True)
-    right = lax.all_to_all(right, "col", split_axis=0, concat_axis=0, tiled=True)
-    left = lax.all_gather(left, "col", axis=0, tiled=False)
-    right = lax.all_gather(right, "row", axis=0, tiled=False)
-    return jnp.einsum("crkg,rckh->gh", left, right, preferred_element_type=F32)
+    left_far = swap(left, "col", 2)
+    lefts = ring(left, "col", 4, True)
+    rights += ring(right_far, "row", 1, False)
+    lefts += ring(left_far, "col", 4, False)
+    lefts += [swap(piece, "col", 1) for piece in lefts]
+    right_slots = ring_places(r, 1) + ring_places(r ^ 4, 1)
+    left_slots = ring_places(c, 4) + ring_places(c ^ 2, 4)
+    left_slots += [slot ^ 1 for slot in left_slots]
+    return product(lefts, jnp.stack(left_slots), rights, jnp.stack(right_slots))
 
 
 def solution(mesh):

time: 242 us -> 189 us (0.78)
  waiting for transfers between devices: 103 us -> 59.3 us
  starting transfers between devices: 0.04 us -> 20.6 us
  blocking collectives: 36.8 us -> 19.1 us
  local copies, waits for them, and re-layouts: 6.61 us -> 21.7 us
  matrix products: 14.6 us -> 0 us
  between operations: 13.4 us -> 0.51 us
    all_gather x2 -> x0, waiting for transfers between devices: 103 us -> none  [the longest x1 51.6 us: per_device(): left = lax.all_gather(left, 'col', axis=0, tiled=False)]
    ppermute x0 -> x22, waiting for transfers between devices: none -> 48.9 us  [the longest x12 41.5 us: shift(): return lax.ppermute(value, axis, [(i, target(i)) for i in range(count)])]
    all_to_all x1 -> x0, blocking collectives: 16.8 us -> none  [per_device(): lax.all_to_all(right, 'col', split_axis=0, concat_axis=0, tiled=True)]
    ppermute x0 -> x22, starting transfers between devices: none -> 15.6 us  [the longest x12 13 us: shift(): return lax.ppermute(value, axis, [(i, target(i)) for i in range(count)])]
    pallas_call x0 -> x1, Pallas kernels: none -> 15.1 us  [product(): pl.pallas_call(lambda *refs: product_kernel(n_left, n_right, *refs), grid...]
    unnamed x10 -> x42, local copies, waits for them, and re-layouts: 5.45 us -> 20.3 us
    dot_general x1 -> x0, matrix products: 14.6 us -> none  [per_device(): return jnp.einsum('crkg,rckh->gh', left, right, preferred_element_type=F32)]
    pallas_call x1, Pallas kernels: 62.6 us -> 49.4 us  [densities(): pl.pallas_call(density_kernel, in_specs=[smem, smem] + [vmem] * 8, out_sp...]
  transfers between devices with their start and end apart: 2 -> 23, of which waited for: 2 -> 10; matrix products, arithmetic and copies ran while one was open for 0% -> 0% of each run, Pallas kernels for 0% -> 0%
where the time goes in v2:
time: 189 us; the launch traced here: 188 us
  Pallas kernels  64.5 us (34%)
  waiting for transfers between devices  59.3 us (31%)
  local copies, waits for them, and re-layouts  21.7 us (11%)
  starting transfers between devices  20.6 us (11%)
  blocking collectives  19.1 us (10%)
  other arithmetic  2.62 us (1%)
    pallas_call x1, Pallas kernels, densities(): pl.pallas_call(density_kernel, in_specs=[smem, smem] + [vmem] * 8, out_sp...  49.4 us
    ppermute x12, waiting for transfers between devices, shift(): return lax.ppermute(value, axis, [(i, target(i)) for i in range(count)])  41.5 us
    unnamed x42, local copies, waits for them, and re-layouts  20.3 us
    all_to_all x1, blocking collectives, per_device(): left = lax.all_to_all(left, 'row', split_axis=0, concat_axis=0, tiled=True)  19.1 us
    pallas_call x1, Pallas kernels, product(): pl.pallas_call(lambda *refs: product_kernel(n_left, n_right, *refs), grid...  15.1 us
    ppermute x12, starting transfers between devices, shift(): return lax.ppermute(value, axis, [(i, target(i)) for i in range(count)])  13 us
    all_to_all x1, waiting for transfers between devices, per_device(): lax.all_to_all(right, 'col', split_axis=0, concat_axis=0, tiled=True)  10.4 us
    ppermute x10, waiting for transfers between devices, swap(): return lax.ppermute(value, axis, [(i, i ^ bit) for i in range(count)])  7.33 us
  transfers between devices with their start and end apart: 23, of which 10 were waited for; matrix products, arithmetic and copies ran while one was open for 0% of the time, Pallas kernels for 0%

profile of v2, /device:TPU:0, one launch (start us, length us, event | category | flops | bytes accessed | tf_op | source)
XLA Modules:
  0.0 188.3 jit_solution(7648407082925805813)
XLA Ops:
  3.8 2.2 %copy-done = f32[4,64,4096]{2,1,0:T(8,128)S(1)} copy-done((f32[4,64,4096]{2,1,0:T(8,128)S(1)}, f32[4,64,4096]{2,1,0:T(8,128)}, u32[]{:S(2)}) %copy-start) | copy-done | bytes 4194328
  9.3 49.4 %density.1 = (bf16[8,16,2048]{2,1,0:T(8,128)(2,1)S(1)}, bf16[16,16,1024]{2,1,0:T(8,128)(2,1)}) custom-call(s32[16]{0:T(128)S(1)} %reshape.18.pairs, s32[16384]{0:T(1024)S(1)} %fusion.2.lines, f32[4,64,4096]{2,1,0:T(8,128)S(1)} %copy-done, f32[4,64,4096]{2,1,0:T(8,128)} %conduction.1, f32[8,128]{1,0:T(8,128)S(1)} %broadcast_in_dim.33.weight, ...), custom_call_target="tpu_custom_call" | custom-call | tf_op jit(solution)/shard_map/density/pallas_call | solution.py:220
  58.7 19.1 %all_to_all.10.refs_2_ = bf16[8,16,2048]{2,1,0:T(8,128)(2,1)S(1)} all-to-all(bf16[8,16,2048]{2,1,0:T(8,128)(2,1)S(1)} %get-tuple-element.7), channel_id=1, replica_groups=mesh['col'=16,'row'=8] {'row'}, dimensions={0} | all-to-all | bytes 1048576 | tf_op jit(solution)/shard_map/all_to_all | solution.py:341
  78.8 5.0 %all-to-all-start.1 = ((bf16[16,16,1024]{2,1,0:T(8,128)(2,1)}), bf16[16,16,1024]{2,1,0:T(8,128)(2,1)S(1)}, u32[]{:S(2)}, u32[]{:S(2)}) async-start(bf16[16,16,1024]{2,1,0:T(8,128)(2,1)} %get-tuple-element.8), calls=%async_computation.1 | async-start | bytes 1048576 | tf_op jit(solution)/shard_map/all_to_all | solution.py:338
  83.8 3.1 %collective-permute-start.1 = (bf16[8,16,2048]{2,1,0:T(8,128)(2,1)S(1)}, bf16[8,16,2048]{2,1,0:T(8,128)(2,1)S(1)}, u32[]{:S(2)}, u32[]{:S(2)}) collective-permute-start(bf16[8,16,2048]{2,1,0:T(8,128)(2,1)S(1)} %all_to_all.10.refs_2_), channel_id=1, source_target_pairs={{0,96},{8,104},{16,112},{24,120},{32,0},{40,8},{48,16},{56,24},{64... | collective-permute-start | bytes 1572872 | tf_op jit(solution)/shard_map/ppermute | solution.py:310
  87.0 10.4 %all-to-all-done.1.refs_18_ = bf16[16,16,1024]{2,1,0:T(8,128)(2,1)S(1)} async-done(((bf16[16,16,1024]{2,1,0:T(8,128)(2,1)}), bf16[16,16,1024]{2,1,0:T(8,128)(2,1)S(1)}, u32[]{:S(2)}, u32[]{:S(2)}) %all-to-all-start.1) | async-done | bytes 524320 | tf_op jit(solution)/shard_map/all_to_all | solution.py:338
  97.9 1.5 collective-permute-start.16
  100.0 3.8 %collective-permute-done.1.refs_4_ = bf16[8,16,2048]{2,1,0:T(8,128)(2,1)S(1)} collective-permute-done((bf16[8,16,2048]{2,1,0:T(8,128)(2,1)S(1)}, bf16[8,16,2048]{2,1,0:T(8,128)(2,1)S(1)}, u32[]{:S(2)}, u32[]{:S(2)}) %collective-permute-start.1) | collective-permute-done | bytes 524320 | tf_op jit(solution)/shard_map/ppermute | solution.py:310
  103.8 1.2 collective-permute-done.refs_3_
  105.9 7.3 %collective-permute-done.18.refs_22_ = bf16[16,16,1024]{2,1,0:T(8,128)(2,1)S(1)} collective-permute-done((bf16[16,16,1024]{2,1,0:T(8,128)(2,1)S(1)}, bf16[16,16,1024]{2,1,0:T(8,128)(2,1)S(1)}, u32[]{:S(2)}, u32[]{:S(2)}) %collective-permute-start.18) | collective-permute-done | bytes 524320 | tf_op jit(solution)/shard_map/ppermute | solution.py:315
  113.2 1.6 collective-permute-start.4
  116.9 1.6 collective-permute-start.2
  118.6 1.1 collective-permute-start.20
  119.7 9.6 %collective-permute-done.4.refs_7_ = bf16[8,16,2048]{2,1,0:T(8,128)(2,1)} collective-permute-done((bf16[8,16,2048]{2,1,0:T(8,128)(2,1)S(1)}, bf16[8,16,2048]{2,1,0:T(8,128)(2,1)}, u32[]{:S(2)}, u32[]{:S(2)}) %collective-permute-start.4) | collective-permute-done | bytes 524320 | tf_op jit(solution)/shard_map/ppermute | solution.py:310
  133.5 1.8 collective-permute-start.6
  135.3 4.0 %collective-permute-done.2.refs_5_ = bf16[8,16,2048]{2,1,0:T(8,128)(2,1)} collective-permute-done((bf16[8,16,2048]{2,1,0:T(8,128)(2,1)S(1)}, bf16[8,16,2048]{2,1,0:T(8,128)(2,1)}, u32[]{:S(2)}, u32[]{:S(2)}) %collective-permute-start.2) | collective-permute-done | bytes 524320 | tf_op jit(solution)/shard_map/ppermute | solution.py:310
  139.8 5.6 %collective-permute-done.19.refs_23_ = bf16[16,16,1024]{2,1,0:T(8,128)(2,1)S(1)} collective-permute-done((bf16[16,16,1024]{2,1,0:T(8,128)(2,1)S(1)}, bf16[16,16,1024]{2,1,0:T(8,128)(2,1)S(1)}, u32[]{:S(2)}, u32[]{:S(2)}) %collective-permute-start.19) | collective-permute-done | bytes 524320 | tf_op jit(solution)/shard_map/ppermute | solution.py:310
  146.2 7.0 %collective-permute-done.17.refs_21_ = bf16[16,16,1024]{2,1,0:T(8,128)(2,1)S(1)} collective-permute-done((bf16[16,16,1024]{2,1,0:T(8,128)(2,1)S(1)}, bf16[16,16,1024]{2,1,0:T(8,128)(2,1)S(1)}, u32[]{:S(2)}, u32[]{:S(2)}) %collective-permute-start.17) | collective-permute-done | bytes 524320 | tf_op jit(solution)/shard_map/ppermute | solution.py:310
  154.7 10.2 %collective-permute-done.21.refs_25_ = bf16[16,16,1024]{2,1,0:T(8,128)(2,1)} collective-permute-done((bf16[16,16,1024]{2,1,0:T(8,128)(2,1)}, bf16[16,16,1024]{2,1,0:T(8,128)(2,1)}, u32[]{:S(2)}, u32[]{:S(2)}) %collective-permute-start.21) | collective-permute-done | bytes 524320 | tf_op jit(solution)/shard_map/ppermute | solution.py:310
  164.9 1.0 copy-done.3
  167.0 1.0 copy-done.7
  168.0 1.0 copy-done.9
  171.1 1.0 copy-done.15
  173.2 15.1 %product.1 = f32[2048,1024]{1,0:T(8,128)} custom-call(s32[16]{0:T(128)S(1)} %stack.99.refs_0_, s32[8]{0:T(128)S(1)} %stack.108.refs_1_, bf16[8,16,2048]{2,1,0:T(8,128)(2,1)S(1)} %all_to_all.10.refs_2_, bf16[8,16,2048]{2,1,0:T(8,128)(2,1)S(1)} %collective-permute-done.refs_3_, bf16[8,16,2048]{2,1,0:T(8,128)(2,1)S(1)} %collective-permute-done.1.refs_4_, ...), custom_call_target="tpu_custom_call" | custom-call | tf_op jit(solution)/shard_map/product/pallas_call | solution.py:282
  (79 shorter events, 23.0 us)
Async XLA Ops:
  3.8 2.2 %copy-start = (f32[4,64,4096]{2,1,0:T(8,128)S(1)}, f32[4,64,4096]{2,1,0:T(8,128)}, u32[]{:S(2)}) copy-start(f32[4,64,4096]{2,1,0:T(8,128)} %valence.1) | copy-start | bytes 12582916
  77.8 20.2 %collective-permute-start.7 = (bf16[8,16,2048]{2,1,0:T(8,128)(2,1)S(1)}, bf16[8,16,2048]{2,1,0:T(8,128)(2,1)S(1)}, u32[]{:S(2)}, u32[]{:S(2)}) collective-permute-start(bf16[8,16,2048]{2,1,0:T(8,128)(2,1)S(1)} %all_to_all.10.refs_2_), channel_id=1, source_target_pairs={{0,8},{8,0},{16,24},{24,16},{32,40},{40,32},{48,56},{56,48},{64,72... | collective-permute-start | bytes 1572872 | tf_op jit(solution)/shard_map/ppermute | solution.py:315
  77.8 21.6 %collective-permute-start.3 = (bf16[8,16,2048]{2,1,0:T(8,128)(2,1)S(1)}, bf16[8,16,2048]{2,1,0:T(8,128)(2,1)S(1)}, u32[]{:S(2)}, u32[]{:S(2)}) collective-permute-start(bf16[8,16,2048]{2,1,0:T(8,128)(2,1)S(1)} %all_to_all.10.refs_2_), channel_id=1, source_target_pairs={{0,16},{8,24},{16,0},{24,8},{32,48},{40,56},{48,32},{56,40},{64,80... | collective-permute-start | bytes 1572872 | tf_op jit(solution)/shard_map/ppermute | solution.py:315
  78.8 18.6 %all-to-all-start.1 = ((bf16[16,16,1024]{2,1,0:T(8,128)(2,1)}), bf16[16,16,1024]{2,1,0:T(8,128)(2,1)S(1)}, u32[]{:S(2)}, u32[]{:S(2)}) async-start(bf16[16,16,1024]{2,1,0:T(8,128)(2,1)} %get-tuple-element.8), calls=%async_computation.1 | async-start | bytes 1048576 | tf_op jit(solution)/shard_map/all_to_all | solution.py:338
  83.8 20.0 %collective-permute-start.1 = (bf16[8,16,2048]{2,1,0:T(8,128)(2,1)S(1)}, bf16[8,16,2048]{2,1,0:T(8,128)(2,1)S(1)}, u32[]{:S(2)}, u32[]{:S(2)}) collective-permute-start(bf16[8,16,2048]{2,1,0:T(8,128)(2,1)S(1)} %all_to_all.10.refs_2_), channel_id=1, source_target_pairs={{0,96},{8,104},{16,112},{24,120},{32,0},{40,8},{48,16},{56,24},{64... | collective-permute-start | bytes 1572872 | tf_op jit(solution)/shard_map/ppermute | solution.py:310
  87.0 18.1 %collective-permute-start = (bf16[8,16,2048]{2,1,0:T(8,128)(2,1)S(1)}, bf16[8,16,2048]{2,1,0:T(8,128)(2,1)S(1)}, u32[]{:S(2)}, u32[]{:S(2)}) collective-permute-start(bf16[8,16,2048]{2,1,0:T(8,128)(2,1)S(1)} %all_to_all.10.refs_2_), channel_id=1, source_target_pairs={{0,32},{8,40},{16,48},{24,56},{32,64},{40,72},{48,80},{56,88},{64,... | collective-permute-start | bytes 1572872 | tf_op jit(solution)/shard_map/ppermute | solution.py:310
  97.4 15.8 %collective-permute-start.18 = (bf16[16,16,1024]{2,1,0:T(8,128)(2,1)S(1)}, bf16[16,16,1024]{2,1,0:T(8,128)(2,1)S(1)}, u32[]{:S(2)}, u32[]{:S(2)}) collective-permute-start(bf16[16,16,1024]{2,1,0:T(8,128)(2,1)S(1)} %all-to-all-done.1.refs_18_), channel_id=1, source_target_pairs={{0,4},{1,5},{2,6},{3,7},{4,0},{5,1},{6,2},{7,3},{8,12},{9,13},{10,... | collective-permute-start | bytes 1572872 | tf_op jit(solution)/shard_map/ppermute | solution.py:315
  97.9 16.8 %collective-permute-start.16 = (bf16[16,16,1024]{2,1,0:T(8,128)(2,1)S(1)}, bf16[16,16,1024]{2,1,0:T(8,128)(2,1)S(1)}, u32[]{:S(2)}, u32[]{:S(2)}) collective-permute-start(bf16[16,16,1024]{2,1,0:T(8,128)(2,1)S(1)} %all-to-all-done.1.refs_18_), channel_id=1, source_target_pairs={{0,3},{1,0},{2,1},{3,2},{4,7},{5,4},{6,5},{7,6},{8,11},{9,8},{10,9... | collective-permute-start | bytes 1572872 | tf_op jit(solution)/shard_map/ppermute | solution.py:310
  99.4 16.2 %collective-permute-start.15 = (bf16[16,16,1024]{2,1,0:T(8,128)(2,1)S(1)}, bf16[16,16,1024]{2,1,0:T(8,128)(2,1)S(1)}, u32[]{:S(2)}, u32[]{:S(2)}) collective-permute-start(bf16[16,16,1024]{2,1,0:T(8,128)(2,1)S(1)} %all-to-all-done.1.refs_18_), channel_id=1, source_target_pairs={{0,1},{1,2},{2,3},{3,0},{4,5},{5,6},{6,7},{7,4},{8,9},{9,10},{10,1... | collective-permute-start | bytes 1572872 | tf_op jit(solution)/shard_map/ppermute | solution.py:310
  103.8 12.3 %collective-permute-start.11 = (bf16[8,16,2048]{2,1,0:T(8,128)(2,1)S(1)}, bf16[8,16,2048]{2,1,0:T(8,128)(2,1)S(1)}, u32[]{:S(2)}, u32[]{:S(2)}) collective-permute-start(bf16[8,16,2048]{2,1,0:T(8,128)(2,1)S(1)} %collective-permute-done.3.refs_6_), channel_id=1, source_target_pairs={{0,8},{8,0},{16,24},{24,16},{32,40},{40,32},{48,56},{56,48},{64,72... | collective-permute-start | bytes 1572872 | tf_op jit(solution)/shard_map/ppermute | solution.py:315
  105.0 13.6 %collective-permute-start.5 = (bf16[8,16,2048]{2,1,0:T(8,128)(2,1)S(1)}, bf16[8,16,2048]{2,1,0:T(8,128)(2,1)}, u32[]{:S(2)}, u32[]{:S(2)}) collective-permute-start(bf16[8,16,2048]{2,1,0:T(8,128)(2,1)S(1)} %collective-permute-done.3.refs_6_), channel_id=1, source_target_pairs={{0,96},{8,104},{16,112},{24,120},{32,0},{40,8},{48,16},{56,24},{64... | collective-permute-start | bytes 1572872 | tf_op jit(solution)/shard_map/ppermute | solution.py:310
  113.2 16.1 %collective-permute-start.4 = (bf16[8,16,2048]{2,1,0:T(8,128)(2,1)S(1)}, bf16[8,16,2048]{2,1,0:T(8,128)(2,1)}, u32[]{:S(2)}, u32[]{:S(2)}) collective-permute-start(bf16[8,16,2048]{2,1,0:T(8,128)(2,1)S(1)} %collective-permute-done.3.refs_6_), channel_id=1, source_target_pairs={{0,32},{8,40},{16,48},{24,56},{32,64},{40,72},{48,80},{56,88},{64,... | collective-permute-start | bytes 1572872 | tf_op jit(solution)/shard_map/ppermute | solution.py:310
  115.6 15.5 %collective-permute-start.9 = (bf16[8,16,2048]{2,1,0:T(8,128)(2,1)S(1)}, bf16[8,16,2048]{2,1,0:T(8,128)(2,1)S(1)}, u32[]{:S(2)}, u32[]{:S(2)}) collective-permute-start(bf16[8,16,2048]{2,1,0:T(8,128)(2,1)S(1)} %collective-permute-done.1.refs_4_), channel_id=1, source_target_pairs={{0,8},{8,0},{16,24},{24,16},{32,40},{40,32},{48,56},{56,48},{64,72... | collective-permute-start | bytes 1572872 | tf_op jit(solution)/shard_map/ppermute | solution.py:315
  115.6 17.1 %collective-permute-start.8 = (bf16[8,16,2048]{2,1,0:T(8,128)(2,1)S(1)}, bf16[8,16,2048]{2,1,0:T(8,128)(2,1)S(1)}, u32[]{:S(2)}, u32[]{:S(2)}) collective-permute-start(bf16[8,16,2048]{2,1,0:T(8,128)(2,1)S(1)} %collective-permute-done.refs_3_), channel_id=1, source_target_pairs={{0,8},{8,0},{16,24},{24,16},{32,40},{40,32},{48,56},{56,48},{64,72... | collective-permute-start | bytes 1572872 | tf_op jit(solution)/shard_map/ppermute | solution.py:315
  116.9 22.4 %collective-permute-start.2 = (bf16[8,16,2048]{2,1,0:T(8,128)(2,1)S(1)}, bf16[8,16,2048]{2,1,0:T(8,128)(2,1)}, u32[]{:S(2)}, u32[]{:S(2)}) collective-permute-start(bf16[8,16,2048]{2,1,0:T(8,128)(2,1)S(1)} %collective-permute-done.refs_3_), channel_id=1, source_target_pairs={{0,32},{8,40},{16,48},{24,56},{32,64},{40,72},{48,80},{56,88},{64,... | collective-permute-start | bytes 1572872 | tf_op jit(solution)/shard_map/ppermute | solution.py:310
  118.6 20.7 %collective-permute-start.20 = (bf16[16,16,1024]{2,1,0:T(8,128)(2,1)S(1)}, bf16[16,16,1024]{2,1,0:T(8,128)(2,1)}, u32[]{:S(2)}, u32[]{:S(2)}) collective-permute-start(bf16[16,16,1024]{2,1,0:T(8,128)(2,1)S(1)} %collective-permute-done.18.refs_22_), channel_id=1, source_target_pairs={{0,3},{1,0},{2,1},{3,2},{4,7},{5,4},{6,5},{7,6},{8,11},{9,8},{10,9... | collective-permute-start | bytes 1572872 | tf_op jit(solution)/shard_map/ppermute | solution.py:310
  129.3 16.1 %collective-permute-start.19 = (bf16[16,16,1024]{2,1,0:T(8,128)(2,1)S(1)}, bf16[16,16,1024]{2,1,0:T(8,128)(2,1)S(1)}, u32[]{:S(2)}, u32[]{:S(2)}) collective-permute-start(bf16[16,16,1024]{2,1,0:T(8,128)(2,1)S(1)} %collective-permute-done.18.refs_22_), channel_id=1, source_target_pairs={{0,1},{1,2},{2,3},{3,0},{4,5},{5,6},{6,7},{7,4},{8,9},{9,10},{10,1... | collective-permute-start | bytes 1572872 | tf_op jit(solution)/shard_map/ppermute | solution.py:310
  131.9 21.3 %collective-permute-start.17 = (bf16[16,16,1024]{2,1,0:T(8,128)(2,1)S(1)}, bf16[16,16,1024]{2,1,0:T(8,128)(2,1)S(1)}, u32[]{:S(2)}, u32[]{:S(2)}) collective-permute-start(bf16[16,16,1024]{2,1,0:T(8,128)(2,1)S(1)} %collective-permute-done.15.refs_19_), channel_id=1, source_target_pairs={{0,1},{1,2},{2,3},{3,0},{4,5},{5,6},{6,7},{7,4},{8,9},{9,10},{10,1... | collective-permute-start | bytes 1572872 | tf_op jit(solution)/shard_map/ppermute | solution.py:310
  133.5 20.6 %collective-permute-start.6 = (bf16[8,16,2048]{2,1,0:T(8,128)(2,1)}, bf16[8,16,2048]{2,1,0:T(8,128)(2,1)}, u32[]{:S(2)}, u32[]{:S(2)}) collective-permute-start(bf16[8,16,2048]{2,1,0:T(8,128)(2,1)} %collective-permute-done.5.refs_8_), channel_id=1, source_target_pairs={{0,96},{8,104},{16,112},{24,120},{32,0},{40,8},{48,16},{56,24},{64... | collective-permute-start | bytes 1572872 | tf_op jit(solution)/shard_map/ppermute | solution.py:310
  139.3 15.3 %collective-permute-start.13 = (bf16[8,16,2048]{2,1,0:T(8,128)(2,1)}, bf16[8,16,2048]{2,1,0:T(8,128)(2,1)}, u32[]{:S(2)}, u32[]{:S(2)}) collective-permute-start(bf16[8,16,2048]{2,1,0:T(8,128)(2,1)} %collective-permute-done.5.refs_8_), channel_id=1, source_target_pairs={{0,8},{8,0},{16,24},{24,16},{32,40},{40,32},{48,56},{56,48},{64,72... | collective-permute-start | bytes 1572872 | tf_op jit(solution)/shard_map/ppermute | solution.py:315
  139.3 15.3 %collective-permute-start.12 = (bf16[8,16,2048]{2,1,0:T(8,128)(2,1)}, bf16[8,16,2048]{2,1,0:T(8,128)(2,1)}, u32[]{:S(2)}, u32[]{:S(2)}) collective-permute-start(bf16[8,16,2048]{2,1,0:T(8,128)(2,1)} %collective-permute-done.4.refs_7_), channel_id=1, source_target_pairs={{0,8},{8,0},{16,24},{24,16},{32,40},{40,32},{48,56},{56,48},{64,72... | collective-permute-start | bytes 1572872 | tf_op jit(solution)/shard_map/ppermute | solution.py:315
  146.2 8.4 %collective-permute-start.10 = (bf16[8,16,2048]{2,1,0:T(8,128)(2,1)}, bf16[8,16,2048]{2,1,0:T(8,128)(2,1)}, u32[]{:S(2)}, u32[]{:S(2)}) collective-permute-start(bf16[8,16,2048]{2,1,0:T(8,128)(2,1)} %collective-permute-done.2.refs_5_), channel_id=1, source_target_pairs={{0,8},{8,0},{16,24},{24,16},{32,40},{40,32},{48,56},{56,48},{64,72... | collective-permute-start | bytes 1572872 | tf_op jit(solution)/shard_map/ppermute | solution.py:315
  154.0 10.8 %collective-permute-start.21 = (bf16[16,16,1024]{2,1,0:T(8,128)(2,1)}, bf16[16,16,1024]{2,1,0:T(8,128)(2,1)}, u32[]{:S(2)}, u32[]{:S(2)}) collective-permute-start(bf16[16,16,1024]{2,1,0:T(8,128)(2,1)} %collective-permute-done.20.refs_24_), channel_id=1, source_target_pairs={{0,3},{1,0},{2,1},{3,2},{4,7},{5,4},{6,5},{7,6},{8,11},{9,8},{10,9... | collective-permute-start | bytes 1572872 | tf_op jit(solution)/shard_map/ppermute | solution.py:310
  154.0 10.8 %collective-permute-start.14 = (bf16[8,16,2048]{2,1,0:T(8,128)(2,1)}, bf16[8,16,2048]{2,1,0:T(8,128)(2,1)}, u32[]{:S(2)}, u32[]{:S(2)}) collective-permute-start(bf16[8,16,2048]{2,1,0:T(8,128)(2,1)} %collective-permute-done.6.refs_9_), channel_id=1, source_target_pairs={{0,8},{8,0},{16,24},{24,16},{32,40},{40,32},{48,56},{56,48},{64,72... | collective-permute-start | bytes 1572872 | tf_op jit(solution)/shard_map/ppermute | solution.py:315
  (20 other events, 18.1 us)

commit v3 on v2

v3 whole, which is shorter than its diff:
```python
import math

import jax
import jax.numpy as jnp
import numpy as np
from jax import lax
from jax.experimental import pallas as pl
from jax.experimental.pallas import tpu as pltpu
from jax.sharding import PartitionSpec as P

EDGE = 64
HALF = EDGE // 2
LANES = 128
BF = jnp.bfloat16
F32 = jnp.float32


def two_terms(table):
    high = table.astype(np.float32).astype(BF)
    low = (table - high.astype(np.float64)).astype(BF)
    return np.asarray(high), np.asarray(low)


def x_table():
    x = np.arange(EDGE)
    a = np.arange(HALF)
    angle = 2.0 * np.pi * ((a[:, None] * x[None, :]) % EDGE) / EDGE
    table = np.concatenate([np.cos(angle), -np.sin(angle)], axis=0)
    table[HALF] = 1.0 - 2.0 * (x % 2)
    high, low = two_terms(table)
    return np.concatenate([high, high, low], axis=1)


def z_table():
    z = np.arange(EDGE)
    angle = 2.0 * np.pi * ((z[:, None] * z[None, :]) % EDGE) / EDGE
    table = np.concatenate([np.cos(angle), np.sin(angle)], axis=1) * EDGE ** (-1.5)
    high, low = two_terms(table)
    return np.block([[high, high], [low, np.zeros_like(low)]]).astype(BF)


def y_table():
    angle = 2.0 * np.pi * np.arange(HALF) / EDGE
    odd = np.arange(LANES)[None, :] >= EDGE
    real = np.where(odd, np.cos(angle)[:, None], 1.0)
    imag = np.where(odd, -np.sin(angle)[:, None], 0.0)
    return np.concatenate([real, imag], axis=0).astype(np.float32)


def small_dft(re, im):
    n = len(re)
    if n == 1:
        return re, im
    even_re, even_im = small_dft(re[0::2], im[0::2])
    odd_re, odd_im = small_dft(re[1::2], im[1::2])
    out_re, out_im = [None] * n, [None] * n
    for k in range(n // 2):
        r, i = odd_re[k], odd_im[k]
        if k == 0:
            pass
        elif 4 * k == n:
            r, i = i, -r
        elif 8 * k == n:
            s = math.sqrt(0.5)
            r, i = (r + i) * s, (i - r) * s
        elif 8 * k == 3 * n:
            s = math.sqrt(0.5)
            r, i = (i - r) * s, (r + i) * -s
        else:
            c, s = math.cos(2 * math.pi * k / n), math.sin(2 * math.pi * k / n)
            r, i = r * c + i * s, i * c - r * s
        out_re[k], out_im[k] = even_re[k] + r, even_im[k] + i
        out_re[k + n // 2], out_im[k + n // 2] = even_re[k] - r, even_im[k] - i
    return out_re, out_im


def split(value):
    high = value.astype(BF)
    return high, (value - high.astype(F32)).astype(BF)


def half_space(index):
    a, b, c = index >> 12, (index >> 6) & (EDGE - 1), index & (EDGE - 1)
    mirrored = a > HALF
    a = jnp.where(mirrored, EDGE - a, a)
    b = jnp.where(mirrored, (EDGE - b) & (EDGE - 1), b)
    c = jnp.where(mirrored, (EDGE - c) & (EDGE - 1), c)
    return a, b, c, mirrored


def density_kernel(
    total_pairs,
    valence_hbm,
    conduction_hbm,
    valence_energy_hbm,
    conduction_energy_hbm,
    pairs_hbm,
    wave_hbm,
    x_factors_hbm,
    z_factors_hbm,
    y_factors_hbm,
    left,
    right,
    staged,
    table,
    valence,
    conduction,
    valence_energy,
    conduction_energy,
    pairs,
    wave,
    rows_vector,
    rows,
    x_factors,
    z_factors,
    y_factors,
    picked_0,
    picked_1,
    sems,
    orbital_sems,
):
    n_pairs = 8
    wide = 2 * LANES
    groups = orbital_sems.shape[1]
    span = EDGE * EDGE // groups

    small = [
        pltpu.make_async_copy(src, dst, sems.at[i])
        for i, (src, dst) in enumerate(
            [
                (pairs_hbm, pairs),
                (x_factors_hbm, x_factors),
                (wave_hbm, wave),
                (valence_energy_hbm, valence_energy),
                (conduction_energy_hbm, conduction_energy),
                (z_factors_hbm, z_factors),
                (y_factors_hbm, y_factors),
            ]
        )
    ]
    for copy in small:
        copy.start()
    orbitals = []
    for n in range(groups):
        at = pl.ds(n * span, span)
        orbitals.append(
            [
                pltpu.make_async_copy(valence_hbm.at[:, :, at], valence.at[:, :, at], orbital_sems.at[0, n]),
                pltpu.make_async_copy(conduction_hbm.at[:, :, at], conduction.at[:, :, at], orbital_sems.at[1, n]),
            ]
        )
        for copy in orbitals[-1]:
            copy.start()
    for copy in small:
        copy.wait()

    a, b, c, _ = half_space(wave[...])
    rows_vector[...] = (a * 8 + (b >> 3)) * EDGE + c
    to_scalar = pltpu.make_async_copy(rows_vector, rows, sems.at[0])
    to_scalar.start()

    v_local = [lax.rem(pairs[0, p], valence.shape[0]) for p in range(n_pairs)]
    c_local = [lax.rem(pairs[1, p], conduction.shape[0]) for p in range(n_pairs)]
    sublane = lax.broadcasted_iota(jnp.int32, (8, LANES), 0)
    gap = jnp.ones((8, LANES), F32)
    for p in range(n_pairs):
        gap = jnp.where(sublane == p, conduction_energy[c_local[p]] - valence_energy[v_local[p]], gap)
    w = -4.0 / (total_pairs * gap)

    def x_stage(chunk, carry):
        lanes = pl.ds(pl.multiple_of(chunk * wide, wide), wide)
        for p in range(n_pairs):
            product = valence[v_local[p], :, lanes] * conduction[c_local[p], :, lanes]
            high, low = split(product)
            spectrum = jnp.dot(
                x_factors[...],
                jnp.concatenate([high, low, high], axis=0),
                preferred_element_type=F32,
            )
            for h in range(2):
                staged[2 * chunk + h, pl.ds(p, EDGE, stride=8), :] = spectrum[:, h * LANES : (h + 1) * LANES]
        return carry

    for n in range(groups):
        for copy in orbitals[n]:
            copy.wait()
        lax.fori_loop(n * span // wide, (n + 1) * span // wide, x_stage, 0)

    first = lax.broadcasted_iota(jnp.int32, (8, LANES), 1) < EDGE

    def yz_stage(a, carry):
        complex_plane = jnp.where((a & (HALF - 1)) == 0, 0.0, 1.0)
        at_re = pl.ds(pl.multiple_of(a * 8, 8), 8)
        at_im = pl.ds(pl.multiple_of(((a & (HALF - 1)) + HALF) * 8, 8), 8)
        re = [staged[y, at_re, :] for y in range(HALF)]
        im = [staged[y, at_im, :] * complex_plane for y in range(HALF)]
        re, im = small_dft(re, im)
        lower, upper = [], []
        for b in range(HALF):
            r, i = re[b], im[b]
            if b:
                c = y_factors[pl.ds(b, 8, stride=0), :]
                s = y_factors[pl.ds(b + HALF, 8, stride=0), :]
                r, i = r * c - i * s, r * s + i * c
            even = jnp.where(first, r, pltpu.roll(i, EDGE, 1))
            odd = jnp.where(first, pltpu.roll(r, EDGE, 1), i)
            for part, line in ((lower, even + odd), (upper, even - odd)):
                turned = pltpu.roll(line, EDGE, 1)
                part += [line, jnp.where(first, turned, -turned)]
        high, low = split(jnp.concatenate(lower + upper, axis=0))
        out = lax.dot_general(
            z_factors[...],
            jnp.concatenate([high, low], axis=1),
            (((1,), (1,)), ((), ())),
            preferred_element_type=F32,
        )
        out = out[:EDGE] + out[EDGE:]
        for n in range(8):
            at = pl.multiple_of((a * 8 + n) * EDGE, EDGE)
            table[pl.ds(at, EDGE), :] = out[:, n * LANES : (n + 1) * LANES]
        return carry

    lax.fori_loop(0, HALF + 1, yz_stage, 0)

    to_scalar.wait()
    per_row, per_col = left.shape[2] // LANES, right.shape[2] // LANES

    def pick(q, picked):
        for j in range(LANES):
            picked[pl.ds(j, 1), :] = table[pl.ds(rows[q, j], 1), :]

    def finish(q, picked):
        turned = picked[...].T
        _, b, _, mirrored = half_space(wave[pl.ds(q, 8, stride=0), :])
        bits = [(b & (1 << i)) != 0 for i in range(3)]
        parts = []
        for k in range(2):
            some = [turned[n * 16 + k * 8 : n * 16 + k * 8 + 8] for n in range(8)]
            for bit in bits:
                some = [jnp.where(bit, some[n + 1], some[n]) for n in range(0, len(some), 2)]
            parts.append(some[0])
        re, im = parts
        im = jnp.where(mirrored, -im, im)
        plain = jnp.concatenate([re, im], axis=0).astype(BF)
        scaled = jnp.concatenate([w * re, w * im], axis=0).astype(BF)
        at = pl.multiple_of((q % per_row) * LANES, LANES)
        left[q // per_row, :, pl.ds(at, LANES)] = scaled
        at = pl.multiple_of((q % per_col) * LANES, LANES)
        right[q // per_col, :, pl.ds(at, LANES)] = plain

    count = wave.shape[0]
    pick(0, picked_0)

    def select(i, carry):
        pick(2 * i + 1, picked_1)
        finish(2 * i, picked_0)
        pick(jnp.minimum(2 * i + 2, count - 1), picked_0)
        finish(2 * i + 1, picked_1)
        return carry

    lax.fori_loop(0, count // 2, select, 0)


def densities(n_row, n_col, valence, conduction, valence_energy, conduction_energy, pair_list, sphere_index):
    n_pairs, waves = pair_list.shape[0], sphere_index.shape[0]
    tables = [jnp.asarray(x_table()), jnp.asarray(z_table()), jnp.asarray(y_table())]
    hbm = pl.BlockSpec(memory_space=pltpu.HBM)
    vmem = pl.BlockSpec(memory_space=pltpu.VMEM)
    return pl.pallas_call(
        lambda *refs: density_kernel(n_pairs * n_row * n_col, *refs),
        in_specs=[hbm] * 9,
        out_specs=[vmem, vmem],
        out_shape=[
            jax.ShapeDtypeStruct((n_row, 2 * n_pairs, waves // n_row), BF),
            jax.ShapeDtypeStruct((n_col, 2 * n_pairs, waves // n_col), BF),
        ],
        scratch_shapes=[
            pltpu.VMEM((HALF, n_pairs * EDGE, LANES), F32),
            pltpu.VMEM(((HALF + 1) * 8 * EDGE, LANES), F32),
            pltpu.VMEM(valence.shape, F32),
            pltpu.VMEM(conduction.shape, F32),
            pltpu.SMEM(valence_energy.shape, F32),
            pltpu.SMEM(conduction_energy.shape, F32),
            pltpu.SMEM((2, n_pairs), jnp.int32),
            pltpu.VMEM((waves // LANES, LANES), jnp.int32),
            pltpu.VMEM((waves // LANES, LANES), jnp.int32),
            pltpu.SMEM((waves // LANES, LANES), jnp.int32),
            pltpu.VMEM(tables[0].shape, BF),
            pltpu.VMEM(tables[1].shape, BF),
            pltpu.VMEM(tables[2].shape, F32),
            pltpu.VMEM((LANES, LANES), F32),
            pltpu.VMEM((LANES, LANES), F32),
            pltpu.SemaphoreType.DMA((7,)),
            pltpu.SemaphoreType.DMA((2, 4)),
        ],
        compiler_params=pltpu.CompilerParams(vmem_limit_bytes=60 * 1024 * 1024),
        name="density",
    )(
        valence,
        conduction,
        valence_energy,
        conduction_energy,
        pair_list.T,
        sphere_index.reshape(-1, LANES),
        *tables,
    )


def product_kernel(n_left, n_right, *refs):
    left_in, right_in = refs[:n_left], refs[n_left : n_left + n_right]
    out, left, right, left_sem, right_sem = refs[n_left + n_right :]

    @pl.when(pl.program_id(0) == 0)
    def _():
        left_slots, right_slots = left_places(lax.axis_index("col")), right_places(lax.axis_index("row"))
        copies = [
            pltpu.make_async_copy(piece, right.at[:, right_slots[j]], right_sem.at[j])
            for j, piece in enumerate(right_in)
        ] + [
            pltpu.make_async_copy(piece, left.at[left_slots[i]], left_sem.at[i])
            for i, piece in enumerate(left_in)
        ]
        for copy in copies:
            copy.start()
        for copy in copies:
            copy.wait()

    rows = out.shape[0]
    at = pl.multiple_of(pl.program_id(0) * rows, rows)
    depth = left.shape[0] * left.shape[1] * left.shape[2]
    out[...] = lax.dot_general(
        left[:, :, :, pl.ds(at, rows)].reshape(depth, rows),
        right[...].reshape(depth, right.shape[3]),
        (((0,), (0,)), ((), ())),
        preferred_element_type=F32,
    )


def product(left, right):
    n_left, n_right = len(left), len(right)
    rows, cols = left[0].shape[2], right[0].shape[2]
    block = 256
    return pl.pallas_call(
        lambda *refs: product_kernel(n_left, n_right, *refs),
        grid=(rows // block,),
        in_specs=[pl.BlockSpec(memory_space=pl.ANY)] * (n_left + n_right),
        out_specs=pl.BlockSpec((block, cols), lambda m: (m, 0)),
        out_shape=jax.ShapeDtypeStruct((rows, cols), F32),
        scratch_shapes=[
            pltpu.VMEM((n_left,) + left[0].shape, BF),
            pltpu.VMEM((right[0].shape[0], n_right) + right[0].shape[1:], BF),
            pltpu.SemaphoreType.DMA((n_left,)),
            pltpu.SemaphoreType.DMA((n_right,)),
        ],
        compiler_params=pltpu.CompilerParams(vmem_limit_bytes=24 * 1024 * 1024),
        name="product",
    )(*left, *right)


RING = 4


def shift(value, axis, step, stride):
    count = lax.axis_size(axis)
    block = RING * stride

    def target(i):
        place = i // stride % RING
        return i // block * block + (place + step) % RING * stride + i % stride

    return lax.ppermute(value, axis, [(i, target(i)) for i in range(count)])


def swap(value, axis, bit):
    count = lax.axis_size(axis)
    return lax.ppermute(value, axis, [(i, i ^ bit) for i in range(count)])


def ring(value, axis, stride, forward):
    before = shift(value, axis, 1, stride)
    after = shift(value, axis, -1, stride)
    far = shift(before, axis, 1, stride) if forward else shift(after, axis, -1, stride)
    return [value, before, after, far]


def ring_places(index, stride):
    place = lax.rem(lax.div(index, stride), RING)
    base = index - place * stride
    return [base + lax.rem(place + step, RING) * stride for step in (0, RING - 1, 1, 2)]


def right_places(row):
    return ring_places(row, 1) + ring_places(row ^ RING, 1)


def left_places(col):
    places = ring_places(col, RING) + ring_places(col ^ 2, RING)
    return places + [place ^ 1 for place in places]


def per_device(valence, conduction, valence_energy, conduction_energy, pair_list, sphere_index):
    n_row, n_col = lax.axis_size("row"), lax.axis_size("col")
    left, right = densities(
        n_row, n_col, valence, conduction, valence_energy, conduction_energy, pair_list, sphere_index
    )
    right = lax.all_to_all(right, "col", split_axis=0, concat_axis=0, tiled=True)
    right_far = swap(right, "row", 4)
    rights = ring(right, "row", 1, True)
    left = lax.all_to_all(left, "row", split_axis=0, concat_axis=0, tiled=True)
    left_far = swap(left, "col", 2)
    lefts = ring(left, "col", 4, True)
    rights += ring(right_far, "row", 1, False)
    lefts += ring(left_far, "col", 4, False)
    lefts += [swap(piece, "col", 1) for piece in lefts]
    return product(lefts, rights)


def solution(mesh):
    return jax.shard_map(
        per_device,
        mesh=mesh,
        in_specs=(
            P("row", None, None),
            P("col", None, None),
            P("row"),
            P("col"),
            P(("col", "row"), None),
            P(),
        ),
        out_specs=P("row", "col"),
        check_vma=False,
    )
```

time: 189 us -> 165 us (0.87)
  local copies, waits for them, and re-layouts: 21.7 us -> 0 us
  waiting for transfers between devices: 59.3 us -> 65.1 us
  Pallas kernels: 64.5 us -> 59.6 us
  other arithmetic: 2.62 us -> 0 us
    unnamed x42 -> x0, local copies, waits for them, and re-layouts: 20.3 us -> none
    ppermute x12, waiting for transfers between devices: 41.5 us -> 47.3 us  [shift(): return lax.ppermute(value, axis, [(i, target(i)) for i in range(count)])]
    pallas_call x1, Pallas kernels: 49.4 us -> 46.9 us  [densities(): pl.pallas_call(lambda *refs: density_kernel(n_pairs * n_row * n_col, *ref...]
    pallas_call x1, Pallas kernels: 15.1 us -> 12.7 us  [product(): pl.pallas_call(lambda *refs: product_kernel(n_left, n_right, *refs), grid...]
where the time goes in v3:
time: 165 us
  waiting for transfers between devices  65.1 us (39%)
  Pallas kernels  59.6 us (36%)
  starting transfers between devices  20.7 us (13%)
  blocking collectives  19.3 us (12%)
    ppermute x12, waiting for transfers between devices, shift(): return lax.ppermute(value, axis, [(i, target(i)) for i in range(count)])  47.3 us
    pallas_call x1, Pallas kernels, densities(): pl.pallas_call(lambda *refs: density_kernel(n_pairs * n_row * n_col, *ref...  46.9 us
    all_to_all x1, blocking collectives, per_device(): left = lax.all_to_all(left, 'row', split_axis=0, concat_axis=0, tiled=True)  19.3 us
    ppermute x12, starting transfers between devices, shift(): return lax.ppermute(value, axis, [(i, target(i)) for i in range(count)])  13.1 us
    pallas_call x1, Pallas kernels, product(): pl.pallas_call(lambda *refs: product_kernel(n_left, n_right, *refs), grid...  12.7 us
    all_to_all x1, waiting for transfers between devices, per_device(): lax.all_to_all(right, 'col', split_axis=0, concat_axis=0, tiled=True)  10.4 us
    ppermute x10, waiting for transfers between devices, swap(): return lax.ppermute(value, axis, [(i, i ^ bit) for i in range(count)])  7.33 us
    all_to_all x1, starting transfers between devices, per_device(): lax.all_to_all(right, 'col', split_axis=0, concat_axis=0, tiled=True)  5.02 us
  transfers between devices with their start and end apart: 23, of which 10 were waited for; matrix products, arithmetic and copies ran while one was open for 0% of the time, Pallas kernels for 0%

profile of v3, /device:TPU:0, one launch (start us, length us, event | category | flops | bytes accessed | tf_op | source)
XLA Modules:
  0.0 164.7 jit_solution(3738818211169131450)
XLA Ops:
  0.0 46.9 %density.1 = (bf16[8,16,2048]{2,1,0:T(8,128)(2,1)}, bf16[16,16,1024]{2,1,0:T(8,128)(2,1)}) custom-call(f32[4,64,4096]{2,1,0:T(8,128)} %refs_0_.1, f32[4,64,4096]{2,1,0:T(8,128)} %refs_1_.1, f32[4]{0:T(128)} %refs_2_.1, f32[4]{0:T(128)} %refs_3_.1, s32[2,8]{1,0:T(2,128)} %bitcast.3, s32[128,128]{1,0:T(8,128)} %bitcast.2, ...), custom_call_target="tpu_custom_call" | custom-call | tf_op jit(solution)/shard_map/density/pallas_call | solution.py:269
  46.9 19.3 %all_to_all.10.refs_0_ = bf16[8,16,2048]{2,1,0:T(8,128)(2,1)S(1)} all-to-all(bf16[8,16,2048]{2,1,0:T(8,128)(2,1)} %get-tuple-element.7), channel_id=1, replica_groups=mesh['col'=16,'row'=8] {'row'}, dimensions={0} | all-to-all | bytes 1048576 | tf_op jit(solution)/shard_map/all_to_all | solution.py:409
  66.2 1.0 collective-permute-start.3
  67.2 5.0 %all-to-all-start.1 = ((bf16[16,16,1024]{2,1,0:T(8,128)(2,1)}), bf16[16,16,1024]{2,1,0:T(8,128)(2,1)S(1)}, u32[]{:S(2)}, u32[]{:S(2)}) async-start(bf16[16,16,1024]{2,1,0:T(8,128)(2,1)} %get-tuple-element.8), calls=%async_computation.1 | async-start | bytes 1048576 | tf_op jit(solution)/shard_map/all_to_all | solution.py:406
  72.3 3.1 %collective-permute-start.1 = (bf16[8,16,2048]{2,1,0:T(8,128)(2,1)S(1)}, bf16[8,16,2048]{2,1,0:T(8,128)(2,1)S(1)}, u32[]{:S(2)}, u32[]{:S(2)}) collective-permute-start(bf16[8,16,2048]{2,1,0:T(8,128)(2,1)S(1)} %all_to_all.10.refs_0_), channel_id=1, source_target_pairs={{0,96},{8,104},{16,112},{24,120},{32,0},{40,8},{48,16},{56,24},{64... | collective-permute-start | bytes 1572872 | tf_op jit(solution)/shard_map/ppermute | solution.py:371
  75.4 10.4 %all-to-all-done.1.refs_16_ = bf16[16,16,1024]{2,1,0:T(8,128)(2,1)S(1)} async-done(((bf16[16,16,1024]{2,1,0:T(8,128)(2,1)}), bf16[16,16,1024]{2,1,0:T(8,128)(2,1)S(1)}, u32[]{:S(2)}, u32[]{:S(2)}) %all-to-all-start.1) | async-done | bytes 524320 | tf_op jit(solution)/shard_map/all_to_all | solution.py:406
  86.4 1.5 collective-permute-start.16
  87.8 0.6 collective-permute-start.15
  88.4 3.8 %collective-permute-done.1.refs_2_ = bf16[8,16,2048]{2,1,0:T(8,128)(2,1)S(1)} collective-permute-done((bf16[8,16,2048]{2,1,0:T(8,128)(2,1)S(1)}, bf16[8,16,2048]{2,1,0:T(8,128)(2,1)S(1)}, u32[]{:S(2)}, u32[]{:S(2)}) %collective-permute-start.1) | collective-permute-done | bytes 524320 | tf_op jit(solution)/shard_map/ppermute | solution.py:371
  92.3 1.2 collective-permute-done.refs_1_
  93.5 0.9 collective-permute-start.5
  94.3 7.3 %collective-permute-done.18.refs_20_ = bf16[16,16,1024]{2,1,0:T(8,128)(2,1)S(1)} collective-permute-done((bf16[16,16,1024]{2,1,0:T(8,128)(2,1)S(1)}, bf16[16,16,1024]{2,1,0:T(8,128)(2,1)S(1)}, u32[]{:S(2)}, u32[]{:S(2)}) %collective-permute-start.18) | collective-permute-done | bytes 524320 | tf_op jit(solution)/shard_map/ppermute | solution.py:376
  101.6 1.6 collective-permute-start.4
  103.7 1.6 collective-permute-start.2
  105.3 1.6 collective-permute-done.5.refs_6_
  106.9 1.1 collective-permute-start.20
  108.0 9.6 %collective-permute-done.4.refs_5_ = bf16[8,16,2048]{2,1,0:T(8,128)(2,1)S(1)} collective-permute-done((bf16[8,16,2048]{2,1,0:T(8,128)(2,1)S(1)}, bf16[8,16,2048]{2,1,0:T(8,128)(2,1)S(1)}, u32[]{:S(2)}, u32[]{:S(2)}) %collective-permute-start.4) | collective-permute-done | bytes 524320 | tf_op jit(solution)/shard_map/ppermute | solution.py:371
  117.7 0.9 collective-permute-start.19
  118.6 1.9 %collective-permute-start.6 = (bf16[8,16,2048]{2,1,0:T(8,128)(2,1)S(1)}, bf16[8,16,2048]{2,1,0:T(8,128)(2,1)S(1)}, u32[]{:S(2)}, u32[]{:S(2)}) collective-permute-start(bf16[8,16,2048]{2,1,0:T(8,128)(2,1)S(1)} %collective-permute-done.5.refs_6_), channel_id=1, source_target_pairs={{0,96},{8,104},{16,112},{24,120},{32,0},{40,8},{48,16},{56,24},{64... | collective-permute-start | bytes 1572872 | tf_op jit(solution)/shard_map/ppermute | solution.py:371
  120.4 7.2 %collective-permute-done.2.refs_3_ = bf16[8,16,2048]{2,1,0:T(8,128)(2,1)S(1)} collective-permute-done((bf16[8,16,2048]{2,1,0:T(8,128)(2,1)S(1)}, bf16[8,16,2048]{2,1,0:T(8,128)(2,1)S(1)}, u32[]{:S(2)}, u32[]{:S(2)}) %collective-permute-start.2) | collective-permute-done | bytes 524320 | tf_op jit(solution)/shard_map/ppermute | solution.py:371
  128.2 5.6 %collective-permute-done.19.refs_21_ = bf16[16,16,1024]{2,1,0:T(8,128)(2,1)S(1)} collective-permute-done((bf16[16,16,1024]{2,1,0:T(8,128)(2,1)S(1)}, bf16[16,16,1024]{2,1,0:T(8,128)(2,1)S(1)}, u32[]{:S(2)}, u32[]{:S(2)}) %collective-permute-start.19) | collective-permute-done | bytes 524320 | tf_op jit(solution)/shard_map/ppermute | solution.py:371
  133.7 7.8 %collective-permute-done.17.refs_19_ = bf16[16,16,1024]{2,1,0:T(8,128)(2,1)S(1)} collective-permute-done((bf16[16,16,1024]{2,1,0:T(8,128)(2,1)S(1)}, bf16[16,16,1024]{2,1,0:T(8,128)(2,1)S(1)}, u32[]{:S(2)}, u32[]{:S(2)}) %collective-permute-start.17) | collective-permute-done | bytes 524320 | tf_op jit(solution)/shard_map/ppermute | solution.py:371
  141.6 10.5 %collective-permute-done.21.refs_23_ = bf16[16,16,1024]{2,1,0:T(8,128)(2,1)S(1)} collective-permute-done((bf16[16,16,1024]{2,1,0:T(8,128)(2,1)S(1)}, bf16[16,16,1024]{2,1,0:T(8,128)(2,1)S(1)}, u32[]{:S(2)}, u32[]{:S(2)}) %collective-permute-start.21) | collective-permute-done | bytes 524320 | tf_op jit(solution)/shard_map/ppermute | solution.py:371
  152.1 12.7 %product.1 = f32[2048,1024]{1,0:T(8,128)} custom-call(bf16[8,16,2048]{2,1,0:T(8,128)(2,1)S(1)} %all_to_all.10.refs_0_, bf16[8,16,2048]{2,1,0:T(8,128)(2,1)S(1)} %collective-permute-done.refs_1_, bf16[8,16,2048]{2,1,0:T(8,128)(2,1)S(1)} %collective-permute-done.1.refs_2_, bf16[8,16,2048]{2,1,0:T(8,128)(2,1)S(1)} %collective-permute-done.2.refs_3_, ...), custom_call_target="tpu_custom_call" | custom-call | tf_op jit(solution)/shard_map/product/pallas_call | solution.py:343
  (25 shorter events, 1.7 us)
Async XLA Ops:
  66.2 20.2 %collective-permute-start.7 = (bf16[8,16,2048]{2,1,0:T(8,128)(2,1)S(1)}, bf16[8,16,2048]{2,1,0:T(8,128)(2,1)S(1)}, u32[]{:S(2)}, u32[]{:S(2)}) collective-permute-start(bf16[8,16,2048]{2,1,0:T(8,128)(2,1)S(1)} %all_to_all.10.refs_0_), channel_id=1, source_target_pairs={{0,8},{8,0},{16,24},{24,16},{32,40},{40,32},{48,56},{56,48},{64,72... | collective-permute-start | bytes 1572872 | tf_op jit(solution)/shard_map/ppermute | solution.py:376
  66.2 21.6 %collective-permute-start.3 = (bf16[8,16,2048]{2,1,0:T(8,128)(2,1)S(1)}, bf16[8,16,2048]{2,1,0:T(8,128)(2,1)S(1)}, u32[]{:S(2)}, u32[]{:S(2)}) collective-permute-start(bf16[8,16,2048]{2,1,0:T(8,128)(2,1)S(1)} %all_to_all.10.refs_0_), channel_id=1, source_target_pairs={{0,16},{8,24},{16,0},{24,8},{32,48},{40,56},{48,32},{56,40},{64,80... | collective-permute-start | bytes 1572872 | tf_op jit(solution)/shard_map/ppermute | solution.py:376
  67.2 18.6 %all-to-all-start.1 = ((bf16[16,16,1024]{2,1,0:T(8,128)(2,1)}), bf16[16,16,1024]{2,1,0:T(8,128)(2,1)S(1)}, u32[]{:S(2)}, u32[]{:S(2)}) async-start(bf16[16,16,1024]{2,1,0:T(8,128)(2,1)} %get-tuple-element.8), calls=%async_computation.1 | async-start | bytes 1048576 | tf_op jit(solution)/shard_map/all_to_all | solution.py:406
  72.3 20.0 %collective-permute-start.1 = (bf16[8,16,2048]{2,1,0:T(8,128)(2,1)S(1)}, bf16[8,16,2048]{2,1,0:T(8,128)(2,1)S(1)}, u32[]{:S(2)}, u32[]{:S(2)}) collective-permute-start(bf16[8,16,2048]{2,1,0:T(8,128)(2,1)S(1)} %all_to_all.10.refs_0_), channel_id=1, source_target_pairs={{0,96},{8,104},{16,112},{24,120},{32,0},{40,8},{48,16},{56,24},{64... | collective-permute-start | bytes 1572872 | tf_op jit(solution)/shard_map/ppermute | solution.py:371
  75.4 18.1 %collective-permute-start = (bf16[8,16,2048]{2,1,0:T(8,128)(2,1)S(1)}, bf16[8,16,2048]{2,1,0:T(8,128)(2,1)S(1)}, u32[]{:S(2)}, u32[]{:S(2)}) collective-permute-start(bf16[8,16,2048]{2,1,0:T(8,128)(2,1)S(1)} %all_to_all.10.refs_0_), channel_id=1, source_target_pairs={{0,32},{8,40},{16,48},{24,56},{32,64},{40,72},{48,80},{56,88},{64,... | collective-permute-start | bytes 1572872 | tf_op jit(solution)/shard_map/ppermute | solution.py:371
  85.8 15.8 %collective-permute-start.18 = (bf16[16,16,1024]{2,1,0:T(8,128)(2,1)S(1)}, bf16[16,16,1024]{2,1,0:T(8,128)(2,1)S(1)}, u32[]{:S(2)}, u32[]{:S(2)}) collective-permute-start(bf16[16,16,1024]{2,1,0:T(8,128)(2,1)S(1)} %all-to-all-done.1.refs_16_), channel_id=1, source_target_pairs={{0,4},{1,5},{2,6},{3,7},{4,0},{5,1},{6,2},{7,3},{8,12},{9,13},{10,... | collective-permute-start | bytes 1572872 | tf_op jit(solution)/shard_map/ppermute | solution.py:376
  86.4 16.8 %collective-permute-start.16 = (bf16[16,16,1024]{2,1,0:T(8,128)(2,1)S(1)}, bf16[16,16,1024]{2,1,0:T(8,128)(2,1)S(1)}, u32[]{:S(2)}, u32[]{:S(2)}) collective-permute-start(bf16[16,16,1024]{2,1,0:T(8,128)(2,1)S(1)} %all-to-all-done.1.refs_16_), channel_id=1, source_target_pairs={{0,3},{1,0},{2,1},{3,2},{4,7},{5,4},{6,5},{7,6},{8,11},{9,8},{10,9... | collective-permute-start | bytes 1572872 | tf_op jit(solution)/shard_map/ppermute | solution.py:371
  87.8 15.4 %collective-permute-start.15 = (bf16[16,16,1024]{2,1,0:T(8,128)(2,1)S(1)}, bf16[16,16,1024]{2,1,0:T(8,128)(2,1)S(1)}, u32[]{:S(2)}, u32[]{:S(2)}) collective-permute-start(bf16[16,16,1024]{2,1,0:T(8,128)(2,1)S(1)} %all-to-all-done.1.refs_16_), channel_id=1, source_target_pairs={{0,1},{1,2},{2,3},{3,0},{4,5},{5,6},{6,7},{7,4},{8,9},{9,10},{10,1... | collective-permute-start | bytes 1572872 | tf_op jit(solution)/shard_map/ppermute | solution.py:371
  92.2 11.5 %collective-permute-start.11 = (bf16[8,16,2048]{2,1,0:T(8,128)(2,1)S(1)}, bf16[8,16,2048]{2,1,0:T(8,128)(2,1)S(1)}, u32[]{:S(2)}, u32[]{:S(2)}) collective-permute-start(bf16[8,16,2048]{2,1,0:T(8,128)(2,1)S(1)} %collective-permute-done.3.refs_4_), channel_id=1, source_target_pairs={{0,8},{8,0},{16,24},{24,16},{32,40},{40,32},{48,56},{56,48},{64,72... | collective-permute-start | bytes 1572872 | tf_op jit(solution)/shard_map/ppermute | solution.py:376
  93.5 13.5 %collective-permute-start.5 = (bf16[8,16,2048]{2,1,0:T(8,128)(2,1)S(1)}, bf16[8,16,2048]{2,1,0:T(8,128)(2,1)S(1)}, u32[]{:S(2)}, u32[]{:S(2)}) collective-permute-start(bf16[8,16,2048]{2,1,0:T(8,128)(2,1)S(1)} %collective-permute-done.3.refs_4_), channel_id=1, source_target_pairs={{0,96},{8,104},{16,112},{24,120},{32,0},{40,8},{48,16},{56,24},{64... | collective-permute-start | bytes 1572872 | tf_op jit(solution)/shard_map/ppermute | solution.py:371
  101.6 16.0 %collective-permute-start.4 = (bf16[8,16,2048]{2,1,0:T(8,128)(2,1)S(1)}, bf16[8,16,2048]{2,1,0:T(8,128)(2,1)S(1)}, u32[]{:S(2)}, u32[]{:S(2)}) collective-permute-start(bf16[8,16,2048]{2,1,0:T(8,128)(2,1)S(1)} %collective-permute-done.3.refs_4_), channel_id=1, source_target_pairs={{0,32},{8,40},{16,48},{24,56},{32,64},{40,72},{48,80},{56,88},{64,... | collective-permute-start | bytes 1572872 | tf_op jit(solution)/shard_map/ppermute | solution.py:371
  103.2 15.4 %collective-permute-start.9 = (bf16[8,16,2048]{2,1,0:T(8,128)(2,1)S(1)}, bf16[8,16,2048]{2,1,0:T(8,128)(2,1)S(1)}, u32[]{:S(2)}, u32[]{:S(2)}) collective-permute-start(bf16[8,16,2048]{2,1,0:T(8,128)(2,1)S(1)} %collective-permute-done.1.refs_2_), channel_id=1, source_target_pairs={{0,8},{8,0},{16,24},{24,16},{32,40},{40,32},{48,56},{56,48},{64,72... | collective-permute-start | bytes 1572872 | tf_op jit(solution)/shard_map/ppermute | solution.py:376
  103.2 15.4 %collective-permute-start.8 = (bf16[8,16,2048]{2,1,0:T(8,128)(2,1)S(1)}, bf16[8,16,2048]{2,1,0:T(8,128)(2,1)S(1)}, u32[]{:S(2)}, u32[]{:S(2)}) collective-permute-start(bf16[8,16,2048]{2,1,0:T(8,128)(2,1)S(1)} %collective-permute-done.refs_1_), channel_id=1, source_target_pairs={{0,8},{8,0},{16,24},{24,16},{32,40},{40,32},{48,56},{56,48},{64,72... | collective-permute-start | bytes 1572872 | tf_op jit(solution)/shard_map/ppermute | solution.py:376
  103.7 23.9 %collective-permute-start.2 = (bf16[8,16,2048]{2,1,0:T(8,128)(2,1)S(1)}, bf16[8,16,2048]{2,1,0:T(8,128)(2,1)S(1)}, u32[]{:S(2)}, u32[]{:S(2)}) collective-permute-start(bf16[8,16,2048]{2,1,0:T(8,128)(2,1)S(1)} %collective-permute-done.refs_1_), channel_id=1, source_target_pairs={{0,32},{8,40},{16,48},{24,56},{32,64},{40,72},{48,80},{56,88},{64,... | collective-permute-start | bytes 1572872 | tf_op jit(solution)/shard_map/ppermute | solution.py:371
  106.9 20.7 %collective-permute-start.20 = (bf16[16,16,1024]{2,1,0:T(8,128)(2,1)S(1)}, bf16[16,16,1024]{2,1,0:T(8,128)(2,1)S(1)}, u32[]{:S(2)}, u32[]{:S(2)}) collective-permute-start(bf16[16,16,1024]{2,1,0:T(8,128)(2,1)S(1)} %collective-permute-done.18.refs_20_), channel_id=1, source_target_pairs={{0,3},{1,0},{2,1},{3,2},{4,7},{5,4},{6,5},{7,6},{8,11},{9,8},{10,9... | collective-permute-start | bytes 1572872 | tf_op jit(solution)/shard_map/ppermute | solution.py:371
  117.7 16.1 %collective-permute-start.19 = (bf16[16,16,1024]{2,1,0:T(8,128)(2,1)S(1)}, bf16[16,16,1024]{2,1,0:T(8,128)(2,1)S(1)}, u32[]{:S(2)}, u32[]{:S(2)}) collective-permute-start(bf16[16,16,1024]{2,1,0:T(8,128)(2,1)S(1)} %collective-permute-done.18.refs_20_), channel_id=1, source_target_pairs={{0,1},{1,2},{2,3},{3,0},{4,5},{5,6},{6,7},{7,4},{8,9},{9,10},{10,1... | collective-permute-start | bytes 1572872 | tf_op jit(solution)/shard_map/ppermute | solution.py:371
  118.6 23.0 %collective-permute-start.17 = (bf16[16,16,1024]{2,1,0:T(8,128)(2,1)S(1)}, bf16[16,16,1024]{2,1,0:T(8,128)(2,1)S(1)}, u32[]{:S(2)}, u32[]{:S(2)}) collective-permute-start(bf16[16,16,1024]{2,1,0:T(8,128)(2,1)S(1)} %collective-permute-done.15.refs_17_), channel_id=1, source_target_pairs={{0,1},{1,2},{2,3},{3,0},{4,5},{5,6},{6,7},{7,4},{8,9},{9,10},{10,1... | collective-permute-start | bytes 1572872 | tf_op jit(solution)/shard_map/ppermute | solution.py:371
  118.6 23.0 %collective-permute-start.6 = (bf16[8,16,2048]{2,1,0:T(8,128)(2,1)S(1)}, bf16[8,16,2048]{2,1,0:T(8,128)(2,1)S(1)}, u32[]{:S(2)}, u32[]{:S(2)}) collective-permute-start(bf16[8,16,2048]{2,1,0:T(8,128)(2,1)S(1)} %collective-permute-done.5.refs_6_), channel_id=1, source_target_pairs={{0,96},{8,104},{16,112},{24,120},{32,0},{40,8},{48,16},{56,24},{64... | collective-permute-start | bytes 1572872 | tf_op jit(solution)/shard_map/ppermute | solution.py:371
  127.6 13.9 %collective-permute-start.13 = (bf16[8,16,2048]{2,1,0:T(8,128)(2,1)S(1)}, bf16[8,16,2048]{2,1,0:T(8,128)(2,1)S(1)}, u32[]{:S(2)}, u32[]{:S(2)}) collective-permute-start(bf16[8,16,2048]{2,1,0:T(8,128)(2,1)S(1)} %collective-permute-done.5.refs_6_), channel_id=1, source_target_pairs={{0,8},{8,0},{16,24},{24,16},{32,40},{40,32},{48,56},{56,48},{64,72... | collective-permute-start | bytes 1572872 | tf_op jit(solution)/shard_map/ppermute | solution.py:376
  127.6 13.9 %collective-permute-start.12 = (bf16[8,16,2048]{2,1,0:T(8,128)(2,1)S(1)}, bf16[8,16,2048]{2,1,0:T(8,128)(2,1)S(1)}, u32[]{:S(2)}, u32[]{:S(2)}) collective-permute-start(bf16[8,16,2048]{2,1,0:T(8,128)(2,1)S(1)} %collective-permute-done.4.refs_5_), channel_id=1, source_target_pairs={{0,8},{8,0},{16,24},{24,16},{32,40},{40,32},{48,56},{56,48},{64,72... | collective-permute-start | bytes 1572872 | tf_op jit(solution)/shard_map/ppermute | solution.py:376
  133.7 7.9 %collective-permute-start.10 = (bf16[8,16,2048]{2,1,0:T(8,128)(2,1)S(1)}, bf16[8,16,2048]{2,1,0:T(8,128)(2,1)S(1)}, u32[]{:S(2)}, u32[]{:S(2)}) collective-permute-start(bf16[8,16,2048]{2,1,0:T(8,128)(2,1)S(1)} %collective-permute-done.2.refs_3_), channel_id=1, source_target_pairs={{0,8},{8,0},{16,24},{24,16},{32,40},{40,32},{48,56},{56,48},{64,72... | collective-permute-start | bytes 1572872 | tf_op jit(solution)/shard_map/ppermute | solution.py:376
  141.5 10.5 %collective-permute-start.21 = (bf16[16,16,1024]{2,1,0:T(8,128)(2,1)S(1)}, bf16[16,16,1024]{2,1,0:T(8,128)(2,1)S(1)}, u32[]{:S(2)}, u32[]{:S(2)}) collective-permute-start(bf16[16,16,1024]{2,1,0:T(8,128)(2,1)S(1)} %collective-permute-done.20.refs_22_), channel_id=1, source_target_pairs={{0,3},{1,0},{2,1},{3,2},{4,7},{5,4},{6,5},{7,6},{8,11},{9,8},{10,9... | collective-permute-start | bytes 1572872 | tf_op jit(solution)/shard_map/ppermute | solution.py:371
  141.5 10.5 %collective-permute-start.14 = (bf16[8,16,2048]{2,1,0:T(8,128)(2,1)S(1)}, bf16[8,16,2048]{2,1,0:T(8,128)(2,1)S(1)}, u32[]{:S(2)}, u32[]{:S(2)}) collective-permute-start(bf16[8,16,2048]{2,1,0:T(8,128)(2,1)S(1)} %collective-permute-done.6.refs_7_), channel_id=1, source_target_pairs={{0,8},{8,0},{16,24},{24,16},{32,40},{40,32},{48,56},{56,48},{64,72... | collective-permute-start | bytes 1572872 | tf_op jit(solution)/shard_map/ppermute | solution.py:376

commit v4 on v3

--- a/solution.py
+++ b/solution.py
@@ -312,7 +312,8 @@
 
     @pl.when(pl.program_id(0) == 0)
     def _():
-        left_slots, right_slots = left_places(lax.axis_index("col")), right_places(lax.axis_index("row"))
+        col = lax.axis_index("col")
+        left_slots, right_slots = left_places(col), right_places(lax.axis_index("row"), col & 1)
         copies = [
             pltpu.make_async_copy(piece, right.at[:, right_slots[j]], right_sem.at[j])
             for j, piece in enumerate(right_in)
@@ -360,15 +361,20 @@
 RING = 4
 
 
-def shift(value, axis, step, stride):
-    count = lax.axis_size(axis)
-    block = RING * stride
-
-    def target(i):
+def shift(value, axis, stride, way):
+    n_col, n_row = lax.axis_size("col"), lax.axis_size("row")
+
+    def moved(i, step):
         place = i // stride % RING
-        return i // block * block + (place + step) % RING * stride + i % stride
-
-    return lax.ppermute(value, axis, [(i, target(i)) for i in range(count)])
+        return i + ((place + step) % RING - place) * stride
+
+    pairs = []
+    for col in range(n_col):
+        for row in range(n_row):
+            step = way if col % 2 == 0 else -way
+            to = (moved(col, step), row) if axis == "col" else (col, moved(row, step))
+            pairs.append((col * n_row + row, to[0] * n_row + to[1]))
+    return lax.ppermute(value, ("col", "row"), pairs)
 
 
 def swap(value, axis, bit):
@@ -376,26 +382,22 @@
     return lax.ppermute(value, axis, [(i, i ^ bit) for i in range(count)])
 
 
-def ring(value, axis, stride, forward):
-    before = shift(value, axis, 1, stride)
-    after = shift(value, axis, -1, stride)
-    far = shift(before, axis, 1, stride) if forward else shift(after, axis, -1, stride)
-    return [value, before, after, far]
-
-
-def ring_places(index, stride):
+def ring_places(index, stride, core):
     place = lax.rem(lax.div(index, stride), RING)
     base = index - place * stride
-    return [base + lax.rem(place + step, RING) * stride for step in (0, RING - 1, 1, 2)]
-
-
-def right_places(row):
-    return ring_places(row, 1) + ring_places(row ^ RING, 1)
+    way = 1 - 2 * core
+    return [base + lax.rem(place + step, RING) * stride for step in (0, RING - way, RING + way, 2)]
+
+
+def right_places(row, core):
+    return ring_places(row, 1, core) + ring_places(row ^ RING, 1, core)
 
 
 def left_places(col):
-    places = ring_places(col, RING) + ring_places(col ^ 2, RING)
-    return places + [place ^ 1 for place in places]
+    core = col & 1
+    mine = ring_places(col, RING, core) + ring_places(col ^ 2, RING, core)
+    theirs = ring_places(col ^ 1, RING, 1 - core) + ring_places(col ^ 3, RING, 1 - core)
+    return mine + theirs
 
 
 def per_device(valence, conduction, valence_energy, conduction_energy, pair_list, sphere_index):
@@ -403,14 +405,17 @@
     left, right = densities(
         n_row, n_col, valence, conduction, valence_energy, conduction_energy, pair_list, sphere_index
     )
+    left = lax.all_to_all(left, "row", split_axis=0, concat_axis=0, tiled=True)
+    left, right = lax.optimization_barrier((left, right))
+    left_z = swap(left, "col", 2)
+    lefts = [left, shift(left, "col", RING, 1), shift(left, "col", RING, -1)]
     right = lax.all_to_all(right, "col", split_axis=0, concat_axis=0, tiled=True)
-    right_far = swap(right, "row", 4)
-    rights = ring(right, "row", 1, True)
-    left = lax.all_to_all(left, "row", split_axis=0, concat_axis=0, tiled=True)
-    left_far = swap(left, "col", 2)
-    lefts = ring(left, "col", 4, True)
-    rights += ring(right_far, "row", 1, False)
-    lefts += ring(left_far, "col", 4, False)
+    right_z = swap(right, "row", RING)
+    rights = [right, shift(right, "row", 1, 1), shift(right, "row", 1, -1)]
+    lefts += [shift(lefts[1], "col", RING, 1), left_z, shift(left_z, "col", RING, 1), shift(left_z, "col", RING, -1)]
+    rights += [shift(rights[1], "row", 1, 1), right_z, shift(right_z, "row", 1, 1), shift(right_z, "row", 1, -1)]
+    lefts += [shift(lefts[5], "col", RING, 1)]
+    rights += [shift(rights[5], "row", 1, 1)]
     lefts += [swap(piece, "col", 1) for piece in lefts]
     return product(lefts, rights)
 

time: 165 us -> 151 us (0.915)
  waiting for transfers between devices: 65.1 us -> 52 us
    ppermute x12, waiting for transfers between devices: 47.3 us -> 34.3 us  [shift(): return lax.ppermute(value, ('col', 'row'), pairs)]
    ppermute x12, starting transfers between devices: 13.1 us -> 11.2 us  [shift(): return lax.ppermute(value, ('col', 'row'), pairs)]
  transfers between devices with their start and end apart: 23 -> 23, of which waited for: 10 -> 9; matrix products, arithmetic and copies ran while one was open for 0% -> 0% of each run, Pallas kernels for 0% -> 0%
where the time goes in v4:
time: 151 us
  Pallas kernels  59.6 us (39%)
  waiting for transfers between devices  52 us (34%)
  starting transfers between devices  20.1 us (13%)
  blocking collectives  19.3 us (13%)
    pallas_call x1, Pallas kernels, densities(): pl.pallas_call(lambda *refs: density_kernel(n_pairs * n_row * n_col, *ref...  46.9 us
    ppermute x12, waiting for transfers between devices, shift(): return lax.ppermute(value, ('col', 'row'), pairs)  34.3 us
    all_to_all x1, blocking collectives, per_device(): left = lax.all_to_all(left, 'row', split_axis=0, concat_axis=0, tiled=True)  19.3 us
    pallas_call x1, Pallas kernels, product(): pl.pallas_call(lambda *refs: product_kernel(n_left, n_right, *refs), grid...  12.6 us
    ppermute x12, starting transfers between devices, shift(): return lax.ppermute(value, ('col', 'row'), pairs)  11.2 us
    all_to_all x1, waiting for transfers between devices, per_device(): lax.all_to_all(right, 'col', split_axis=0, concat_axis=0, tiled=True)  10.4 us
    ppermute x10, waiting for transfers between devices, swap(): return lax.ppermute(value, axis, [(i, i ^ bit) for i in range(count)])  7.33 us
    all_to_all x1, starting transfers between devices, per_device(): lax.all_to_all(right, 'col', split_axis=0, concat_axis=0, tiled=True)  5.02 us
  transfers between devices with their start and end apart: 23, of which 9 were waited for; matrix products, arithmetic and copies ran while one was open for 0% of the time, Pallas kernels for 0%

profile of v4, /device:TPU:0, one launch (start us, length us, event | category | flops | bytes accessed | tf_op | source)
XLA Modules:
  0.0 151.1 jit_solution(13414990706656379237)
XLA Ops:
  0.0 46.9 %density.1 = (bf16[8,16,2048]{2,1,0:T(8,128)(2,1)}, bf16[16,16,1024]{2,1,0:T(8,128)(2,1)}) custom-call(f32[4,64,4096]{2,1,0:T(8,128)} %refs_0_.1, f32[4,64,4096]{2,1,0:T(8,128)} %refs_1_.1, f32[4]{0:T(128)} %refs_2_.1, f32[4]{0:T(128)} %refs_3_.1, s32[2,8]{1,0:T(2,128)} %bitcast.3, s32[128,128]{1,0:T(8,128)} %bitcast.2, ...), custom_call_target="tpu_custom_call" | custom-call | tf_op jit(solution)/shard_map/density/pallas_call | solution.py:269
  46.9 19.3 %all_to_all.10.refs_0_ = bf16[8,16,2048]{2,1,0:T(8,128)(2,1)S(1)} all-to-all(bf16[8,16,2048]{2,1,0:T(8,128)(2,1)} %get-tuple-element.9), channel_id=1, replica_groups=mesh['col'=16,'row'=8] {'row'}, dimensions={0} | all-to-all | bytes 1048576 | tf_op jit(solution)/shard_map/all_to_all | solution.py:408
  66.2 1.0 collective-permute-start.3
  67.2 5.0 %all-to-all-start.1 = ((bf16[16,16,1024]{2,1,0:T(8,128)(2,1)}), bf16[16,16,1024]{2,1,0:T(8,128)(2,1)S(1)}, u32[]{:S(2)}, u32[]{:S(2)}) async-start(bf16[16,16,1024]{2,1,0:T(8,128)(2,1)} %get-tuple-element.12), calls=%async_computation.1 | async-start | bytes 1048576 | tf_op jit(solution)/shard_map/all_to_all | solution.py:412
  72.3 3.1 %collective-permute-start.1 = (bf16[8,16,2048]{2,1,0:T(8,128)(2,1)S(1)}, bf16[8,16,2048]{2,1,0:T(8,128)(2,1)S(1)}, u32[]{:S(2)}, u32[]{:S(2)}) collective-permute-start(bf16[8,16,2048]{2,1,0:T(8,128)(2,1)S(1)} %all_to_all.10.refs_0_), channel_id=1, source_target_pairs={{0,96},{1,97},{2,98},{3,99},{4,100},{5,101},{6,102},{7,103},{8,40}... | collective-permute-start | bytes 1572872 | tf_op jit(solution)/shard_map/ppermute | solution.py:377
  75.4 10.4 %all-to-all-done.1.refs_16_ = bf16[16,16,1024]{2,1,0:T(8,128)(2,1)S(1)} async-done(((bf16[16,16,1024]{2,1,0:T(8,128)(2,1)}), bf16[16,16,1024]{2,1,0:T(8,128)(2,1)S(1)}, u32[]{:S(2)}, u32[]{:S(2)}) %all-to-all-start.1) | async-done | bytes 524320 | tf_op jit(solution)/shard_map/all_to_all | solution.py:412
  85.8 0.6 collective-permute-start.18
  86.4 1.5 collective-permute-start.16
  87.8 0.6 collective-permute-start.15
  88.4 3.8 %collective-permute-done.1.refs_2_ = bf16[8,16,2048]{2,1,0:T(8,128)(2,1)S(1)} collective-permute-done((bf16[8,16,2048]{2,1,0:T(8,128)(2,1)S(1)}, bf16[8,16,2048]{2,1,0:T(8,128)(2,1)S(1)}, u32[]{:S(2)}, u32[]{:S(2)}) %collective-permute-start.1) | collective-permute-done | bytes 524320 | tf_op jit(solution)/shard_map/ppermute | solution.py:377
  92.2 0.8 collective-permute-start.11
  93.5 0.9 collective-permute-start.5
  94.3 7.3 %collective-permute-done.18.refs_20_ = bf16[16,16,1024]{2,1,0:T(8,128)(2,1)S(1)} collective-permute-done((bf16[16,16,1024]{2,1,0:T(8,128)(2,1)S(1)}, bf16[16,16,1024]{2,1,0:T(8,128)(2,1)S(1)}, u32[]{:S(2)}, u32[]{:S(2)}) %collective-permute-start.18) | collective-permute-done | bytes 524320 | tf_op jit(solution)/shard_map/ppermute | solution.py:382
  101.6 1.6 %collective-permute-start.4 = (bf16[8,16,2048]{2,1,0:T(8,128)(2,1)S(1)}, bf16[8,16,2048]{2,1,0:T(8,128)(2,1)S(1)}, u32[]{:S(2)}, u32[]{:S(2)}) collective-permute-start(bf16[8,16,2048]{2,1,0:T(8,128)(2,1)S(1)} %collective-permute-done.3.refs_4_), channel_id=1, source_target_pairs={{0,32},{1,33},{2,34},{3,35},{4,36},{5,37},{6,38},{7,39},{8,104},{9... | collective-permute-start | bytes 1572872 | tf_op jit(solution)/shard_map/ppermute | solution.py:377
  103.2 0.8 collective-permute-start.9
  104.1 1.2 collective-permute-start.2
  105.3 1.1 collective-permute-start.20
  106.4 5.6 %collective-permute-done.4.refs_5_ = bf16[8,16,2048]{2,1,0:T(8,128)(2,1)S(1)} collective-permute-done((bf16[8,16,2048]{2,1,0:T(8,128)(2,1)S(1)}, bf16[8,16,2048]{2,1,0:T(8,128)(2,1)S(1)}, u32[]{:S(2)}, u32[]{:S(2)}) %collective-permute-start.4) | collective-permute-done | bytes 524320 | tf_op jit(solution)/shard_map/ppermute | solution.py:377
  112.0 0.9 collective-permute-start.19
  113.3 4.3 %collective-permute-done.2.refs_3_ = bf16[8,16,2048]{2,1,0:T(8,128)(2,1)S(1)} collective-permute-done((bf16[8,16,2048]{2,1,0:T(8,128)(2,1)S(1)}, bf16[8,16,2048]{2,1,0:T(8,128)(2,1)S(1)}, u32[]{:S(2)}, u32[]{:S(2)}) %collective-permute-start.2) | collective-permute-done | bytes 524320 | tf_op jit(solution)/shard_map/ppermute | solution.py:377
  118.1 4.3 %collective-permute-done.19.refs_21_ = bf16[16,16,1024]{2,1,0:T(8,128)(2,1)S(1)} collective-permute-done((bf16[16,16,1024]{2,1,0:T(8,128)(2,1)S(1)}, bf16[16,16,1024]{2,1,0:T(8,128)(2,1)S(1)}, u32[]{:S(2)}, u32[]{:S(2)}) %collective-permute-start.19) | collective-permute-done | bytes 524320 | tf_op jit(solution)/shard_map/ppermute | solution.py:377
  122.4 5.6 %collective-permute-done.17.refs_19_ = bf16[16,16,1024]{2,1,0:T(8,128)(2,1)S(1)} collective-permute-done((bf16[16,16,1024]{2,1,0:T(8,128)(2,1)S(1)}, bf16[16,16,1024]{2,1,0:T(8,128)(2,1)S(1)}, u32[]{:S(2)}, u32[]{:S(2)}) %collective-permute-start.17) | collective-permute-done | bytes 524320 | tf_op jit(solution)/shard_map/ppermute | solution.py:377
  128.1 10.3 %collective-permute-done.21.refs_23_ = bf16[16,16,1024]{2,1,0:T(8,128)(2,1)S(1)} collective-permute-done((bf16[16,16,1024]{2,1,0:T(8,128)(2,1)S(1)}, bf16[16,16,1024]{2,1,0:T(8,128)(2,1)S(1)}, u32[]{:S(2)}, u32[]{:S(2)}) %collective-permute-start.21) | collective-permute-done | bytes 524320 | tf_op jit(solution)/shard_map/ppermute | solution.py:377
  138.4 12.6 %product.1 = f32[2048,1024]{1,0:T(8,128)} custom-call(bf16[8,16,2048]{2,1,0:T(8,128)(2,1)S(1)} %all_to_all.10.refs_0_, bf16[8,16,2048]{2,1,0:T(8,128)(2,1)S(1)} %collective-permute-done.refs_1_, bf16[8,16,2048]{2,1,0:T(8,128)(2,1)S(1)} %collective-permute-done.1.refs_2_, bf16[8,16,2048]{2,1,0:T(8,128)(2,1)S(1)} %collective-permute-done.2.refs_3_, ...), custom_call_target="tpu_custom_call" | custom-call | tf_op jit(solution)/shard_map/product/pallas_call | solution.py:344
  (25 shorter events, 1.4 us)
Async XLA Ops:
  66.2 20.2 %collective-permute-start.7 = (bf16[8,16,2048]{2,1,0:T(8,128)(2,1)S(1)}, bf16[8,16,2048]{2,1,0:T(8,128)(2,1)S(1)}, u32[]{:S(2)}, u32[]{:S(2)}) collective-permute-start(bf16[8,16,2048]{2,1,0:T(8,128)(2,1)S(1)} %all_to_all.10.refs_0_), channel_id=1, source_target_pairs={{0,8},{8,0},{16,24},{24,16},{32,40},{40,32},{48,56},{56,48},{64,72... | collective-permute-start | bytes 1572872 | tf_op jit(solution)/shard_map/ppermute | solution.py:382
  66.2 21.6 %collective-permute-start.3 = (bf16[8,16,2048]{2,1,0:T(8,128)(2,1)S(1)}, bf16[8,16,2048]{2,1,0:T(8,128)(2,1)S(1)}, u32[]{:S(2)}, u32[]{:S(2)}) collective-permute-start(bf16[8,16,2048]{2,1,0:T(8,128)(2,1)S(1)} %all_to_all.10.refs_0_), channel_id=1, source_target_pairs={{0,16},{8,24},{16,0},{24,8},{32,48},{40,56},{48,32},{56,40},{64,80... | collective-permute-start | bytes 1572872 | tf_op jit(solution)/shard_map/ppermute | solution.py:382
  67.2 18.6 %all-to-all-start.1 = ((bf16[16,16,1024]{2,1,0:T(8,128)(2,1)}), bf16[16,16,1024]{2,1,0:T(8,128)(2,1)S(1)}, u32[]{:S(2)}, u32[]{:S(2)}) async-start(bf16[16,16,1024]{2,1,0:T(8,128)(2,1)} %get-tuple-element.12), calls=%async_computation.1 | async-start | bytes 1048576 | tf_op jit(solution)/shard_map/all_to_all | solution.py:412
  72.3 20.0 %collective-permute-start.1 = (bf16[8,16,2048]{2,1,0:T(8,128)(2,1)S(1)}, bf16[8,16,2048]{2,1,0:T(8,128)(2,1)S(1)}, u32[]{:S(2)}, u32[]{:S(2)}) collective-permute-start(bf16[8,16,2048]{2,1,0:T(8,128)(2,1)S(1)} %all_to_all.10.refs_0_), channel_id=1, source_target_pairs={{0,96},{1,97},{2,98},{3,99},{4,100},{5,101},{6,102},{7,103},{8,40}... | collective-permute-start | bytes 1572872 | tf_op jit(solution)/shard_map/ppermute | solution.py:377
  75.4 18.1 %collective-permute-start = (bf16[8,16,2048]{2,1,0:T(8,128)(2,1)S(1)}, bf16[8,16,2048]{2,1,0:T(8,128)(2,1)S(1)}, u32[]{:S(2)}, u32[]{:S(2)}) collective-permute-start(bf16[8,16,2048]{2,1,0:T(8,128)(2,1)S(1)} %all_to_all.10.refs_0_), channel_id=1, source_target_pairs={{0,32},{1,33},{2,34},{3,35},{4,36},{5,37},{6,38},{7,39},{8,104},{9... | collective-permute-start | bytes 1572872 | tf_op jit(solution)/shard_map/ppermute | solution.py:377
  85.8 15.8 %collective-permute-start.18 = (bf16[16,16,1024]{2,1,0:T(8,128)(2,1)S(1)}, bf16[16,16,1024]{2,1,0:T(8,128)(2,1)S(1)}, u32[]{:S(2)}, u32[]{:S(2)}) collective-permute-start(bf16[16,16,1024]{2,1,0:T(8,128)(2,1)S(1)} %all-to-all-done.1.refs_16_), channel_id=1, source_target_pairs={{0,4},{1,5},{2,6},{3,7},{4,0},{5,1},{6,2},{7,3},{8,12},{9,13},{10,... | collective-permute-start | bytes 1572872 | tf_op jit(solution)/shard_map/ppermute | solution.py:382
  86.4 16.8 %collective-permute-start.16 = (bf16[16,16,1024]{2,1,0:T(8,128)(2,1)S(1)}, bf16[16,16,1024]{2,1,0:T(8,128)(2,1)S(1)}, u32[]{:S(2)}, u32[]{:S(2)}) collective-permute-start(bf16[16,16,1024]{2,1,0:T(8,128)(2,1)S(1)} %all-to-all-done.1.refs_16_), channel_id=1, source_target_pairs={{0,3},{1,0},{2,1},{3,2},{4,7},{5,4},{6,5},{7,6},{8,9},{9,10},{10,1... | collective-permute-start | bytes 1572872 | tf_op jit(solution)/shard_map/ppermute | solution.py:377
  87.8 16.2 %collective-permute-start.15 = (bf16[16,16,1024]{2,1,0:T(8,128)(2,1)S(1)}, bf16[16,16,1024]{2,1,0:T(8,128)(2,1)S(1)}, u32[]{:S(2)}, u32[]{:S(2)}) collective-permute-start(bf16[16,16,1024]{2,1,0:T(8,128)(2,1)S(1)} %all-to-all-done.1.refs_16_), channel_id=1, source_target_pairs={{0,1},{1,2},{2,3},{3,0},{4,5},{5,6},{6,7},{7,4},{8,11},{9,8},{10,9... | collective-permute-start | bytes 1572872 | tf_op jit(solution)/shard_map/ppermute | solution.py:377
  92.2 11.9 %collective-permute-start.11 = (bf16[8,16,2048]{2,1,0:T(8,128)(2,1)S(1)}, bf16[8,16,2048]{2,1,0:T(8,128)(2,1)S(1)}, u32[]{:S(2)}, u32[]{:S(2)}) collective-permute-start(bf16[8,16,2048]{2,1,0:T(8,128)(2,1)S(1)} %collective-permute-done.3.refs_4_), channel_id=1, source_target_pairs={{0,8},{8,0},{16,24},{24,16},{32,40},{40,32},{48,56},{56,48},{64,72... | collective-permute-start | bytes 1572872 | tf_op jit(solution)/shard_map/ppermute | solution.py:382
  93.5 11.8 %collective-permute-start.5 = (bf16[8,16,2048]{2,1,0:T(8,128)(2,1)S(1)}, bf16[8,16,2048]{2,1,0:T(8,128)(2,1)S(1)}, u32[]{:S(2)}, u32[]{:S(2)}) collective-permute-start(bf16[8,16,2048]{2,1,0:T(8,128)(2,1)S(1)} %collective-permute-done.3.refs_4_), channel_id=1, source_target_pairs={{0,96},{1,97},{2,98},{3,99},{4,100},{5,101},{6,102},{7,103},{8,40}... | collective-permute-start | bytes 1572872 | tf_op jit(solution)/shard_map/ppermute | solution.py:377
  101.6 10.4 %collective-permute-start.4 = (bf16[8,16,2048]{2,1,0:T(8,128)(2,1)S(1)}, bf16[8,16,2048]{2,1,0:T(8,128)(2,1)S(1)}, u32[]{:S(2)}, u32[]{:S(2)}) collective-permute-start(bf16[8,16,2048]{2,1,0:T(8,128)(2,1)S(1)} %collective-permute-done.3.refs_4_), channel_id=1, source_target_pairs={{0,32},{1,33},{2,34},{3,35},{4,36},{5,37},{6,38},{7,39},{8,104},{9... | collective-permute-start | bytes 1572872 | tf_op jit(solution)/shard_map/ppermute | solution.py:377
  103.2 9.7 %collective-permute-start.9 = (bf16[8,16,2048]{2,1,0:T(8,128)(2,1)S(1)}, bf16[8,16,2048]{2,1,0:T(8,128)(2,1)S(1)}, u32[]{:S(2)}, u32[]{:S(2)}) collective-permute-start(bf16[8,16,2048]{2,1,0:T(8,128)(2,1)S(1)} %collective-permute-done.1.refs_2_), channel_id=1, source_target_pairs={{0,8},{8,0},{16,24},{24,16},{32,40},{40,32},{48,56},{56,48},{64,72... | collective-permute-start | bytes 1572872 | tf_op jit(solution)/shard_map/ppermute | solution.py:382
  104.0 8.9 %collective-permute-start.8 = (bf16[8,16,2048]{2,1,0:T(8,128)(2,1)S(1)}, bf16[8,16,2048]{2,1,0:T(8,128)(2,1)S(1)}, u32[]{:S(2)}, u32[]{:S(2)}) collective-permute-start(bf16[8,16,2048]{2,1,0:T(8,128)(2,1)S(1)} %collective-permute-done.refs_1_), channel_id=1, source_target_pairs={{0,8},{8,0},{16,24},{24,16},{32,40},{40,32},{48,56},{56,48},{64,72... | collective-permute-start | bytes 1572872 | tf_op jit(solution)/shard_map/ppermute | solution.py:382
  104.1 13.5 %collective-permute-start.2 = (bf16[8,16,2048]{2,1,0:T(8,128)(2,1)S(1)}, bf16[8,16,2048]{2,1,0:T(8,128)(2,1)S(1)}, u32[]{:S(2)}, u32[]{:S(2)}) collective-permute-start(bf16[8,16,2048]{2,1,0:T(8,128)(2,1)S(1)} %collective-permute-done.refs_1_), channel_id=1, source_target_pairs={{0,32},{1,33},{2,34},{3,35},{4,36},{5,37},{6,38},{7,39},{8,104},{9... | collective-permute-start | bytes 1572872 | tf_op jit(solution)/shard_map/ppermute | solution.py:377
  105.3 12.3 %collective-permute-start.20 = (bf16[16,16,1024]{2,1,0:T(8,128)(2,1)S(1)}, bf16[16,16,1024]{2,1,0:T(8,128)(2,1)S(1)}, u32[]{:S(2)}, u32[]{:S(2)}) collective-permute-start(bf16[16,16,1024]{2,1,0:T(8,128)(2,1)S(1)} %collective-permute-done.18.refs_20_), channel_id=1, source_target_pairs={{0,3},{1,0},{2,1},{3,2},{4,7},{5,4},{6,5},{7,6},{8,9},{9,10},{10,1... | collective-permute-start | bytes 1572872 | tf_op jit(solution)/shard_map/ppermute | solution.py:377
  112.0 10.4 %collective-permute-start.19 = (bf16[16,16,1024]{2,1,0:T(8,128)(2,1)S(1)}, bf16[16,16,1024]{2,1,0:T(8,128)(2,1)S(1)}, u32[]{:S(2)}, u32[]{:S(2)}) collective-permute-start(bf16[16,16,1024]{2,1,0:T(8,128)(2,1)S(1)} %collective-permute-done.18.refs_20_), channel_id=1, source_target_pairs={{0,1},{1,2},{2,3},{3,0},{4,5},{5,6},{6,7},{7,4},{8,11},{9,8},{10,9... | collective-permute-start | bytes 1572872 | tf_op jit(solution)/shard_map/ppermute | solution.py:377
  112.9 15.1 %collective-permute-start.17 = (bf16[16,16,1024]{2,1,0:T(8,128)(2,1)S(1)}, bf16[16,16,1024]{2,1,0:T(8,128)(2,1)S(1)}, u32[]{:S(2)}, u32[]{:S(2)}) collective-permute-start(bf16[16,16,1024]{2,1,0:T(8,128)(2,1)S(1)} %collective-permute-done.15.refs_17_), channel_id=1, source_target_pairs={{0,1},{1,2},{2,3},{3,0},{4,5},{5,6},{6,7},{7,4},{8,11},{9,8},{10,9... | collective-permute-start | bytes 1572872 | tf_op jit(solution)/shard_map/ppermute | solution.py:377
  112.9 15.1 %collective-permute-start.6 = (bf16[8,16,2048]{2,1,0:T(8,128)(2,1)S(1)}, bf16[8,16,2048]{2,1,0:T(8,128)(2,1)S(1)}, u32[]{:S(2)}, u32[]{:S(2)}) collective-permute-start(bf16[8,16,2048]{2,1,0:T(8,128)(2,1)S(1)} %collective-permute-done.4.refs_5_), channel_id=1, source_target_pairs={{0,32},{1,33},{2,34},{3,35},{4,36},{5,37},{6,38},{7,39},{8,104},{9... | collective-permute-start | bytes 1572872 | tf_op jit(solution)/shard_map/ppermute | solution.py:377
  117.6 10.4 %collective-permute-start.12 = (bf16[8,16,2048]{2,1,0:T(8,128)(2,1)S(1)}, bf16[8,16,2048]{2,1,0:T(8,128)(2,1)S(1)}, u32[]{:S(2)}, u32[]{:S(2)}) collective-permute-start(bf16[8,16,2048]{2,1,0:T(8,128)(2,1)S(1)} %collective-permute-done.4.refs_5_), channel_id=1, source_target_pairs={{0,8},{8,0},{16,24},{24,16},{32,40},{40,32},{48,56},{56,48},{64,72... | collective-permute-start | bytes 1572872 | tf_op jit(solution)/shard_map/ppermute | solution.py:382
  117.6 10.4 %collective-permute-start.13 = (bf16[8,16,2048]{2,1,0:T(8,128)(2,1)S(1)}, bf16[8,16,2048]{2,1,0:T(8,128)(2,1)S(1)}, u32[]{:S(2)}, u32[]{:S(2)}) collective-permute-start(bf16[8,16,2048]{2,1,0:T(8,128)(2,1)S(1)} %collective-permute-done.5.refs_6_), channel_id=1, source_target_pairs={{0,8},{8,0},{16,24},{24,16},{32,40},{40,32},{48,56},{56,48},{64,72... | collective-permute-start | bytes 1572872 | tf_op jit(solution)/shard_map/ppermute | solution.py:382
  122.4 5.7 %collective-permute-start.10 = (bf16[8,16,2048]{2,1,0:T(8,128)(2,1)S(1)}, bf16[8,16,2048]{2,1,0:T(8,128)(2,1)S(1)}, u32[]{:S(2)}, u32[]{:S(2)}) collective-permute-start(bf16[8,16,2048]{2,1,0:T(8,128)(2,1)S(1)} %collective-permute-done.2.refs_3_), channel_id=1, source_target_pairs={{0,8},{8,0},{16,24},{24,16},{32,40},{40,32},{48,56},{56,48},{64,72... | collective-permute-start | bytes 1572872 | tf_op jit(solution)/shard_map/ppermute | solution.py:382
  128.0 10.4 %collective-permute-start.21 = (bf16[16,16,1024]{2,1,0:T(8,128)(2,1)S(1)}, bf16[16,16,1024]{2,1,0:T(8,128)(2,1)S(1)}, u32[]{:S(2)}, u32[]{:S(2)}) collective-permute-start(bf16[16,16,1024]{2,1,0:T(8,128)(2,1)S(1)} %collective-permute-done.19.refs_21_), channel_id=1, source_target_pairs={{0,1},{1,2},{2,3},{3,0},{4,5},{5,6},{6,7},{7,4},{8,11},{9,8},{10,9... | collective-permute-start | bytes 1572872 | tf_op jit(solution)/shard_map/ppermute | solution.py:377
  128.0 10.4 %collective-permute-start.14 = (bf16[8,16,2048]{2,1,0:T(8,128)(2,1)S(1)}, bf16[8,16,2048]{2,1,0:T(8,128)(2,1)S(1)}, u32[]{:S(2)}, u32[]{:S(2)}) collective-permute-start(bf16[8,16,2048]{2,1,0:T(8,128)(2,1)S(1)} %collective-permute-done.6.refs_7_), channel_id=1, source_target_pairs={{0,8},{8,0},{16,24},{24,16},{32,40},{40,32},{48,56},{56,48},{64,72... | collective-permute-start | bytes 1572872 | tf_op jit(solution)/shard_map/ppermute | solution.py:382

commit v5 on v4

--- a/solution.py
+++ b/solution.py
@@ -34,7 +34,8 @@
 def z_table():
     z = np.arange(EDGE)
     angle = 2.0 * np.pi * ((z[:, None] * z[None, :]) % EDGE) / EDGE
-    table = np.concatenate([np.cos(angle), np.sin(angle)], axis=1) * EDGE ** (-1.5)
+    cosine, sine = np.cos(angle), np.sin(angle)
+    table = np.block([[cosine, sine], [-sine, cosine]]) * EDGE ** (-1.5)
     high, low = two_terms(table)
     return np.block([[high, high], [low, np.zeros_like(low)]]).astype(BF)
 
@@ -188,6 +189,8 @@
 
     first = lax.broadcasted_iota(jnp.int32, (8, LANES), 1) < EDGE
 
+    lower_lanes = lax.broadcasted_iota(jnp.int32, (EDGE, LANES), 1) < EDGE
+
     def yz_stage(a, carry):
         complex_plane = jnp.where((a & (HALF - 1)) == 0, 0.0, 1.0)
         at_re = pl.ds(pl.multiple_of(a * 8, 8), 8)
@@ -204,9 +207,8 @@
                 r, i = r * c - i * s, r * s + i * c
             even = jnp.where(first, r, pltpu.roll(i, EDGE, 1))
             odd = jnp.where(first, pltpu.roll(r, EDGE, 1), i)
-            for part, line in ((lower, even + odd), (upper, even - odd)):
-                turned = pltpu.roll(line, EDGE, 1)
-                part += [line, jnp.where(first, turned, -turned)]
+            lower.append(even + odd)
+            upper.append(even - odd)
         high, low = split(jnp.concatenate(lower + upper, axis=0))
         out = lax.dot_general(
             z_factors[...],
@@ -214,10 +216,12 @@
             (((1,), (1,)), ((), ())),
             preferred_element_type=F32,
         )
-        out = out[:EDGE] + out[EDGE:]
-        for n in range(8):
-            at = pl.multiple_of((a * 8 + n) * EDGE, EDGE)
-            table[pl.ds(at, EDGE), :] = out[:, n * LANES : (n + 1) * LANES]
+        out = out[: 2 * EDGE] + out[2 * EDGE :]
+        for n in range(4):
+            re, im = out[:EDGE, n * LANES : (n + 1) * LANES], out[EDGE:, n * LANES : (n + 1) * LANES]
+            at = pl.multiple_of((a * 8 + 2 * n) * EDGE, EDGE)
+            table[pl.ds(at, EDGE), :] = jnp.where(lower_lanes, re, pltpu.roll(im, EDGE, 1))
+            table[pl.ds(at + EDGE, EDGE), :] = jnp.where(lower_lanes, pltpu.roll(re, EDGE, 1), im)
         return carry
 
     lax.fori_loop(0, HALF + 1, yz_stage, 0)
@@ -225,9 +229,14 @@
     to_scalar.wait()
     per_row, per_col = left.shape[2] // LANES, right.shape[2] // LANES
 
+    sublane_bits = [(sublane & (1 << i)) != 0 for i in range(3)]
+
     def pick(q, picked):
-        for j in range(LANES):
-            picked[pl.ds(j, 1), :] = table[pl.ds(rows[q, j], 1), :]
+        for j in range(0, LANES, 8):
+            some = [table[pl.ds(rows[q, j + t], 8, stride=0), :] for t in range(8)]
+            for bit in sublane_bits:
+                some = [jnp.where(bit, some[n + 1], some[n]) for n in range(0, len(some), 2)]
+            picked[pl.ds(j, 8), :] = some[0]
 
     def finish(q, picked):
         turned = picked[...].T
@@ -235,7 +244,7 @@
         bits = [(b & (1 << i)) != 0 for i in range(3)]
         parts = []
         for k in range(2):
-            some = [turned[n * 16 + k * 8 : n * 16 + k * 8 + 8] for n in range(8)]
+            some = [turned[k * EDGE + n * 8 : k * EDGE + n * 8 + 8] for n in range(8)]
             for bit in bits:
                 some = [jnp.where(bit, some[n + 1], some[n]) for n in range(0, len(some), 2)]
             parts.append(some[0])
@@ -308,18 +317,14 @@
 
 def product_kernel(n_left, n_right, *refs):
     left_in, right_in = refs[:n_left], refs[n_left : n_left + n_right]
-    out, left, right, left_sem, right_sem = refs[n_left + n_right :]
+    out, right, right_sem = refs[n_left + n_right :]
 
     @pl.when(pl.program_id(0) == 0)
     def _():
-        col = lax.axis_index("col")
-        left_slots, right_slots = left_places(col), right_places(lax.axis_index("row"), col & 1)
+        right_slots = right_places(lax.axis_index("row"), lax.axis_index("col") & 1)
         copies = [
             pltpu.make_async_copy(piece, right.at[:, right_slots[j]], right_sem.at[j])
             for j, piece in enumerate(right_in)
-        ] + [
-            pltpu.make_async_copy(piece, left.at[left_slots[i]], left_sem.at[i])
-            for i, piece in enumerate(left_in)
         ]
         for copy in copies:
             copy.start()
@@ -328,10 +333,11 @@
 
     rows = out.shape[0]
     at = pl.multiple_of(pl.program_id(0) * rows, rows)
-    depth = left.shape[0] * left.shape[1] * left.shape[2]
+    left_slots = left_places(lax.axis_index("col"))
+    depth = right.shape[1] * right.shape[2]
     out[...] = lax.dot_general(
-        left[:, :, :, pl.ds(at, rows)].reshape(depth, rows),
-        right[...].reshape(depth, right.shape[3]),
+        jnp.concatenate([piece[:, :, pl.ds(at, rows)].reshape(depth, rows) for piece in left_in], axis=0),
+        jnp.concatenate([right[slot].reshape(depth, right.shape[3]) for slot in left_slots], axis=0),
         (((0,), (0,)), ((), ())),
         preferred_element_type=F32,
     )
@@ -344,13 +350,11 @@
     return pl.pallas_call(
         lambda *refs: product_kernel(n_left, n_right, *refs),
         grid=(rows // block,),
-        in_specs=[pl.BlockSpec(memory_space=pl.ANY)] * (n_left + n_right),
+        in_specs=[pl.BlockSpec(memory_space=pltpu.VMEM)] * n_left + [pl.BlockSpec(memory_space=pl.ANY)] * n_right,
         out_specs=pl.BlockSpec((block, cols), lambda m: (m, 0)),
         out_shape=jax.ShapeDtypeStruct((rows, cols), F32),
         scratch_shapes=[
-            pltpu.VMEM((n_left,) + left[0].shape, BF),
             pltpu.VMEM((right[0].shape[0], n_right) + right[0].shape[1:], BF),
-            pltpu.SemaphoreType.DMA((n_left,)),
             pltpu.SemaphoreType.DMA((n_right,)),
         ],
         compiler_params=pltpu.CompilerParams(vmem_limit_bytes=24 * 1024 * 1024),
@@ -405,16 +409,16 @@
     left, right = densities(
         n_row, n_col, valence, conduction, valence_energy, conduction_energy, pair_list, sphere_index
     )
+    right = lax.all_to_all(right, "col", split_axis=0, concat_axis=0, tiled=True)
+    right, left = lax.optimization_barrier((right, left))
+    right_z = swap(right, "row", RING)
+    rights = [right, shift(right, "row", 1, 1), shift(right, "row", 1, -1)]
     left = lax.all_to_all(left, "row", split_axis=0, concat_axis=0, tiled=True)
-    left, right = lax.optimization_barrier((left, right))
     left_z = swap(left, "col", 2)
     lefts = [left, shift(left, "col", RING, 1), shift(left, "col", RING, -1)]
-    right = lax.all_to_all(right, "col", split_axis=0, concat_axis=0, tiled=True)
-    right_z = swap(right, "row", RING)
-    rights = [right, shift(right, "row", 1, 1), shift(right, "row", 1, -1)]
-    lefts += [shift(lefts[1], "col", RING, 1), left_z, shift(left_z, "col", RING, 1), shift(left_z, "col", RING, -1)]
     rights += [shift(rights[1], "row", 1, 1), right_z, shift(right_z, "row", 1, 1), shift(right_z, "row", 1, -1)]
-    lefts += [shift(lefts[5], "col", RING, 1)]
+    lefts += [shift(lefts[1], "col", RING, 1)]
+    lefts += [left_z, shift(left_z, "col", RING, 1), shift(left_z, "col", RING, -1), swap(lefts[3], "col", 2)]
     rights += [shift(rights[5], "row", 1, 1)]
     lefts += [swap(piece, "col", 1) for piece in lefts]
     return product(lefts, rights)

time: 151 us -> 143 us (0.947)
  waiting for transfers between devices: 52 us -> 44.6 us
  starting transfers between devices: 20.1 us -> 25 us
  Pallas kernels: 59.6 us -> 55.5 us
  blocking collectives: 19.3 us -> 16.9 us
    ppermute x12 -> x11, waiting for transfers between devices: 34.3 us -> 17.3 us  [shift(): return lax.ppermute(value, ('col', 'row'), pairs)]
    ppermute x10 -> x11, waiting for transfers between devices: 7.33 us -> 15.2 us  [swap(): return lax.ppermute(value, axis, [(i, i ^ bit) for i in range(count)])]
    ppermute x10 -> x11, starting transfers between devices: 3.88 us -> 8.34 us  [swap(): return lax.ppermute(value, axis, [(i, i ^ bit) for i in range(count)])]
    pallas_call x1, Pallas kernels: 46.9 us -> 43.7 us  [densities(): pl.pallas_call(lambda *refs: density_kernel(n_pairs * n_row * n_col, *ref...]
    all_to_all x1, blocking collectives: 19.3 us -> 16.9 us  [per_device(): lax.all_to_all(right, 'col', split_axis=0, concat_axis=0, tiled=True)]
    ppermute x12 -> x11, starting transfers between devices: 11.2 us -> 13.2 us  [shift(): return lax.ppermute(value, ('col', 'row'), pairs)]
    all_to_all x1, waiting for transfers between devices: 10.4 us -> 12.1 us  [per_device(): left = lax.all_to_all(left, 'row', split_axis=0, concat_axis=0, tiled=True)]
    all_to_all x1, starting transfers between devices: 5.02 us -> 3.49 us  [per_device(): left = lax.all_to_all(left, 'row', split_axis=0, concat_axis=0, tiled=True)]
  transfers between devices with their start and end apart: 23 -> 23, of which waited for: 9 -> 10; matrix products, arithmetic and copies ran while one was open for 0% -> 0% of each run, Pallas kernels for 0% -> 0%
where the time goes in v5:
time: 143 us; the launch traced here: 142 us
  Pallas kernels  55.5 us (39%)
  waiting for transfers between devices  44.6 us (31%)
  starting transfers between devices  25 us (17%)
  blocking collectives  16.9 us (12%)
    pallas_call x1, Pallas kernels, densities(): pl.pallas_call(lambda *refs: density_kernel(n_pairs * n_row * n_col, *ref...  43.7 us
    ppermute x11, waiting for transfers between devices, shift(): return lax.ppermute(value, ('col', 'row'), pairs)  17.3 us
    all_to_all x1, blocking collectives, per_device(): lax.all_to_all(right, 'col', split_axis=0, concat_axis=0, tiled=True)  16.9 us
    ppermute x11, waiting for transfers between devices, swap(): return lax.ppermute(value, axis, [(i, i ^ bit) for i in range(count)])  15.2 us
    ppermute x11, starting transfers between devices, shift(): return lax.ppermute(value, ('col', 'row'), pairs)  13.2 us
    all_to_all x1, waiting for transfers between devices, per_device(): left = lax.all_to_all(left, 'row', split_axis=0, concat_axis=0, tiled=True)  12.1 us
    pallas_call x1, Pallas kernels, product(): pl.pallas_call(lambda *refs: product_kernel(n_left, n_right, *refs), grid...  11.8 us
    ppermute x11, starting transfers between devices, swap(): return lax.ppermute(value, axis, [(i, i ^ bit) for i in range(count)])  8.34 us
  transfers between devices with their start and end apart: 23, of which 10 were waited for; matrix products, arithmetic and copies ran while one was open for 0% of the time, Pallas kernels for 0%

profile of v5, /device:TPU:0, one launch (start us, length us, event | category | flops | bytes accessed | tf_op | source)
XLA Modules:
  0.0 142.0 jit_solution(5446576276167467337)
XLA Ops:
  0.0 43.7 %density.1 = (bf16[8,16,2048]{2,1,0:T(8,128)(2,1)}, bf16[16,16,1024]{2,1,0:T(8,128)(2,1)}) custom-call(f32[4,64,4096]{2,1,0:T(8,128)} %refs_0_.1, f32[4,64,4096]{2,1,0:T(8,128)} %refs_1_.1, f32[4]{0:T(128)} %refs_2_.1, f32[4]{0:T(128)} %refs_3_.1, s32[2,8]{1,0:T(2,128)} %bitcast.3, s32[128,128]{1,0:T(8,128)} %bitcast.2, ...), custom_call_target="tpu_custom_call" | custom-call | tf_op jit(solution)/shard_map/density/pallas_call | solution.py:278
  43.7 16.9 %all_to_all.10.refs_16_ = bf16[16,16,1024]{2,1,0:T(8,128)(2,1)S(1)} all-to-all(bf16[16,16,1024]{2,1,0:T(8,128)(2,1)} %get-tuple-element.9), channel_id=1, replica_groups=mesh['col'=16,'row'=8] {'col'}, dimensions={0} | all-to-all | bytes 1048576 | tf_op jit(solution)/shard_map/all_to_all | solution.py:412
  60.6 3.6 %collective-permute-start.18 = (bf16[16,16,1024]{2,1,0:T(8,128)(2,1)S(1)}, bf16[16,16,1024]{2,1,0:T(8,128)(2,1)S(1)}, u32[]{:S(2)}, u32[]{:S(2)}) collective-permute-start(bf16[16,16,1024]{2,1,0:T(8,128)(2,1)S(1)} %all_to_all.10.refs_16_), channel_id=1, source_target_pairs={{0,4},{1,5},{2,6},{3,7},{4,0},{5,1},{6,2},{7,3},{8,12},{9,13},{10,... | collective-permute-start | bytes 1572872 | tf_op jit(solution)/shard_map/ppermute | solution.py:386
  64.2 2.8 %collective-permute-start.16 = (bf16[16,16,1024]{2,1,0:T(8,128)(2,1)S(1)}, bf16[16,16,1024]{2,1,0:T(8,128)(2,1)S(1)}, u32[]{:S(2)}, u32[]{:S(2)}) collective-permute-start(bf16[16,16,1024]{2,1,0:T(8,128)(2,1)S(1)} %all_to_all.10.refs_16_), channel_id=1, source_target_pairs={{0,3},{1,0},{2,1},{3,2},{4,7},{5,4},{6,5},{7,6},{8,9},{9,10},{10,1... | collective-permute-start | bytes 1572872 | tf_op jit(solution)/shard_map/ppermute | solution.py:381
  66.9 3.5 %all-to-all-start.1 = ((bf16[8,16,2048]{2,1,0:T(8,128)(2,1)}), bf16[8,16,2048]{2,1,0:T(8,128)(2,1)S(1)}, u32[]{:S(2)}, u32[]{:S(2)}) async-start(bf16[8,16,2048]{2,1,0:T(8,128)(2,1)} %get-tuple-element.11), calls=%async_computation.1 | async-start | bytes 1048576 | tf_op jit(solution)/shard_map/all_to_all | solution.py:416
  70.4 1.9 %collective-permute-start.15 = (bf16[16,16,1024]{2,1,0:T(8,128)(2,1)S(1)}, bf16[16,16,1024]{2,1,0:T(8,128)(2,1)S(1)}, u32[]{:S(2)}, u32[]{:S(2)}) collective-permute-start(bf16[16,16,1024]{2,1,0:T(8,128)(2,1)S(1)} %all_to_all.10.refs_16_), channel_id=1, source_target_pairs={{0,1},{1,2},{2,3},{3,0},{4,5},{5,6},{6,7},{7,4},{8,11},{9,8},{10,9... | collective-permute-start | bytes 1572872 | tf_op jit(solution)/shard_map/ppermute | solution.py:381
  72.4 12.1 %all-to-all-done.1.refs_0_ = bf16[8,16,2048]{2,1,0:T(8,128)(2,1)S(1)} async-done(((bf16[8,16,2048]{2,1,0:T(8,128)(2,1)}), bf16[8,16,2048]{2,1,0:T(8,128)(2,1)S(1)}, u32[]{:S(2)}, u32[]{:S(2)}) %all-to-all-start.1) | async-done | bytes 524320 | tf_op jit(solution)/shard_map/all_to_all | solution.py:416
  84.5 0.7 collective-permute-start.1
  85.2 1.4 collective-permute-start
  86.6 3.6 %collective-permute-start.20 = (bf16[16,16,1024]{2,1,0:T(8,128)(2,1)S(1)}, bf16[16,16,1024]{2,1,0:T(8,128)(2,1)S(1)}, u32[]{:S(2)}, u32[]{:S(2)}) collective-permute-start(bf16[16,16,1024]{2,1,0:T(8,128)(2,1)S(1)} %collective-permute-done.18.refs_20_), channel_id=1, source_target_pairs={{0,3},{1,0},{2,1},{3,2},{4,7},{5,4},{6,5},{7,6},{8,9},{9,10},{10,1... | collective-permute-start | bytes 1572872 | tf_op jit(solution)/shard_map/ppermute | solution.py:381
  90.2 8.6 %collective-permute-done.3.refs_4_ = bf16[8,16,2048]{2,1,0:T(8,128)(2,1)S(1)} collective-permute-done((bf16[8,16,2048]{2,1,0:T(8,128)(2,1)S(1)}, bf16[8,16,2048]{2,1,0:T(8,128)(2,1)S(1)}, u32[]{:S(2)}, u32[]{:S(2)}) %collective-permute-start.3) | collective-permute-done | bytes 524320 | tf_op jit(solution)/shard_map/ppermute | solution.py:386
  98.9 2.9 %collective-permute-start.11 = (bf16[8,16,2048]{2,1,0:T(8,128)(2,1)S(1)}, bf16[8,16,2048]{2,1,0:T(8,128)(2,1)S(1)}, u32[]{:S(2)}, u32[]{:S(2)}) collective-permute-start(bf16[8,16,2048]{2,1,0:T(8,128)(2,1)S(1)} %collective-permute-done.3.refs_4_), channel_id=1, source_target_pairs={{0,8},{8,0},{16,24},{24,16},{32,40},{40,32},{48,56},{56,48},{64,72... | collective-permute-start | bytes 1572872 | tf_op jit(solution)/shard_map/ppermute | solution.py:386
  101.8 0.4 collective-permute-done.20.refs_22_
  102.3 2.8 %collective-permute-start.5 = (bf16[8,16,2048]{2,1,0:T(8,128)(2,1)S(1)}, bf16[8,16,2048]{2,1,0:T(8,128)(2,1)S(1)}, u32[]{:S(2)}, u32[]{:S(2)}) collective-permute-start(bf16[8,16,2048]{2,1,0:T(8,128)(2,1)S(1)} %collective-permute-done.3.refs_4_), channel_id=1, source_target_pairs={{0,96},{1,97},{2,98},{3,99},{4,100},{5,101},{6,102},{7,103},{8,40}... | collective-permute-start | bytes 1572872 | tf_op jit(solution)/shard_map/ppermute | solution.py:381
  105.1 4.5 %collective-permute-done.17.refs_19_ = bf16[16,16,1024]{2,1,0:T(8,128)(2,1)S(1)} collective-permute-done((bf16[16,16,1024]{2,1,0:T(8,128)(2,1)S(1)}, bf16[16,16,1024]{2,1,0:T(8,128)(2,1)S(1)}, u32[]{:S(2)}, u32[]{:S(2)}) %collective-permute-start.17) | collective-permute-done | bytes 524320 | tf_op jit(solution)/shard_map/ppermute | solution.py:381
  109.6 0.5 collective-permute-start.8
  110.1 7.3 %collective-permute-done.2.refs_3_ = bf16[8,16,2048]{2,1,0:T(8,128)(2,1)S(1)} collective-permute-done((bf16[8,16,2048]{2,1,0:T(8,128)(2,1)S(1)}, bf16[8,16,2048]{2,1,0:T(8,128)(2,1)S(1)}, u32[]{:S(2)}, u32[]{:S(2)}) %collective-permute-start.2) | collective-permute-done | bytes 524320 | tf_op jit(solution)/shard_map/ppermute | solution.py:381
  117.3 0.7 collective-permute-start.6
  118.0 4.9 %collective-permute-done.4.refs_5_ = bf16[8,16,2048]{2,1,0:T(8,128)(2,1)S(1)} collective-permute-done((bf16[8,16,2048]{2,1,0:T(8,128)(2,1)S(1)}, bf16[8,16,2048]{2,1,0:T(8,128)(2,1)S(1)}, u32[]{:S(2)}, u32[]{:S(2)}) %collective-permute-start.4) | collective-permute-done | bytes 524320 | tf_op jit(solution)/shard_map/ppermute | solution.py:381
  122.9 0.5 collective-permute-start.13
  123.5 4.8 %collective-permute-done.6.refs_7_ = bf16[8,16,2048]{2,1,0:T(8,128)(2,1)S(1)} collective-permute-done((bf16[8,16,2048]{2,1,0:T(8,128)(2,1)S(1)}, bf16[8,16,2048]{2,1,0:T(8,128)(2,1)S(1)}, u32[]{:S(2)}, u32[]{:S(2)}) %collective-permute-start.6) | collective-permute-done | bytes 524320 | tf_op jit(solution)/shard_map/ppermute | solution.py:386
  128.3 0.1 collective-permute-done.21.refs_23_
  128.4 1.8 %collective-permute-done.14.refs_15_ = bf16[8,16,2048]{2,1,0:T(8,128)(2,1)S(1)} collective-permute-done((bf16[8,16,2048]{2,1,0:T(8,128)(2,1)S(1)}, bf16[8,16,2048]{2,1,0:T(8,128)(2,1)S(1)}, u32[]{:S(2)}, u32[]{:S(2)}) %collective-permute-start.14) | collective-permute-done | bytes 524320 | tf_op jit(solution)/shard_map/ppermute | solution.py:386
  130.2 11.8 %product.1 = f32[2048,1024]{1,0:T(8,128)} custom-call(bf16[8,16,2048]{2,1,0:T(8,128)(2,1)S(1)} %all-to-all-done.1.refs_0_, bf16[8,16,2048]{2,1,0:T(8,128)(2,1)S(1)} %collective-permute-done.refs_1_, bf16[8,16,2048]{2,1,0:T(8,128)(2,1)S(1)} %collective-permute-done.1.refs_2_, bf16[8,16,2048]{2,1,0:T(8,128)(2,1)S(1)} %collective-permute-done.2.refs_3_, ...), custom_call_target="tpu_custom_call" | custom-call | tf_op jit(solution)/shard_map/product/pallas_call | solution.py:350
  (25 shorter events, 0.2 us)
Async XLA Ops:
  60.6 23.9 %collective-permute-start.18 = (bf16[16,16,1024]{2,1,0:T(8,128)(2,1)S(1)}, bf16[16,16,1024]{2,1,0:T(8,128)(2,1)S(1)}, u32[]{:S(2)}, u32[]{:S(2)}) collective-permute-start(bf16[16,16,1024]{2,1,0:T(8,128)(2,1)S(1)} %all_to_all.10.refs_16_), channel_id=1, source_target_pairs={{0,4},{1,5},{2,6},{3,7},{4,0},{5,1},{6,2},{7,3},{8,12},{9,13},{10,... | collective-permute-start | bytes 1572872 | tf_op jit(solution)/shard_map/ppermute | solution.py:386
  64.2 21.0 %collective-permute-start.16 = (bf16[16,16,1024]{2,1,0:T(8,128)(2,1)S(1)}, bf16[16,16,1024]{2,1,0:T(8,128)(2,1)S(1)}, u32[]{:S(2)}, u32[]{:S(2)}) collective-permute-start(bf16[16,16,1024]{2,1,0:T(8,128)(2,1)S(1)} %all_to_all.10.refs_16_), channel_id=1, source_target_pairs={{0,3},{1,0},{2,1},{3,2},{4,7},{5,4},{6,5},{7,6},{8,9},{9,10},{10,1... | collective-permute-start | bytes 1572872 | tf_op jit(solution)/shard_map/ppermute | solution.py:381
  66.9 17.5 %all-to-all-start.1 = ((bf16[8,16,2048]{2,1,0:T(8,128)(2,1)}), bf16[8,16,2048]{2,1,0:T(8,128)(2,1)S(1)}, u32[]{:S(2)}, u32[]{:S(2)}) async-start(bf16[8,16,2048]{2,1,0:T(8,128)(2,1)} %get-tuple-element.11), calls=%async_computation.1 | async-start | bytes 1048576 | tf_op jit(solution)/shard_map/all_to_all | solution.py:416
  70.4 16.1 %collective-permute-start.15 = (bf16[16,16,1024]{2,1,0:T(8,128)(2,1)S(1)}, bf16[16,16,1024]{2,1,0:T(8,128)(2,1)S(1)}, u32[]{:S(2)}, u32[]{:S(2)}) collective-permute-start(bf16[16,16,1024]{2,1,0:T(8,128)(2,1)S(1)} %all_to_all.10.refs_16_), channel_id=1, source_target_pairs={{0,1},{1,2},{2,3},{3,0},{4,5},{5,6},{6,7},{7,4},{8,11},{9,8},{10,9... | collective-permute-start | bytes 1572872 | tf_op jit(solution)/shard_map/ppermute | solution.py:381
  84.5 5.7 %collective-permute-start.7 = (bf16[8,16,2048]{2,1,0:T(8,128)(2,1)S(1)}, bf16[8,16,2048]{2,1,0:T(8,128)(2,1)S(1)}, u32[]{:S(2)}, u32[]{:S(2)}) collective-permute-start(bf16[8,16,2048]{2,1,0:T(8,128)(2,1)S(1)} %all-to-all-done.1.refs_0_), channel_id=1, source_target_pairs={{0,8},{8,0},{16,24},{24,16},{32,40},{40,32},{48,56},{56,48},{64,72... | collective-permute-start | bytes 1572872 | tf_op jit(solution)/shard_map/ppermute | solution.py:386
  84.5 14.3 %collective-permute-start.3 = (bf16[8,16,2048]{2,1,0:T(8,128)(2,1)S(1)}, bf16[8,16,2048]{2,1,0:T(8,128)(2,1)S(1)}, u32[]{:S(2)}, u32[]{:S(2)}) collective-permute-start(bf16[8,16,2048]{2,1,0:T(8,128)(2,1)S(1)} %all-to-all-done.1.refs_0_), channel_id=1, source_target_pairs={{0,16},{8,24},{16,0},{24,8},{32,48},{40,56},{48,32},{56,40},{64,80... | collective-permute-start | bytes 1572872 | tf_op jit(solution)/shard_map/ppermute | solution.py:386
  84.5 14.4 %collective-permute-start.1 = (bf16[8,16,2048]{2,1,0:T(8,128)(2,1)S(1)}, bf16[8,16,2048]{2,1,0:T(8,128)(2,1)S(1)}, u32[]{:S(2)}, u32[]{:S(2)}) collective-permute-start(bf16[8,16,2048]{2,1,0:T(8,128)(2,1)S(1)} %all-to-all-done.1.refs_0_), channel_id=1, source_target_pairs={{0,96},{1,97},{2,98},{3,99},{4,100},{5,101},{6,102},{7,103},{8,40}... | collective-permute-start | bytes 1572872 | tf_op jit(solution)/shard_map/ppermute | solution.py:381
  85.2 16.7 %collective-permute-start = (bf16[8,16,2048]{2,1,0:T(8,128)(2,1)S(1)}, bf16[8,16,2048]{2,1,0:T(8,128)(2,1)S(1)}, u32[]{:S(2)}, u32[]{:S(2)}) collective-permute-start(bf16[8,16,2048]{2,1,0:T(8,128)(2,1)S(1)} %all-to-all-done.1.refs_0_), channel_id=1, source_target_pairs={{0,32},{1,33},{2,34},{3,35},{4,36},{5,37},{6,38},{7,39},{8,104},{9... | collective-permute-start | bytes 1572872 | tf_op jit(solution)/shard_map/ppermute | solution.py:381
  86.6 15.7 %collective-permute-start.20 = (bf16[16,16,1024]{2,1,0:T(8,128)(2,1)S(1)}, bf16[16,16,1024]{2,1,0:T(8,128)(2,1)S(1)}, u32[]{:S(2)}, u32[]{:S(2)}) collective-permute-start(bf16[16,16,1024]{2,1,0:T(8,128)(2,1)S(1)} %collective-permute-done.18.refs_20_), channel_id=1, source_target_pairs={{0,3},{1,0},{2,1},{3,2},{4,7},{5,4},{6,5},{7,6},{8,9},{9,10},{10,1... | collective-permute-start | bytes 1572872 | tf_op jit(solution)/shard_map/ppermute | solution.py:381
  90.2 14.9 %collective-permute-start.19 = (bf16[16,16,1024]{2,1,0:T(8,128)(2,1)S(1)}, bf16[16,16,1024]{2,1,0:T(8,128)(2,1)S(1)}, u32[]{:S(2)}, u32[]{:S(2)}) collective-permute-start(bf16[16,16,1024]{2,1,0:T(8,128)(2,1)S(1)} %collective-permute-done.18.refs_20_), channel_id=1, source_target_pairs={{0,1},{1,2},{2,3},{3,0},{4,5},{5,6},{6,7},{7,4},{8,11},{9,8},{10,9... | collective-permute-start | bytes 1572872 | tf_op jit(solution)/shard_map/ppermute | solution.py:381
  98.8 10.7 %collective-permute-start.17 = (bf16[16,16,1024]{2,1,0:T(8,128)(2,1)S(1)}, bf16[16,16,1024]{2,1,0:T(8,128)(2,1)S(1)}, u32[]{:S(2)}, u32[]{:S(2)}) collective-permute-start(bf16[16,16,1024]{2,1,0:T(8,128)(2,1)S(1)} %collective-permute-done.15.refs_17_), channel_id=1, source_target_pairs={{0,1},{1,2},{2,3},{3,0},{4,5},{5,6},{6,7},{7,4},{8,11},{9,8},{10,9... | collective-permute-start | bytes 1572872 | tf_op jit(solution)/shard_map/ppermute | solution.py:381
  98.9 10.7 %collective-permute-start.11 = (bf16[8,16,2048]{2,1,0:T(8,128)(2,1)S(1)}, bf16[8,16,2048]{2,1,0:T(8,128)(2,1)S(1)}, u32[]{:S(2)}, u32[]{:S(2)}) collective-permute-start(bf16[8,16,2048]{2,1,0:T(8,128)(2,1)S(1)} %collective-permute-done.3.refs_4_), channel_id=1, source_target_pairs={{0,8},{8,0},{16,24},{24,16},{32,40},{40,32},{48,56},{56,48},{64,72... | collective-permute-start | bytes 1572872 | tf_op jit(solution)/shard_map/ppermute | solution.py:386
  101.8 15.5 %collective-permute-start.2 = (bf16[8,16,2048]{2,1,0:T(8,128)(2,1)S(1)}, bf16[8,16,2048]{2,1,0:T(8,128)(2,1)S(1)}, u32[]{:S(2)}, u32[]{:S(2)}) collective-permute-start(bf16[8,16,2048]{2,1,0:T(8,128)(2,1)S(1)} %collective-permute-done.refs_1_), channel_id=1, source_target_pairs={{0,32},{1,33},{2,34},{3,35},{4,36},{5,37},{6,38},{7,39},{8,104},{9... | collective-permute-start | bytes 1572872 | tf_op jit(solution)/shard_map/ppermute | solution.py:381
  102.3 15.7 %collective-permute-start.5 = (bf16[8,16,2048]{2,1,0:T(8,128)(2,1)S(1)}, bf16[8,16,2048]{2,1,0:T(8,128)(2,1)S(1)}, u32[]{:S(2)}, u32[]{:S(2)}) collective-permute-start(bf16[8,16,2048]{2,1,0:T(8,128)(2,1)S(1)} %collective-permute-done.3.refs_4_), channel_id=1, source_target_pairs={{0,96},{1,97},{2,98},{3,99},{4,100},{5,101},{6,102},{7,103},{8,40}... | collective-permute-start | bytes 1572872 | tf_op jit(solution)/shard_map/ppermute | solution.py:381
  105.1 17.9 %collective-permute-start.4 = (bf16[8,16,2048]{2,1,0:T(8,128)(2,1)S(1)}, bf16[8,16,2048]{2,1,0:T(8,128)(2,1)S(1)}, u32[]{:S(2)}, u32[]{:S(2)}) collective-permute-start(bf16[8,16,2048]{2,1,0:T(8,128)(2,1)S(1)} %collective-permute-done.3.refs_4_), channel_id=1, source_target_pairs={{0,32},{1,33},{2,34},{3,35},{4,36},{5,37},{6,38},{7,39},{8,104},{9... | collective-permute-start | bytes 1572872 | tf_op jit(solution)/shard_map/ppermute | solution.py:381
  109.5 13.4 %collective-permute-start.9 = (bf16[8,16,2048]{2,1,0:T(8,128)(2,1)S(1)}, bf16[8,16,2048]{2,1,0:T(8,128)(2,1)S(1)}, u32[]{:S(2)}, u32[]{:S(2)}) collective-permute-start(bf16[8,16,2048]{2,1,0:T(8,128)(2,1)S(1)} %collective-permute-done.1.refs_2_), channel_id=1, source_target_pairs={{0,8},{8,0},{16,24},{24,16},{32,40},{40,32},{48,56},{56,48},{64,72... | collective-permute-start | bytes 1572872 | tf_op jit(solution)/shard_map/ppermute | solution.py:386
  109.6 13.9 %collective-permute-start.8 = (bf16[8,16,2048]{2,1,0:T(8,128)(2,1)S(1)}, bf16[8,16,2048]{2,1,0:T(8,128)(2,1)S(1)}, u32[]{:S(2)}, u32[]{:S(2)}) collective-permute-start(bf16[8,16,2048]{2,1,0:T(8,128)(2,1)S(1)} %collective-permute-done.refs_1_), channel_id=1, source_target_pairs={{0,8},{8,0},{16,24},{24,16},{32,40},{40,32},{48,56},{56,48},{64,72... | collective-permute-start | bytes 1572872 | tf_op jit(solution)/shard_map/ppermute | solution.py:386
  117.3 11.0 %collective-permute-start.6 = (bf16[8,16,2048]{2,1,0:T(8,128)(2,1)S(1)}, bf16[8,16,2048]{2,1,0:T(8,128)(2,1)S(1)}, u32[]{:S(2)}, u32[]{:S(2)}) collective-permute-start(bf16[8,16,2048]{2,1,0:T(8,128)(2,1)S(1)} %collective-permute-done.2.refs_3_), channel_id=1, source_target_pairs={{0,16},{8,24},{16,0},{24,8},{32,48},{40,56},{48,32},{56,40},{64,80... | collective-permute-start | bytes 1572872 | tf_op jit(solution)/shard_map/ppermute | solution.py:386
  118.0 10.4 %collective-permute-start.21 = (bf16[16,16,1024]{2,1,0:T(8,128)(2,1)S(1)}, bf16[16,16,1024]{2,1,0:T(8,128)(2,1)S(1)}, u32[]{:S(2)}, u32[]{:S(2)}) collective-permute-start(bf16[16,16,1024]{2,1,0:T(8,128)(2,1)S(1)} %collective-permute-done.19.refs_21_), channel_id=1, source_target_pairs={{0,1},{1,2},{2,3},{3,0},{4,5},{5,6},{6,7},{7,4},{8,11},{9,8},{10,9... | collective-permute-start | bytes 1572872 | tf_op jit(solution)/shard_map/ppermute | solution.py:381
  122.9 5.5 %collective-permute-start.10 = (bf16[8,16,2048]{2,1,0:T(8,128)(2,1)S(1)}, bf16[8,16,2048]{2,1,0:T(8,128)(2,1)S(1)}, u32[]{:S(2)}, u32[]{:S(2)}) collective-permute-start(bf16[8,16,2048]{2,1,0:T(8,128)(2,1)S(1)} %collective-permute-done.2.refs_3_), channel_id=1, source_target_pairs={{0,8},{8,0},{16,24},{24,16},{32,40},{40,32},{48,56},{56,48},{64,72... | collective-permute-start | bytes 1572872 | tf_op jit(solution)/shard_map/ppermute | solution.py:386
  122.9 5.5 %collective-permute-start.13 = (bf16[8,16,2048]{2,1,0:T(8,128)(2,1)S(1)}, bf16[8,16,2048]{2,1,0:T(8,128)(2,1)S(1)}, u32[]{:S(2)}, u32[]{:S(2)}) collective-permute-start(bf16[8,16,2048]{2,1,0:T(8,128)(2,1)S(1)} %collective-permute-done.5.refs_6_), channel_id=1, source_target_pairs={{0,8},{8,0},{16,24},{24,16},{32,40},{40,32},{48,56},{56,48},{64,72... | collective-permute-start | bytes 1572872 | tf_op jit(solution)/shard_map/ppermute | solution.py:386
  123.5 5.0 %collective-permute-start.12 = (bf16[8,16,2048]{2,1,0:T(8,128)(2,1)S(1)}, bf16[8,16,2048]{2,1,0:T(8,128)(2,1)S(1)}, u32[]{:S(2)}, u32[]{:S(2)}) collective-permute-start(bf16[8,16,2048]{2,1,0:T(8,128)(2,1)S(1)} %collective-permute-done.4.refs_5_), channel_id=1, source_target_pairs={{0,8},{8,0},{16,24},{24,16},{32,40},{40,32},{48,56},{56,48},{64,72... | collective-permute-start | bytes 1572872 | tf_op jit(solution)/shard_map/ppermute | solution.py:386
  128.3 1.9 %collective-permute-start.14 = (bf16[8,16,2048]{2,1,0:T(8,128)(2,1)S(1)}, bf16[8,16,2048]{2,1,0:T(8,128)(2,1)S(1)}, u32[]{:S(2)}, u32[]{:S(2)}) collective-permute-start(bf16[8,16,2048]{2,1,0:T(8,128)(2,1)S(1)} %collective-permute-done.6.refs_7_), channel_id=1, source_target_pairs={{0,8},{8,0},{16,24},{24,16},{32,40},{40,32},{48,56},{56,48},{64,72... | collective-permute-start | bytes 1572872 | tf_op jit(solution)/shard_map/ppermute | solution.py:386

commit v6 on v5

--- a/solution.py
+++ b/solution.py
@@ -185,7 +185,7 @@
     for n in range(groups):
         for copy in orbitals[n]:
             copy.wait()
-        lax.fori_loop(n * span // wide, (n + 1) * span // wide, x_stage, 0)
+        lax.fori_loop(n * span // wide, (n + 1) * span // wide, x_stage, 0, unroll=4)
 
     first = lax.broadcasted_iota(jnp.int32, (8, LANES), 1) < EDGE
 
@@ -224,7 +224,7 @@
             table[pl.ds(at + EDGE, EDGE), :] = jnp.where(lower_lanes, pltpu.roll(re, EDGE, 1), im)
         return carry
 
-    lax.fori_loop(0, HALF + 1, yz_stage, 0)
+    lax.fori_loop(0, HALF + 1, yz_stage, 0, unroll=3)
 
     to_scalar.wait()
     per_row, per_col = left.shape[2] // LANES, right.shape[2] // LANES
@@ -232,8 +232,9 @@
     sublane_bits = [(sublane & (1 << i)) != 0 for i in range(3)]
 
     def pick(q, picked):
+        line = rows.at[q]
         for j in range(0, LANES, 8):
-            some = [table[pl.ds(rows[q, j + t], 8, stride=0), :] for t in range(8)]
+            some = [table[pl.ds(line[j + t], 8, stride=0), :] for t in range(8)]
             for bit in sublane_bits:
                 some = [jnp.where(bit, some[n + 1], some[n]) for n in range(0, len(some), 2)]
             picked[pl.ds(j, 8), :] = some[0]
@@ -267,7 +268,7 @@
         finish(2 * i + 1, picked_1)
         return carry
 
-    lax.fori_loop(0, count // 2, select, 0)
+    lax.fori_loop(0, count // 2, select, 0, unroll=8)
 
 
 def densities(n_row, n_col, valence, conduction, valence_energy, conduction_energy, pair_list, sphere_index):

time: 143 us -> 131 us (0.916)
  Pallas kernels: 55.5 us -> 43.5 us
    pallas_call x1, Pallas kernels: 43.7 us -> 31.7 us  [densities(): pl.pallas_call(lambda *refs: density_kernel(n_pairs * n_row * n_col, *ref...]
where the time goes in v6:
time: 131 us; the launch traced here: 130 us
  waiting for transfers between devices  44.6 us (34%)
  Pallas kernels  43.5 us (33%)
  starting transfers between devices  25 us (19%)
  blocking collectives  16.9 us (13%)
    pallas_call x1, Pallas kernels, densities(): pl.pallas_call(lambda *refs: density_kernel(n_pairs * n_row * n_col, *ref...  31.7 us
    ppermute x11, waiting for transfers between devices, shift(): return lax.ppermute(value, ('col', 'row'), pairs)  17.3 us
    all_to_all x1, blocking collectives, per_device(): lax.all_to_all(right, 'col', split_axis=0, concat_axis=0, tiled=True)  16.9 us
    ppermute x11, waiting for transfers between devices, swap(): return lax.ppermute(value, axis, [(i, i ^ bit) for i in range(count)])  15.2 us
    ppermute x11, starting transfers between devices, shift(): return lax.ppermute(value, ('col', 'row'), pairs)  13.2 us
    all_to_all x1, waiting for transfers between devices, per_device(): left = lax.all_to_all(left, 'row', split_axis=0, concat_axis=0, tiled=True)  12.1 us
    pallas_call x1, Pallas kernels, product(): pl.pallas_call(lambda *refs: product_kernel(n_left, n_right, *refs), grid...  11.8 us
    ppermute x11, starting transfers between devices, swap(): return lax.ppermute(value, axis, [(i, i ^ bit) for i in range(count)])  8.34 us
  transfers between devices with their start and end apart: 23, of which 10 were waited for; matrix products, arithmetic and copies ran while one was open for 0% of the time, Pallas kernels for 0%

profile of v6, /device:TPU:0, one launch (start us, length us, event | category | flops | bytes accessed | tf_op | source)
XLA Modules:
  0.0 130.1 jit_solution(14621896245380979926)
XLA Ops:
  0.0 31.7 %density.1 = (bf16[8,16,2048]{2,1,0:T(8,128)(2,1)}, bf16[16,16,1024]{2,1,0:T(8,128)(2,1)}) custom-call(f32[4,64,4096]{2,1,0:T(8,128)} %refs_0_.1, f32[4,64,4096]{2,1,0:T(8,128)} %refs_1_.1, f32[4]{0:T(128)} %refs_2_.1, f32[4]{0:T(128)} %refs_3_.1, s32[2,8]{1,0:T(2,128)} %bitcast.3, s32[128,128]{1,0:T(8,128)} %bitcast.2, ...), custom_call_target="tpu_custom_call" | custom-call | tf_op jit(solution)/shard_map/density/pallas_call | solution.py:279
  31.7 16.9 %all_to_all.10.refs_16_ = bf16[16,16,1024]{2,1,0:T(8,128)(2,1)S(1)} all-to-all(bf16[16,16,1024]{2,1,0:T(8,128)(2,1)} %get-tuple-element.9), channel_id=1, replica_groups=mesh['col'=16,'row'=8] {'col'}, dimensions={0} | all-to-all | bytes 1048576 | tf_op jit(solution)/shard_map/all_to_all | solution.py:413
  48.6 3.6 %collective-permute-start.18 = (bf16[16,16,1024]{2,1,0:T(8,128)(2,1)S(1)}, bf16[16,16,1024]{2,1,0:T(8,128)(2,1)S(1)}, u32[]{:S(2)}, u32[]{:S(2)}) collective-permute-start(bf16[16,16,1024]{2,1,0:T(8,128)(2,1)S(1)} %all_to_all.10.refs_16_), channel_id=1, source_target_pairs={{0,4},{1,5},{2,6},{3,7},{4,0},{5,1},{6,2},{7,3},{8,12},{9,13},{10,... | collective-permute-start | bytes 1572872 | tf_op jit(solution)/shard_map/ppermute | solution.py:387
  52.2 2.8 %collective-permute-start.16 = (bf16[16,16,1024]{2,1,0:T(8,128)(2,1)S(1)}, bf16[16,16,1024]{2,1,0:T(8,128)(2,1)S(1)}, u32[]{:S(2)}, u32[]{:S(2)}) collective-permute-start(bf16[16,16,1024]{2,1,0:T(8,128)(2,1)S(1)} %all_to_all.10.refs_16_), channel_id=1, source_target_pairs={{0,3},{1,0},{2,1},{3,2},{4,7},{5,4},{6,5},{7,6},{8,9},{9,10},{10,1... | collective-permute-start | bytes 1572872 | tf_op jit(solution)/shard_map/ppermute | solution.py:382
  55.0 3.5 %all-to-all-start.1 = ((bf16[8,16,2048]{2,1,0:T(8,128)(2,1)}), bf16[8,16,2048]{2,1,0:T(8,128)(2,1)S(1)}, u32[]{:S(2)}, u32[]{:S(2)}) async-start(bf16[8,16,2048]{2,1,0:T(8,128)(2,1)} %get-tuple-element.11), calls=%async_computation.1 | async-start | bytes 1048576 | tf_op jit(solution)/shard_map/all_to_all | solution.py:417
  58.5 1.9 %collective-permute-start.15 = (bf16[16,16,1024]{2,1,0:T(8,128)(2,1)S(1)}, bf16[16,16,1024]{2,1,0:T(8,128)(2,1)S(1)}, u32[]{:S(2)}, u32[]{:S(2)}) collective-permute-start(bf16[16,16,1024]{2,1,0:T(8,128)(2,1)S(1)} %all_to_all.10.refs_16_), channel_id=1, source_target_pairs={{0,1},{1,2},{2,3},{3,0},{4,5},{5,6},{6,7},{7,4},{8,11},{9,8},{10,9... | collective-permute-start | bytes 1572872 | tf_op jit(solution)/shard_map/ppermute | solution.py:382
  60.4 12.1 %all-to-all-done.1.refs_0_ = bf16[8,16,2048]{2,1,0:T(8,128)(2,1)S(1)} async-done(((bf16[8,16,2048]{2,1,0:T(8,128)(2,1)}), bf16[8,16,2048]{2,1,0:T(8,128)(2,1)S(1)}, u32[]{:S(2)}, u32[]{:S(2)}) %all-to-all-start.1) | async-done | bytes 524320 | tf_op jit(solution)/shard_map/all_to_all | solution.py:417
  72.5 0.7 collective-permute-start.1
  73.2 1.4 %collective-permute-start = (bf16[8,16,2048]{2,1,0:T(8,128)(2,1)S(1)}, bf16[8,16,2048]{2,1,0:T(8,128)(2,1)S(1)}, u32[]{:S(2)}, u32[]{:S(2)}) collective-permute-start(bf16[8,16,2048]{2,1,0:T(8,128)(2,1)S(1)} %all-to-all-done.1.refs_0_), channel_id=1, source_target_pairs={{0,32},{1,33},{2,34},{3,35},{4,36},{5,37},{6,38},{7,39},{8,104},{9... | collective-permute-start | bytes 1572872 | tf_op jit(solution)/shard_map/ppermute | solution.py:382
  74.6 3.6 %collective-permute-start.20 = (bf16[16,16,1024]{2,1,0:T(8,128)(2,1)S(1)}, bf16[16,16,1024]{2,1,0:T(8,128)(2,1)S(1)}, u32[]{:S(2)}, u32[]{:S(2)}) collective-permute-start(bf16[16,16,1024]{2,1,0:T(8,128)(2,1)S(1)} %collective-permute-done.18.refs_20_), channel_id=1, source_target_pairs={{0,3},{1,0},{2,1},{3,2},{4,7},{5,4},{6,5},{7,6},{8,9},{9,10},{10,1... | collective-permute-start | bytes 1572872 | tf_op jit(solution)/shard_map/ppermute | solution.py:382
  78.2 8.6 %collective-permute-done.3.refs_4_ = bf16[8,16,2048]{2,1,0:T(8,128)(2,1)S(1)} collective-permute-done((bf16[8,16,2048]{2,1,0:T(8,128)(2,1)S(1)}, bf16[8,16,2048]{2,1,0:T(8,128)(2,1)S(1)}, u32[]{:S(2)}, u32[]{:S(2)}) %collective-permute-start.3) | collective-permute-done | bytes 524320 | tf_op jit(solution)/shard_map/ppermute | solution.py:387
  86.9 2.9 %collective-permute-start.11 = (bf16[8,16,2048]{2,1,0:T(8,128)(2,1)S(1)}, bf16[8,16,2048]{2,1,0:T(8,128)(2,1)S(1)}, u32[]{:S(2)}, u32[]{:S(2)}) collective-permute-start(bf16[8,16,2048]{2,1,0:T(8,128)(2,1)S(1)} %collective-permute-done.3.refs_4_), channel_id=1, source_target_pairs={{0,8},{8,0},{16,24},{24,16},{32,40},{40,32},{48,56},{56,48},{64,72... | collective-permute-start | bytes 1572872 | tf_op jit(solution)/shard_map/ppermute | solution.py:387
  89.9 0.4 collective-permute-done.20.refs_22_
  90.3 2.8 %collective-permute-start.5 = (bf16[8,16,2048]{2,1,0:T(8,128)(2,1)S(1)}, bf16[8,16,2048]{2,1,0:T(8,128)(2,1)S(1)}, u32[]{:S(2)}, u32[]{:S(2)}) collective-permute-start(bf16[8,16,2048]{2,1,0:T(8,128)(2,1)S(1)} %collective-permute-done.3.refs_4_), channel_id=1, source_target_pairs={{0,96},{1,97},{2,98},{3,99},{4,100},{5,101},{6,102},{7,103},{8,40}... | collective-permute-start | bytes 1572872 | tf_op jit(solution)/shard_map/ppermute | solution.py:382
  93.1 4.5 %collective-permute-done.17.refs_19_ = bf16[16,16,1024]{2,1,0:T(8,128)(2,1)S(1)} collective-permute-done((bf16[16,16,1024]{2,1,0:T(8,128)(2,1)S(1)}, bf16[16,16,1024]{2,1,0:T(8,128)(2,1)S(1)}, u32[]{:S(2)}, u32[]{:S(2)}) %collective-permute-start.17) | collective-permute-done | bytes 524320 | tf_op jit(solution)/shard_map/ppermute | solution.py:382
  97.6 0.5 collective-permute-start.8
  98.1 7.3 %collective-permute-done.2.refs_3_ = bf16[8,16,2048]{2,1,0:T(8,128)(2,1)S(1)} collective-permute-done((bf16[8,16,2048]{2,1,0:T(8,128)(2,1)S(1)}, bf16[8,16,2048]{2,1,0:T(8,128)(2,1)S(1)}, u32[]{:S(2)}, u32[]{:S(2)}) %collective-permute-start.2) | collective-permute-done | bytes 524320 | tf_op jit(solution)/shard_map/ppermute | solution.py:382
  105.4 0.7 collective-permute-start.6
  106.1 4.9 %collective-permute-done.4.refs_5_ = bf16[8,16,2048]{2,1,0:T(8,128)(2,1)S(1)} collective-permute-done((bf16[8,16,2048]{2,1,0:T(8,128)(2,1)S(1)}, bf16[8,16,2048]{2,1,0:T(8,128)(2,1)S(1)}, u32[]{:S(2)}, u32[]{:S(2)}) %collective-permute-start.4) | collective-permute-done | bytes 524320 | tf_op jit(solution)/shard_map/ppermute | solution.py:382
  111.0 0.5 collective-permute-start.13
  111.6 4.8 %collective-permute-done.6.refs_7_ = bf16[8,16,2048]{2,1,0:T(8,128)(2,1)S(1)} collective-permute-done((bf16[8,16,2048]{2,1,0:T(8,128)(2,1)S(1)}, bf16[8,16,2048]{2,1,0:T(8,128)(2,1)S(1)}, u32[]{:S(2)}, u32[]{:S(2)}) %collective-permute-start.6) | collective-permute-done | bytes 524320 | tf_op jit(solution)/shard_map/ppermute | solution.py:387
  116.3 0.1 collective-permute-done.21.refs_23_
  116.5 1.8 %collective-permute-done.14.refs_15_ = bf16[8,16,2048]{2,1,0:T(8,128)(2,1)S(1)} collective-permute-done((bf16[8,16,2048]{2,1,0:T(8,128)(2,1)S(1)}, bf16[8,16,2048]{2,1,0:T(8,128)(2,1)S(1)}, u32[]{:S(2)}, u32[]{:S(2)}) %collective-permute-start.14) | collective-permute-done | bytes 524320 | tf_op jit(solution)/shard_map/ppermute | solution.py:387
  118.2 11.8 %product.1 = f32[2048,1024]{1,0:T(8,128)} custom-call(bf16[8,16,2048]{2,1,0:T(8,128)(2,1)S(1)} %all-to-all-done.1.refs_0_, bf16[8,16,2048]{2,1,0:T(8,128)(2,1)S(1)} %collective-permute-done.refs_1_, bf16[8,16,2048]{2,1,0:T(8,128)(2,1)S(1)} %collective-permute-done.1.refs_2_, bf16[8,16,2048]{2,1,0:T(8,128)(2,1)S(1)} %collective-permute-done.2.refs_3_, ...), custom_call_target="tpu_custom_call" | custom-call | tf_op jit(solution)/shard_map/product/pallas_call | solution.py:351
  (25 shorter events, 0.2 us)
Async XLA Ops:
  48.6 23.9 %collective-permute-start.18 = (bf16[16,16,1024]{2,1,0:T(8,128)(2,1)S(1)}, bf16[16,16,1024]{2,1,0:T(8,128)(2,1)S(1)}, u32[]{:S(2)}, u32[]{:S(2)}) collective-permute-start(bf16[16,16,1024]{2,1,0:T(8,128)(2,1)S(1)} %all_to_all.10.refs_16_), channel_id=1, source_target_pairs={{0,4},{1,5},{2,6},{3,7},{4,0},{5,1},{6,2},{7,3},{8,12},{9,13},{10,... | collective-permute-start | bytes 1572872 | tf_op jit(solution)/shard_map/ppermute | solution.py:387
  52.2 21.0 %collective-permute-start.16 = (bf16[16,16,1024]{2,1,0:T(8,128)(2,1)S(1)}, bf16[16,16,1024]{2,1,0:T(8,128)(2,1)S(1)}, u32[]{:S(2)}, u32[]{:S(2)}) collective-permute-start(bf16[16,16,1024]{2,1,0:T(8,128)(2,1)S(1)} %all_to_all.10.refs_16_), channel_id=1, source_target_pairs={{0,3},{1,0},{2,1},{3,2},{4,7},{5,4},{6,5},{7,6},{8,9},{9,10},{10,1... | collective-permute-start | bytes 1572872 | tf_op jit(solution)/shard_map/ppermute | solution.py:382
  55.0 17.5 %all-to-all-start.1 = ((bf16[8,16,2048]{2,1,0:T(8,128)(2,1)}), bf16[8,16,2048]{2,1,0:T(8,128)(2,1)S(1)}, u32[]{:S(2)}, u32[]{:S(2)}) async-start(bf16[8,16,2048]{2,1,0:T(8,128)(2,1)} %get-tuple-element.11), calls=%async_computation.1 | async-start | bytes 1048576 | tf_op jit(solution)/shard_map/all_to_all | solution.py:417
  58.5 16.1 %collective-permute-start.15 = (bf16[16,16,1024]{2,1,0:T(8,128)(2,1)S(1)}, bf16[16,16,1024]{2,1,0:T(8,128)(2,1)S(1)}, u32[]{:S(2)}, u32[]{:S(2)}) collective-permute-start(bf16[16,16,1024]{2,1,0:T(8,128)(2,1)S(1)} %all_to_all.10.refs_16_), channel_id=1, source_target_pairs={{0,1},{1,2},{2,3},{3,0},{4,5},{5,6},{6,7},{7,4},{8,11},{9,8},{10,9... | collective-permute-start | bytes 1572872 | tf_op jit(solution)/shard_map/ppermute | solution.py:382
  72.5 5.7 %collective-permute-start.7 = (bf16[8,16,2048]{2,1,0:T(8,128)(2,1)S(1)}, bf16[8,16,2048]{2,1,0:T(8,128)(2,1)S(1)}, u32[]{:S(2)}, u32[]{:S(2)}) collective-permute-start(bf16[8,16,2048]{2,1,0:T(8,128)(2,1)S(1)} %all-to-all-done.1.refs_0_), channel_id=1, source_target_pairs={{0,8},{8,0},{16,24},{24,16},{32,40},{40,32},{48,56},{56,48},{64,72... | collective-permute-start | bytes 1572872 | tf_op jit(solution)/shard_map/ppermute | solution.py:387
  72.5 14.3 %collective-permute-start.3 = (bf16[8,16,2048]{2,1,0:T(8,128)(2,1)S(1)}, bf16[8,16,2048]{2,1,0:T(8,128)(2,1)S(1)}, u32[]{:S(2)}, u32[]{:S(2)}) collective-permute-start(bf16[8,16,2048]{2,1,0:T(8,128)(2,1)S(1)} %all-to-all-done.1.refs_0_), channel_id=1, source_target_pairs={{0,16},{8,24},{16,0},{24,8},{32,48},{40,56},{48,32},{56,40},{64,80... | collective-permute-start | bytes 1572872 | tf_op jit(solution)/shard_map/ppermute | solution.py:387
  72.5 14.4 %collective-permute-start.1 = (bf16[8,16,2048]{2,1,0:T(8,128)(2,1)S(1)}, bf16[8,16,2048]{2,1,0:T(8,128)(2,1)S(1)}, u32[]{:S(2)}, u32[]{:S(2)}) collective-permute-start(bf16[8,16,2048]{2,1,0:T(8,128)(2,1)S(1)} %all-to-all-done.1.refs_0_), channel_id=1, source_target_pairs={{0,96},{1,97},{2,98},{3,99},{4,100},{5,101},{6,102},{7,103},{8,40}... | collective-permute-start | bytes 1572872 | tf_op jit(solution)/shard_map/ppermute | solution.py:382
  73.2 16.7 %collective-permute-start = (bf16[8,16,2048]{2,1,0:T(8,128)(2,1)S(1)}, bf16[8,16,2048]{2,1,0:T(8,128)(2,1)S(1)}, u32[]{:S(2)}, u32[]{:S(2)}) collective-permute-start(bf16[8,16,2048]{2,1,0:T(8,128)(2,1)S(1)} %all-to-all-done.1.refs_0_), channel_id=1, source_target_pairs={{0,32},{1,33},{2,34},{3,35},{4,36},{5,37},{6,38},{7,39},{8,104},{9... | collective-permute-start | bytes 1572872 | tf_op jit(solution)/shard_map/ppermute | solution.py:382
  74.6 15.7 %collective-permute-start.20 = (bf16[16,16,1024]{2,1,0:T(8,128)(2,1)S(1)}, bf16[16,16,1024]{2,1,0:T(8,128)(2,1)S(1)}, u32[]{:S(2)}, u32[]{:S(2)}) collective-permute-start(bf16[16,16,1024]{2,1,0:T(8,128)(2,1)S(1)} %collective-permute-done.18.refs_20_), channel_id=1, source_target_pairs={{0,3},{1,0},{2,1},{3,2},{4,7},{5,4},{6,5},{7,6},{8,9},{9,10},{10,1... | collective-permute-start | bytes 1572872 | tf_op jit(solution)/shard_map/ppermute | solution.py:382
  78.2 14.9 %collective-permute-start.19 = (bf16[16,16,1024]{2,1,0:T(8,128)(2,1)S(1)}, bf16[16,16,1024]{2,1,0:T(8,128)(2,1)S(1)}, u32[]{:S(2)}, u32[]{:S(2)}) collective-permute-start(bf16[16,16,1024]{2,1,0:T(8,128)(2,1)S(1)} %collective-permute-done.18.refs_20_), channel_id=1, source_target_pairs={{0,1},{1,2},{2,3},{3,0},{4,5},{5,6},{6,7},{7,4},{8,11},{9,8},{10,9... | collective-permute-start | bytes 1572872 | tf_op jit(solution)/shard_map/ppermute | solution.py:382
  86.8 10.7 %collective-permute-start.17 = (bf16[16,16,1024]{2,1,0:T(8,128)(2,1)S(1)}, bf16[16,16,1024]{2,1,0:T(8,128)(2,1)S(1)}, u32[]{:S(2)}, u32[]{:S(2)}) collective-permute-start(bf16[16,16,1024]{2,1,0:T(8,128)(2,1)S(1)} %collective-permute-done.15.refs_17_), channel_id=1, source_target_pairs={{0,1},{1,2},{2,3},{3,0},{4,5},{5,6},{6,7},{7,4},{8,11},{9,8},{10,9... | collective-permute-start | bytes 1572872 | tf_op jit(solution)/shard_map/ppermute | solution.py:382
  86.9 10.7 %collective-permute-start.11 = (bf16[8,16,2048]{2,1,0:T(8,128)(2,1)S(1)}, bf16[8,16,2048]{2,1,0:T(8,128)(2,1)S(1)}, u32[]{:S(2)}, u32[]{:S(2)}) collective-permute-start(bf16[8,16,2048]{2,1,0:T(8,128)(2,1)S(1)} %collective-permute-done.3.refs_4_), channel_id=1, source_target_pairs={{0,8},{8,0},{16,24},{24,16},{32,40},{40,32},{48,56},{56,48},{64,72... | collective-permute-start | bytes 1572872 | tf_op jit(solution)/shard_map/ppermute | solution.py:387
  89.9 15.5 %collective-permute-start.2 = (bf16[8,16,2048]{2,1,0:T(8,128)(2,1)S(1)}, bf16[8,16,2048]{2,1,0:T(8,128)(2,1)S(1)}, u32[]{:S(2)}, u32[]{:S(2)}) collective-permute-start(bf16[8,16,2048]{2,1,0:T(8,128)(2,1)S(1)} %collective-permute-done.refs_1_), channel_id=1, source_target_pairs={{0,32},{1,33},{2,34},{3,35},{4,36},{5,37},{6,38},{7,39},{8,104},{9... | collective-permute-start | bytes 1572872 | tf_op jit(solution)/shard_map/ppermute | solution.py:382
  90.3 15.7 %collective-permute-start.5 = (bf16[8,16,2048]{2,1,0:T(8,128)(2,1)S(1)}, bf16[8,16,2048]{2,1,0:T(8,128)(2,1)S(1)}, u32[]{:S(2)}, u32[]{:S(2)}) collective-permute-start(bf16[8,16,2048]{2,1,0:T(8,128)(2,1)S(1)} %collective-permute-done.3.refs_4_), channel_id=1, source_target_pairs={{0,96},{1,97},{2,98},{3,99},{4,100},{5,101},{6,102},{7,103},{8,40}... | collective-permute-start | bytes 1572872 | tf_op jit(solution)/shard_map/ppermute | solution.py:382
  93.1 17.9 %collective-permute-start.4 = (bf16[8,16,2048]{2,1,0:T(8,128)(2,1)S(1)}, bf16[8,16,2048]{2,1,0:T(8,128)(2,1)S(1)}, u32[]{:S(2)}, u32[]{:S(2)}) collective-permute-start(bf16[8,16,2048]{2,1,0:T(8,128)(2,1)S(1)} %collective-permute-done.3.refs_4_), channel_id=1, source_target_pairs={{0,32},{1,33},{2,34},{3,35},{4,36},{5,37},{6,38},{7,39},{8,104},{9... | collective-permute-start | bytes 1572872 | tf_op jit(solution)/shard_map/ppermute | solution.py:382
  97.6 13.4 %collective-permute-start.9 = (bf16[8,16,2048]{2,1,0:T(8,128)(2,1)S(1)}, bf16[8,16,2048]{2,1,0:T(8,128)(2,1)S(1)}, u32[]{:S(2)}, u32[]{:S(2)}) collective-permute-start(bf16[8,16,2048]{2,1,0:T(8,128)(2,1)S(1)} %collective-permute-done.1.refs_2_), channel_id=1, source_target_pairs={{0,8},{8,0},{16,24},{24,16},{32,40},{40,32},{48,56},{56,48},{64,72... | collective-permute-start | bytes 1572872 | tf_op jit(solution)/shard_map/ppermute | solution.py:387
  97.6 13.9 %collective-permute-start.8 = (bf16[8,16,2048]{2,1,0:T(8,128)(2,1)S(1)}, bf16[8,16,2048]{2,1,0:T(8,128)(2,1)S(1)}, u32[]{:S(2)}, u32[]{:S(2)}) collective-permute-start(bf16[8,16,2048]{2,1,0:T(8,128)(2,1)S(1)} %collective-permute-done.refs_1_), channel_id=1, source_target_pairs={{0,8},{8,0},{16,24},{24,16},{32,40},{40,32},{48,56},{56,48},{64,72... | collective-permute-start | bytes 1572872 | tf_op jit(solution)/shard_map/ppermute | solution.py:387
  105.4 11.0 %collective-permute-start.6 = (bf16[8,16,2048]{2,1,0:T(8,128)(2,1)S(1)}, bf16[8,16,2048]{2,1,0:T(8,128)(2,1)S(1)}, u32[]{:S(2)}, u32[]{:S(2)}) collective-permute-start(bf16[8,16,2048]{2,1,0:T(8,128)(2,1)S(1)} %collective-permute-done.2.refs_3_), channel_id=1, source_target_pairs={{0,16},{8,24},{16,0},{24,8},{32,48},{40,56},{48,32},{56,40},{64,80... | collective-permute-start | bytes 1572872 | tf_op jit(solution)/shard_map/ppermute | solution.py:387
  106.1 10.4 %collective-permute-start.21 = (bf16[16,16,1024]{2,1,0:T(8,128)(2,1)S(1)}, bf16[16,16,1024]{2,1,0:T(8,128)(2,1)S(1)}, u32[]{:S(2)}, u32[]{:S(2)}) collective-permute-start(bf16[16,16,1024]{2,1,0:T(8,128)(2,1)S(1)} %collective-permute-done.19.refs_21_), channel_id=1, source_target_pairs={{0,1},{1,2},{2,3},{3,0},{4,5},{5,6},{6,7},{7,4},{8,11},{9,8},{10,9... | collective-permute-start | bytes 1572872 | tf_op jit(solution)/shard_map/ppermute | solution.py:382
  111.0 5.5 %collective-permute-start.10 = (bf16[8,16,2048]{2,1,0:T(8,128)(2,1)S(1)}, bf16[8,16,2048]{2,1,0:T(8,128)(2,1)S(1)}, u32[]{:S(2)}, u32[]{:S(2)}) collective-permute-start(bf16[8,16,2048]{2,1,0:T(8,128)(2,1)S(1)} %collective-permute-done.2.refs_3_), channel_id=1, source_target_pairs={{0,8},{8,0},{16,24},{24,16},{32,40},{40,32},{48,56},{56,48},{64,72... | collective-permute-start | bytes 1572872 | tf_op jit(solution)/shard_map/ppermute | solution.py:387
  111.0 5.5 %collective-permute-start.13 = (bf16[8,16,2048]{2,1,0:T(8,128)(2,1)S(1)}, bf16[8,16,2048]{2,1,0:T(8,128)(2,1)S(1)}, u32[]{:S(2)}, u32[]{:S(2)}) collective-permute-start(bf16[8,16,2048]{2,1,0:T(8,128)(2,1)S(1)} %collective-permute-done.5.refs_6_), channel_id=1, source_target_pairs={{0,8},{8,0},{16,24},{24,16},{32,40},{40,32},{48,56},{56,48},{64,72... | collective-permute-start | bytes 1572872 | tf_op jit(solution)/shard_map/ppermute | solution.py:387
  111.5 5.0 %collective-permute-start.12 = (bf16[8,16,2048]{2,1,0:T(8,128)(2,1)S(1)}, bf16[8,16,2048]{2,1,0:T(8,128)(2,1)S(1)}, u32[]{:S(2)}, u32[]{:S(2)}) collective-permute-start(bf16[8,16,2048]{2,1,0:T(8,128)(2,1)S(1)} %collective-permute-done.4.refs_5_), channel_id=1, source_target_pairs={{0,8},{8,0},{16,24},{24,16},{32,40},{40,32},{48,56},{56,48},{64,72... | collective-permute-start | bytes 1572872 | tf_op jit(solution)/shard_map/ppermute | solution.py:387
  116.3 1.9 %collective-permute-start.14 = (bf16[8,16,2048]{2,1,0:T(8,128)(2,1)S(1)}, bf16[8,16,2048]{2,1,0:T(8,128)(2,1)S(1)}, u32[]{:S(2)}, u32[]{:S(2)}) collective-permute-start(bf16[8,16,2048]{2,1,0:T(8,128)(2,1)S(1)} %collective-permute-done.6.refs_7_), channel_id=1, source_target_pairs={{0,8},{8,0},{16,24},{24,16},{32,40},{40,32},{48,56},{56,48},{64,72... | collective-permute-start | bytes 1572872 | tf_op jit(solution)/shard_map/ppermute | solution.py:387

commit v7 on v6

--- a/solution.py
+++ b/solution.py
@@ -317,28 +317,14 @@
 
 
 def product_kernel(n_left, n_right, *refs):
-    left_in, right_in = refs[:n_left], refs[n_left : n_left + n_right]
-    out, right, right_sem = refs[n_left + n_right :]
-
-    @pl.when(pl.program_id(0) == 0)
-    def _():
-        right_slots = right_places(lax.axis_index("row"), lax.axis_index("col") & 1)
-        copies = [
-            pltpu.make_async_copy(piece, right.at[:, right_slots[j]], right_sem.at[j])
-            for j, piece in enumerate(right_in)
-        ]
-        for copy in copies:
-            copy.start()
-        for copy in copies:
-            copy.wait()
-
+    left, right, out = refs[:n_left], refs[n_left : n_left + n_right], refs[n_left + n_right]
+    col, row = lax.axis_index("col"), lax.axis_index("row")
+    left_slots, right_slots = left_places(col), right_places(row, col & 1)
     rows = out.shape[0]
     at = pl.multiple_of(pl.program_id(0) * rows, rows)
-    left_slots = left_places(lax.axis_index("col"))
-    depth = right.shape[1] * right.shape[2]
     out[...] = lax.dot_general(
-        jnp.concatenate([piece[:, :, pl.ds(at, rows)].reshape(depth, rows) for piece in left_in], axis=0),
-        jnp.concatenate([right[slot].reshape(depth, right.shape[3]) for slot in left_slots], axis=0),
+        jnp.concatenate([piece[slot, :, pl.ds(at, rows)] for slot in right_slots for piece in left], axis=0),
+        jnp.concatenate([piece[slot] for piece in right for slot in left_slots], axis=0),
         (((0,), (0,)), ((), ())),
         preferred_element_type=F32,
     )
@@ -347,18 +333,14 @@
 def product(left, right):
     n_left, n_right = len(left), len(right)
     rows, cols = left[0].shape[2], right[0].shape[2]
-    block = 256
+    block = 512
     return pl.pallas_call(
         lambda *refs: product_kernel(n_left, n_right, *refs),
         grid=(rows // block,),
-        in_specs=[pl.BlockSpec(memory_space=pltpu.VMEM)] * n_left + [pl.BlockSpec(memory_space=pl.ANY)] * n_right,
+        in_specs=[pl.BlockSpec(memory_space=pltpu.VMEM)] * (n_left + n_right),
         out_specs=pl.BlockSpec((block, cols), lambda m: (m, 0)),
         out_shape=jax.ShapeDtypeStruct((rows, cols), F32),
-        scratch_shapes=[
-            pltpu.VMEM((right[0].shape[0], n_right) + right[0].shape[1:], BF),
-            pltpu.SemaphoreType.DMA((n_right,)),
-        ],
-        compiler_params=pltpu.CompilerParams(vmem_limit_bytes=24 * 1024 * 1024),
+        compiler_params=pltpu.CompilerParams(vmem_limit_bytes=32 * 1024 * 1024),
         name="product",
     )(*left, *right)
 

time: 131 us -> 131 us (level)
  no operation moved by 1% of the time
where the time goes in v7:
time: 131 us; the launch traced here: 129 us
  waiting for transfers between devices  44.6 us (34%)
  Pallas kernels  42.7 us (33%)
  starting transfers between devices  25 us (19%)
  blocking collectives  16.9 us (13%)
    pallas_call x1, Pallas kernels, densities(): pl.pallas_call(lambda *refs: density_kernel(n_pairs * n_row * n_col, *ref...  31.7 us
    ppermute x11, waiting for transfers between devices, shift(): return lax.ppermute(value, ('col', 'row'), pairs)  17.3 us
    all_to_all x1, blocking collectives, per_device(): lax.all_to_all(right, 'col', split_axis=0, concat_axis=0, tiled=True)  16.9 us
    ppermute x11, waiting for transfers between devices, swap(): return lax.ppermute(value, axis, [(i, i ^ bit) for i in range(count)])  15.2 us
    ppermute x11, starting transfers between devices, shift(): return lax.ppermute(value, ('col', 'row'), pairs)  13.2 us
    all_to_all x1, waiting for transfers between devices, per_device(): left = lax.all_to_all(left, 'row', split_axis=0, concat_axis=0, tiled=True)  12.1 us
    pallas_call x1, Pallas kernels, product(): pl.pallas_call(lambda *refs: product_kernel(n_left, n_right, *refs), grid...  11 us
    ppermute x11, starting transfers between devices, swap(): return lax.ppermute(value, axis, [(i, i ^ bit) for i in range(count)])  8.34 us
  transfers between devices with their start and end apart: 23, of which 10 were waited for; matrix products, arithmetic and copies ran while one was open for 0% of the time, Pallas kernels for 0%

profile of v7, /device:TPU:0, one launch (start us, length us, event | category | flops | bytes accessed | tf_op | source)
XLA Modules:
  0.0 129.2 jit_solution(14169793677370441351)
XLA Ops:
  0.0 31.7 %density.1 = (bf16[8,16,2048]{2,1,0:T(8,128)(2,1)}, bf16[16,16,1024]{2,1,0:T(8,128)(2,1)}) custom-call(f32[4,64,4096]{2,1,0:T(8,128)} %refs_0_.1, f32[4,64,4096]{2,1,0:T(8,128)} %refs_1_.1, f32[4]{0:T(128)} %refs_2_.1, f32[4]{0:T(128)} %refs_3_.1, s32[2,8]{1,0:T(2,128)} %bitcast.3, s32[128,128]{1,0:T(8,128)} %bitcast.2, ...), custom_call_target="tpu_custom_call" | custom-call | tf_op jit(solution)/shard_map/density/pallas_call | solution.py:279
  31.7 16.9 %all_to_all.10.refs_16_ = bf16[16,16,1024]{2,1,0:T(8,128)(2,1)S(1)} all-to-all(bf16[16,16,1024]{2,1,0:T(8,128)(2,1)} %get-tuple-element.9), channel_id=1, replica_groups=mesh['col'=16,'row'=8] {'col'}, dimensions={0} | all-to-all | bytes 1048576 | tf_op jit(solution)/shard_map/all_to_all | solution.py:395
  48.6 3.6 %collective-permute-start.18 = (bf16[16,16,1024]{2,1,0:T(8,128)(2,1)S(1)}, bf16[16,16,1024]{2,1,0:T(8,128)(2,1)S(1)}, u32[]{:S(2)}, u32[]{:S(2)}) collective-permute-start(bf16[16,16,1024]{2,1,0:T(8,128)(2,1)S(1)} %all_to_all.10.refs_16_), channel_id=1, source_target_pairs={{0,4},{1,5},{2,6},{3,7},{4,0},{5,1},{6,2},{7,3},{8,12},{9,13},{10,... | collective-permute-start | bytes 1572872 | tf_op jit(solution)/shard_map/ppermute | solution.py:369
  52.2 2.8 %collective-permute-start.16 = (bf16[16,16,1024]{2,1,0:T(8,128)(2,1)S(1)}, bf16[16,16,1024]{2,1,0:T(8,128)(2,1)S(1)}, u32[]{:S(2)}, u32[]{:S(2)}) collective-permute-start(bf16[16,16,1024]{2,1,0:T(8,128)(2,1)S(1)} %all_to_all.10.refs_16_), channel_id=1, source_target_pairs={{0,3},{1,0},{2,1},{3,2},{4,7},{5,4},{6,5},{7,6},{8,9},{9,10},{10,1... | collective-permute-start | bytes 1572872 | tf_op jit(solution)/shard_map/ppermute | solution.py:364
  55.0 3.5 %all-to-all-start.1 = ((bf16[8,16,2048]{2,1,0:T(8,128)(2,1)}), bf16[8,16,2048]{2,1,0:T(8,128)(2,1)S(1)}, u32[]{:S(2)}, u32[]{:S(2)}) async-start(bf16[8,16,2048]{2,1,0:T(8,128)(2,1)} %get-tuple-element.11), calls=%async_computation.1 | async-start | bytes 1048576 | tf_op jit(solution)/shard_map/all_to_all | solution.py:399
  58.5 1.9 %collective-permute-start.15 = (bf16[16,16,1024]{2,1,0:T(8,128)(2,1)S(1)}, bf16[16,16,1024]{2,1,0:T(8,128)(2,1)S(1)}, u32[]{:S(2)}, u32[]{:S(2)}) collective-permute-start(bf16[16,16,1024]{2,1,0:T(8,128)(2,1)S(1)} %all_to_all.10.refs_16_), channel_id=1, source_target_pairs={{0,1},{1,2},{2,3},{3,0},{4,5},{5,6},{6,7},{7,4},{8,11},{9,8},{10,9... | collective-permute-start | bytes 1572872 | tf_op jit(solution)/shard_map/ppermute | solution.py:364
  60.4 12.1 %all-to-all-done.1.refs_0_ = bf16[8,16,2048]{2,1,0:T(8,128)(2,1)S(1)} async-done(((bf16[8,16,2048]{2,1,0:T(8,128)(2,1)}), bf16[8,16,2048]{2,1,0:T(8,128)(2,1)S(1)}, u32[]{:S(2)}, u32[]{:S(2)}) %all-to-all-start.1) | async-done | bytes 524320 | tf_op jit(solution)/shard_map/all_to_all | solution.py:399
  72.5 0.7 collective-permute-start.1
  73.2 1.4 %collective-permute-start = (bf16[8,16,2048]{2,1,0:T(8,128)(2,1)S(1)}, bf16[8,16,2048]{2,1,0:T(8,128)(2,1)S(1)}, u32[]{:S(2)}, u32[]{:S(2)}) collective-permute-start(bf16[8,16,2048]{2,1,0:T(8,128)(2,1)S(1)} %all-to-all-done.1.refs_0_), channel_id=1, source_target_pairs={{0,32},{1,33},{2,34},{3,35},{4,36},{5,37},{6,38},{7,39},{8,104},{9... | collective-permute-start | bytes 1572872 | tf_op jit(solution)/shard_map/ppermute | solution.py:364
  74.6 3.6 %collective-permute-start.20 = (bf16[16,16,1024]{2,1,0:T(8,128)(2,1)S(1)}, bf16[16,16,1024]{2,1,0:T(8,128)(2,1)S(1)}, u32[]{:S(2)}, u32[]{:S(2)}) collective-permute-start(bf16[16,16,1024]{2,1,0:T(8,128)(2,1)S(1)} %collective-permute-done.18.refs_20_), channel_id=1, source_target_pairs={{0,3},{1,0},{2,1},{3,2},{4,7},{5,4},{6,5},{7,6},{8,9},{9,10},{10,1... | collective-permute-start | bytes 1572872 | tf_op jit(solution)/shard_map/ppermute | solution.py:364
  78.2 8.6 %collective-permute-done.3.refs_4_ = bf16[8,16,2048]{2,1,0:T(8,128)(2,1)S(1)} collective-permute-done((bf16[8,16,2048]{2,1,0:T(8,128)(2,1)S(1)}, bf16[8,16,2048]{2,1,0:T(8,128)(2,1)S(1)}, u32[]{:S(2)}, u32[]{:S(2)}) %collective-permute-start.3) | collective-permute-done | bytes 524320 | tf_op jit(solution)/shard_map/ppermute | solution.py:369
  86.9 2.9 %collective-permute-start.11 = (bf16[8,16,2048]{2,1,0:T(8,128)(2,1)S(1)}, bf16[8,16,2048]{2,1,0:T(8,128)(2,1)S(1)}, u32[]{:S(2)}, u32[]{:S(2)}) collective-permute-start(bf16[8,16,2048]{2,1,0:T(8,128)(2,1)S(1)} %collective-permute-done.3.refs_4_), channel_id=1, source_target_pairs={{0,8},{8,0},{16,24},{24,16},{32,40},{40,32},{48,56},{56,48},{64,72... | collective-permute-start | bytes 1572872 | tf_op jit(solution)/shard_map/ppermute | solution.py:369
  89.9 0.4 collective-permute-done.20.refs_22_
  90.3 2.8 %collective-permute-start.5 = (bf16[8,16,2048]{2,1,0:T(8,128)(2,1)S(1)}, bf16[8,16,2048]{2,1,0:T(8,128)(2,1)S(1)}, u32[]{:S(2)}, u32[]{:S(2)}) collective-permute-start(bf16[8,16,2048]{2,1,0:T(8,128)(2,1)S(1)} %collective-permute-done.3.refs_4_), channel_id=1, source_target_pairs={{0,96},{1,97},{2,98},{3,99},{4,100},{5,101},{6,102},{7,103},{8,40}... | collective-permute-start | bytes 1572872 | tf_op jit(solution)/shard_map/ppermute | solution.py:364
  93.1 4.5 %collective-permute-done.17.refs_19_ = bf16[16,16,1024]{2,1,0:T(8,128)(2,1)S(1)} collective-permute-done((bf16[16,16,1024]{2,1,0:T(8,128)(2,1)S(1)}, bf16[16,16,1024]{2,1,0:T(8,128)(2,1)S(1)}, u32[]{:S(2)}, u32[]{:S(2)}) %collective-permute-start.17) | collective-permute-done | bytes 524320 | tf_op jit(solution)/shard_map/ppermute | solution.py:364
  97.6 0.5 collective-permute-start.8
  98.1 7.3 %collective-permute-done.2.refs_3_ = bf16[8,16,2048]{2,1,0:T(8,128)(2,1)S(1)} collective-permute-done((bf16[8,16,2048]{2,1,0:T(8,128)(2,1)S(1)}, bf16[8,16,2048]{2,1,0:T(8,128)(2,1)S(1)}, u32[]{:S(2)}, u32[]{:S(2)}) %collective-permute-start.2) | collective-permute-done | bytes 524320 | tf_op jit(solution)/shard_map/ppermute | solution.py:364
  105.3 0.7 collective-permute-start.6
  106.1 4.9 %collective-permute-done.4.refs_5_ = bf16[8,16,2048]{2,1,0:T(8,128)(2,1)S(1)} collective-permute-done((bf16[8,16,2048]{2,1,0:T(8,128)(2,1)S(1)}, bf16[8,16,2048]{2,1,0:T(8,128)(2,1)S(1)}, u32[]{:S(2)}, u32[]{:S(2)}) %collective-permute-start.4) | collective-permute-done | bytes 524320 | tf_op jit(solution)/shard_map/ppermute | solution.py:364
  111.0 0.5 collective-permute-start.13
  111.6 4.8 %collective-permute-done.6.refs_7_ = bf16[8,16,2048]{2,1,0:T(8,128)(2,1)S(1)} collective-permute-done((bf16[8,16,2048]{2,1,0:T(8,128)(2,1)S(1)}, bf16[8,16,2048]{2,1,0:T(8,128)(2,1)S(1)}, u32[]{:S(2)}, u32[]{:S(2)}) %collective-permute-start.6) | collective-permute-done | bytes 524320 | tf_op jit(solution)/shard_map/ppermute | solution.py:369
  116.3 0.1 collective-permute-done.21.refs_23_
  116.5 1.8 %collective-permute-done.14.refs_15_ = bf16[8,16,2048]{2,1,0:T(8,128)(2,1)S(1)} collective-permute-done((bf16[8,16,2048]{2,1,0:T(8,128)(2,1)S(1)}, bf16[8,16,2048]{2,1,0:T(8,128)(2,1)S(1)}, u32[]{:S(2)}, u32[]{:S(2)}) %collective-permute-start.14) | collective-permute-done | bytes 524320 | tf_op jit(solution)/shard_map/ppermute | solution.py:369
  118.2 11.0 %product.1 = f32[2048,1024]{1,0:T(8,128)} custom-call(bf16[8,16,2048]{2,1,0:T(8,128)(2,1)S(1)} %all-to-all-done.1.refs_0_, bf16[8,16,2048]{2,1,0:T(8,128)(2,1)S(1)} %collective-permute-done.refs_1_, bf16[8,16,2048]{2,1,0:T(8,128)(2,1)S(1)} %collective-permute-done.1.refs_2_, bf16[8,16,2048]{2,1,0:T(8,128)(2,1)S(1)} %collective-permute-done.2.refs_3_, ...), custom_call_target="tpu_custom_call" | custom-call | tf_op jit(solution)/shard_map/product/pallas_call | solution.py:337
  (25 shorter events, 0.2 us)
Async XLA Ops:
  48.6 23.9 %collective-permute-start.18 = (bf16[16,16,1024]{2,1,0:T(8,128)(2,1)S(1)}, bf16[16,16,1024]{2,1,0:T(8,128)(2,1)S(1)}, u32[]{:S(2)}, u32[]{:S(2)}) collective-permute-start(bf16[16,16,1024]{2,1,0:T(8,128)(2,1)S(1)} %all_to_all.10.refs_16_), channel_id=1, source_target_pairs={{0,4},{1,5},{2,6},{3,7},{4,0},{5,1},{6,2},{7,3},{8,12},{9,13},{10,... | collective-permute-start | bytes 1572872 | tf_op jit(solution)/shard_map/ppermute | solution.py:369
  52.2 21.0 %collective-permute-start.16 = (bf16[16,16,1024]{2,1,0:T(8,128)(2,1)S(1)}, bf16[16,16,1024]{2,1,0:T(8,128)(2,1)S(1)}, u32[]{:S(2)}, u32[]{:S(2)}) collective-permute-start(bf16[16,16,1024]{2,1,0:T(8,128)(2,1)S(1)} %all_to_all.10.refs_16_), channel_id=1, source_target_pairs={{0,3},{1,0},{2,1},{3,2},{4,7},{5,4},{6,5},{7,6},{8,9},{9,10},{10,1... | collective-permute-start | bytes 1572872 | tf_op jit(solution)/shard_map/ppermute | solution.py:364
  55.0 17.5 %all-to-all-start.1 = ((bf16[8,16,2048]{2,1,0:T(8,128)(2,1)}), bf16[8,16,2048]{2,1,0:T(8,128)(2,1)S(1)}, u32[]{:S(2)}, u32[]{:S(2)}) async-start(bf16[8,16,2048]{2,1,0:T(8,128)(2,1)} %get-tuple-element.11), calls=%async_computation.1 | async-start | bytes 1048576 | tf_op jit(solution)/shard_map/all_to_all | solution.py:399
  58.5 16.1 %collective-permute-start.15 = (bf16[16,16,1024]{2,1,0:T(8,128)(2,1)S(1)}, bf16[16,16,1024]{2,1,0:T(8,128)(2,1)S(1)}, u32[]{:S(2)}, u32[]{:S(2)}) collective-permute-start(bf16[16,16,1024]{2,1,0:T(8,128)(2,1)S(1)} %all_to_all.10.refs_16_), channel_id=1, source_target_pairs={{0,1},{1,2},{2,3},{3,0},{4,5},{5,6},{6,7},{7,4},{8,11},{9,8},{10,9... | collective-permute-start | bytes 1572872 | tf_op jit(solution)/shard_map/ppermute | solution.py:364
  72.5 5.7 %collective-permute-start.7 = (bf16[8,16,2048]{2,1,0:T(8,128)(2,1)S(1)}, bf16[8,16,2048]{2,1,0:T(8,128)(2,1)S(1)}, u32[]{:S(2)}, u32[]{:S(2)}) collective-permute-start(bf16[8,16,2048]{2,1,0:T(8,128)(2,1)S(1)} %all-to-all-done.1.refs_0_), channel_id=1, source_target_pairs={{0,8},{8,0},{16,24},{24,16},{32,40},{40,32},{48,56},{56,48},{64,72... | collective-permute-start | bytes 1572872 | tf_op jit(solution)/shard_map/ppermute | solution.py:369
  72.5 14.3 %collective-permute-start.3 = (bf16[8,16,2048]{2,1,0:T(8,128)(2,1)S(1)}, bf16[8,16,2048]{2,1,0:T(8,128)(2,1)S(1)}, u32[]{:S(2)}, u32[]{:S(2)}) collective-permute-start(bf16[8,16,2048]{2,1,0:T(8,128)(2,1)S(1)} %all-to-all-done.1.refs_0_), channel_id=1, source_target_pairs={{0,16},{8,24},{16,0},{24,8},{32,48},{40,56},{48,32},{56,40},{64,80... | collective-permute-start | bytes 1572872 | tf_op jit(solution)/shard_map/ppermute | solution.py:369
  72.5 14.4 %collective-permute-start.1 = (bf16[8,16,2048]{2,1,0:T(8,128)(2,1)S(1)}, bf16[8,16,2048]{2,1,0:T(8,128)(2,1)S(1)}, u32[]{:S(2)}, u32[]{:S(2)}) collective-permute-start(bf16[8,16,2048]{2,1,0:T(8,128)(2,1)S(1)} %all-to-all-done.1.refs_0_), channel_id=1, source_target_pairs={{0,96},{1,97},{2,98},{3,99},{4,100},{5,101},{6,102},{7,103},{8,40}... | collective-permute-start | bytes 1572872 | tf_op jit(solution)/shard_map/ppermute | solution.py:364
  73.2 16.7 %collective-permute-start = (bf16[8,16,2048]{2,1,0:T(8,128)(2,1)S(1)}, bf16[8,16,2048]{2,1,0:T(8,128)(2,1)S(1)}, u32[]{:S(2)}, u32[]{:S(2)}) collective-permute-start(bf16[8,16,2048]{2,1,0:T(8,128)(2,1)S(1)} %all-to-all-done.1.refs_0_), channel_id=1, source_target_pairs={{0,32},{1,33},{2,34},{3,35},{4,36},{5,37},{6,38},{7,39},{8,104},{9... | collective-permute-start | bytes 1572872 | tf_op jit(solution)/shard_map/ppermute | solution.py:364
  74.6 15.7 %collective-permute-start.20 = (bf16[16,16,1024]{2,1,0:T(8,128)(2,1)S(1)}, bf16[16,16,1024]{2,1,0:T(8,128)(2,1)S(1)}, u32[]{:S(2)}, u32[]{:S(2)}) collective-permute-start(bf16[16,16,1024]{2,1,0:T(8,128)(2,1)S(1)} %collective-permute-done.18.refs_20_), channel_id=1, source_target_pairs={{0,3},{1,0},{2,1},{3,2},{4,7},{5,4},{6,5},{7,6},{8,9},{9,10},{10,1... | collective-permute-start | bytes 1572872 | tf_op jit(solution)/shard_map/ppermute | solution.py:364
  78.2 14.9 %collective-permute-start.19 = (bf16[16,16,1024]{2,1,0:T(8,128)(2,1)S(1)}, bf16[16,16,1024]{2,1,0:T(8,128)(2,1)S(1)}, u32[]{:S(2)}, u32[]{:S(2)}) collective-permute-start(bf16[16,16,1024]{2,1,0:T(8,128)(2,1)S(1)} %collective-permute-done.18.refs_20_), channel_id=1, source_target_pairs={{0,1},{1,2},{2,3},{3,0},{4,5},{5,6},{6,7},{7,4},{8,11},{9,8},{10,9... | collective-permute-start | bytes 1572872 | tf_op jit(solution)/shard_map/ppermute | solution.py:364
  86.8 10.7 %collective-permute-start.17 = (bf16[16,16,1024]{2,1,0:T(8,128)(2,1)S(1)}, bf16[16,16,1024]{2,1,0:T(8,128)(2,1)S(1)}, u32[]{:S(2)}, u32[]{:S(2)}) collective-permute-start(bf16[16,16,1024]{2,1,0:T(8,128)(2,1)S(1)} %collective-permute-done.15.refs_17_), channel_id=1, source_target_pairs={{0,1},{1,2},{2,3},{3,0},{4,5},{5,6},{6,7},{7,4},{8,11},{9,8},{10,9... | collective-permute-start | bytes 1572872 | tf_op jit(solution)/shard_map/ppermute | solution.py:364
  86.9 10.7 %collective-permute-start.11 = (bf16[8,16,2048]{2,1,0:T(8,128)(2,1)S(1)}, bf16[8,16,2048]{2,1,0:T(8,128)(2,1)S(1)}, u32[]{:S(2)}, u32[]{:S(2)}) collective-permute-start(bf16[8,16,2048]{2,1,0:T(8,128)(2,1)S(1)} %collective-permute-done.3.refs_4_), channel_id=1, source_target_pairs={{0,8},{8,0},{16,24},{24,16},{32,40},{40,32},{48,56},{56,48},{64,72... | collective-permute-start | bytes 1572872 | tf_op jit(solution)/shard_map/ppermute | solution.py:369
  89.9 15.5 %collective-permute-start.2 = (bf16[8,16,2048]{2,1,0:T(8,128)(2,1)S(1)}, bf16[8,16,2048]{2,1,0:T(8,128)(2,1)S(1)}, u32[]{:S(2)}, u32[]{:S(2)}) collective-permute-start(bf16[8,16,2048]{2,1,0:T(8,128)(2,1)S(1)} %collective-permute-done.refs_1_), channel_id=1, source_target_pairs={{0,32},{1,33},{2,34},{3,35},{4,36},{5,37},{6,38},{7,39},{8,104},{9... | collective-permute-start | bytes 1572872 | tf_op jit(solution)/shard_map/ppermute | solution.py:364
  90.3 15.7 %collective-permute-start.5 = (bf16[8,16,2048]{2,1,0:T(8,128)(2,1)S(1)}, bf16[8,16,2048]{2,1,0:T(8,128)(2,1)S(1)}, u32[]{:S(2)}, u32[]{:S(2)}) collective-permute-start(bf16[8,16,2048]{2,1,0:T(8,128)(2,1)S(1)} %collective-permute-done.3.refs_4_), channel_id=1, source_target_pairs={{0,96},{1,97},{2,98},{3,99},{4,100},{5,101},{6,102},{7,103},{8,40}... | collective-permute-start | bytes 1572872 | tf_op jit(solution)/shard_map/ppermute | solution.py:364
  93.1 17.9 %collective-permute-start.4 = (bf16[8,16,2048]{2,1,0:T(8,128)(2,1)S(1)}, bf16[8,16,2048]{2,1,0:T(8,128)(2,1)S(1)}, u32[]{:S(2)}, u32[]{:S(2)}) collective-permute-start(bf16[8,16,2048]{2,1,0:T(8,128)(2,1)S(1)} %collective-permute-done.3.refs_4_), channel_id=1, source_target_pairs={{0,32},{1,33},{2,34},{3,35},{4,36},{5,37},{6,38},{7,39},{8,104},{9... | collective-permute-start | bytes 1572872 | tf_op jit(solution)/shard_map/ppermute | solution.py:364
  97.6 13.4 %collective-permute-start.9 = (bf16[8,16,2048]{2,1,0:T(8,128)(2,1)S(1)}, bf16[8,16,2048]{2,1,0:T(8,128)(2,1)S(1)}, u32[]{:S(2)}, u32[]{:S(2)}) collective-permute-start(bf16[8,16,2048]{2,1,0:T(8,128)(2,1)S(1)} %collective-permute-done.1.refs_2_), channel_id=1, source_target_pairs={{0,8},{8,0},{16,24},{24,16},{32,40},{40,32},{48,56},{56,48},{64,72... | collective-permute-start | bytes 1572872 | tf_op jit(solution)/shard_map/ppermute | solution.py:369
  97.6 13.9 %collective-permute-start.8 = (bf16[8,16,2048]{2,1,0:T(8,128)(2,1)S(1)}, bf16[8,16,2048]{2,1,0:T(8,128)(2,1)S(1)}, u32[]{:S(2)}, u32[]{:S(2)}) collective-permute-start(bf16[8,16,2048]{2,1,0:T(8,128)(2,1)S(1)} %collective-permute-done.refs_1_), channel_id=1, source_target_pairs={{0,8},{8,0},{16,24},{24,16},{32,40},{40,32},{48,56},{56,48},{64,72... | collective-permute-start | bytes 1572872 | tf_op jit(solution)/shard_map/ppermute | solution.py:369
  105.3 11.0 %collective-permute-start.6 = (bf16[8,16,2048]{2,1,0:T(8,128)(2,1)S(1)}, bf16[8,16,2048]{2,1,0:T(8,128)(2,1)S(1)}, u32[]{:S(2)}, u32[]{:S(2)}) collective-permute-start(bf16[8,16,2048]{2,1,0:T(8,128)(2,1)S(1)} %collective-permute-done.2.refs_3_), channel_id=1, source_target_pairs={{0,16},{8,24},{16,0},{24,8},{32,48},{40,56},{48,32},{56,40},{64,80... | collective-permute-start | bytes 1572872 | tf_op jit(solution)/shard_map/ppermute | solution.py:369
  106.1 10.4 %collective-permute-start.21 = (bf16[16,16,1024]{2,1,0:T(8,128)(2,1)S(1)}, bf16[16,16,1024]{2,1,0:T(8,128)(2,1)S(1)}, u32[]{:S(2)}, u32[]{:S(2)}) collective-permute-start(bf16[16,16,1024]{2,1,0:T(8,128)(2,1)S(1)} %collective-permute-done.19.refs_21_), channel_id=1, source_target_pairs={{0,1},{1,2},{2,3},{3,0},{4,5},{5,6},{6,7},{7,4},{8,11},{9,8},{10,9... | collective-permute-start | bytes 1572872 | tf_op jit(solution)/shard_map/ppermute | solution.py:364
  111.0 5.5 %collective-permute-start.10 = (bf16[8,16,2048]{2,1,0:T(8,128)(2,1)S(1)}, bf16[8,16,2048]{2,1,0:T(8,128)(2,1)S(1)}, u32[]{:S(2)}, u32[]{:S(2)}) collective-permute-start(bf16[8,16,2048]{2,1,0:T(8,128)(2,1)S(1)} %collective-permute-done.2.refs_3_), channel_id=1, source_target_pairs={{0,8},{8,0},{16,24},{24,16},{32,40},{40,32},{48,56},{56,48},{64,72... | collective-permute-start | bytes 1572872 | tf_op jit(solution)/shard_map/ppermute | solution.py:369
  111.0 5.5 %collective-permute-start.13 = (bf16[8,16,2048]{2,1,0:T(8,128)(2,1)S(1)}, bf16[8,16,2048]{2,1,0:T(8,128)(2,1)S(1)}, u32[]{:S(2)}, u32[]{:S(2)}) collective-permute-start(bf16[8,16,2048]{2,1,0:T(8,128)(2,1)S(1)} %collective-permute-done.5.refs_6_), channel_id=1, source_target_pairs={{0,8},{8,0},{16,24},{24,16},{32,40},{40,32},{48,56},{56,48},{64,72... | collective-permute-start | bytes 1572872 | tf_op jit(solution)/shard_map/ppermute | solution.py:369
  111.5 5.0 %collective-permute-start.12 = (bf16[8,16,2048]{2,1,0:T(8,128)(2,1)S(1)}, bf16[8,16,2048]{2,1,0:T(8,128)(2,1)S(1)}, u32[]{:S(2)}, u32[]{:S(2)}) collective-permute-start(bf16[8,16,2048]{2,1,0:T(8,128)(2,1)S(1)} %collective-permute-done.4.refs_5_), channel_id=1, source_target_pairs={{0,8},{8,0},{16,24},{24,16},{32,40},{40,32},{48,56},{56,48},{64,72... | collective-permute-start | bytes 1572872 | tf_op jit(solution)/shard_map/ppermute | solution.py:369
  116.3 1.9 %collective-permute-start.14 = (bf16[8,16,2048]{2,1,0:T(8,128)(2,1)S(1)}, bf16[8,16,2048]{2,1,0:T(8,128)(2,1)S(1)}, u32[]{:S(2)}, u32[]{:S(2)}) collective-permute-start(bf16[8,16,2048]{2,1,0:T(8,128)(2,1)S(1)} %collective-permute-done.6.refs_7_), channel_id=1, source_target_pairs={{0,8},{8,0},{16,24},{24,16},{32,40},{40,32},{48,56},{56,48},{64,72... | collective-permute-start | bytes 1572872 | tf_op jit(solution)/shard_map/ppermute | solution.py:369

commit v8 on v7

--- a/solution.py
+++ b/solution.py
@@ -28,7 +28,7 @@
     table = np.concatenate([np.cos(angle), -np.sin(angle)], axis=0)
     table[HALF] = 1.0 - 2.0 * (x % 2)
     high, low = two_terms(table)
-    return np.concatenate([high, high, low], axis=1)
+    return np.block([[high, high], [low, np.zeros_like(low)]]).astype(BF)
 
 
 def z_table():
@@ -175,9 +175,10 @@
             high, low = split(product)
             spectrum = jnp.dot(
                 x_factors[...],
-                jnp.concatenate([high, low, high], axis=0),
+                jnp.concatenate([high, low], axis=0),
                 preferred_element_type=F32,
             )
+            spectrum = spectrum[:EDGE] + spectrum[EDGE:]
             for h in range(2):
                 staged[2 * chunk + h, pl.ds(p, EDGE, stride=8), :] = spectrum[:, h * LANES : (h + 1) * LANES]
         return carry
@@ -394,9 +395,9 @@
     )
     right = lax.all_to_all(right, "col", split_axis=0, concat_axis=0, tiled=True)
     right, left = lax.optimization_barrier((right, left))
+    left = lax.all_to_all(left, "row", split_axis=0, concat_axis=0, tiled=True)
     right_z = swap(right, "row", RING)
     rights = [right, shift(right, "row", 1, 1), shift(right, "row", 1, -1)]
-    left = lax.all_to_all(left, "row", split_axis=0, concat_axis=0, tiled=True)
     left_z = swap(left, "col", 2)
     lefts = [left, shift(left, "col", RING, 1), shift(left, "col", RING, -1)]
     rights += [shift(rights[1], "row", 1, 1), right_z, shift(right_z, "row", 1, 1), shift(right_z, "row", 1, -1)]

time: 131 us -> 130 us (level)
  no operation moved by 1% of the time
where the time goes in v8:
time: 130 us; the launch traced here: 129 us
  waiting for transfers between devices  44.6 us (34%)
  Pallas kernels  42.4 us (33%)
  starting transfers between devices  25 us (19%)
  blocking collectives  16.9 us (13%)
    pallas_call x1, Pallas kernels, densities(): pl.pallas_call(lambda *refs: density_kernel(n_pairs * n_row * n_col, *ref...  31.5 us
    ppermute x11, waiting for transfers between devices, shift(): return lax.ppermute(value, ('col', 'row'), pairs)  17.3 us
    all_to_all x1, blocking collectives, per_device(): lax.all_to_all(right, 'col', split_axis=0, concat_axis=0, tiled=True)  16.9 us
    ppermute x11, waiting for transfers between devices, swap(): return lax.ppermute(value, axis, [(i, i ^ bit) for i in range(count)])  15.2 us
    ppermute x11, starting transfers between devices, shift(): return lax.ppermute(value, ('col', 'row'), pairs)  13.2 us
    all_to_all x1, waiting for transfers between devices, per_device(): left = lax.all_to_all(left, 'row', split_axis=0, concat_axis=0, tiled=True)  12.1 us
    pallas_call x1, Pallas kernels, product(): pl.pallas_call(lambda *refs: product_kernel(n_left, n_right, *refs), grid...  11 us
    ppermute x11, starting transfers between devices, swap(): return lax.ppermute(value, axis, [(i, i ^ bit) for i in range(count)])  8.33 us
  transfers between devices with their start and end apart: 23, of which 10 were waited for; matrix products, arithmetic and copies ran while one was open for 0% of the time, Pallas kernels for 0%

profile of v8, /device:TPU:0, one launch (start us, length us, event | category | flops | bytes accessed | tf_op | source)
XLA Modules:
  0.0 128.9 jit_solution(129909131836975294)
XLA Ops:
  0.0 31.5 %density.1 = (bf16[8,16,2048]{2,1,0:T(8,128)(2,1)}, bf16[16,16,1024]{2,1,0:T(8,128)(2,1)}) custom-call(f32[4,64,4096]{2,1,0:T(8,128)} %refs_0_.1, f32[4,64,4096]{2,1,0:T(8,128)} %refs_1_.1, f32[4]{0:T(128)} %refs_2_.1, f32[4]{0:T(128)} %refs_3_.1, s32[2,8]{1,0:T(2,128)} %bitcast.3, s32[128,128]{1,0:T(8,128)} %bitcast.2, ...), custom_call_target="tpu_custom_call" | custom-call | tf_op jit(solution)/shard_map/density/pallas_call | solution.py:280
  31.5 16.9 %all_to_all.10.refs_16_ = bf16[16,16,1024]{2,1,0:T(8,128)(2,1)S(1)} all-to-all(bf16[16,16,1024]{2,1,0:T(8,128)(2,1)} %get-tuple-element.9), channel_id=1, replica_groups=mesh['col'=16,'row'=8] {'col'}, dimensions={0} | all-to-all | bytes 1048576 | tf_op jit(solution)/shard_map/all_to_all | solution.py:396
  48.4 3.6 %collective-permute-start.18 = (bf16[16,16,1024]{2,1,0:T(8,128)(2,1)S(1)}, bf16[16,16,1024]{2,1,0:T(8,128)(2,1)S(1)}, u32[]{:S(2)}, u32[]{:S(2)}) collective-permute-start(bf16[16,16,1024]{2,1,0:T(8,128)(2,1)S(1)} %all_to_all.10.refs_16_), channel_id=1, source_target_pairs={{0,4},{1,5},{2,6},{3,7},{4,0},{5,1},{6,2},{7,3},{8,12},{9,13},{10,... | collective-permute-start | bytes 1572872 | tf_op jit(solution)/shard_map/ppermute | solution.py:370
  51.9 2.8 %collective-permute-start.16 = (bf16[16,16,1024]{2,1,0:T(8,128)(2,1)S(1)}, bf16[16,16,1024]{2,1,0:T(8,128)(2,1)S(1)}, u32[]{:S(2)}, u32[]{:S(2)}) collective-permute-start(bf16[16,16,1024]{2,1,0:T(8,128)(2,1)S(1)} %all_to_all.10.refs_16_), channel_id=1, source_target_pairs={{0,3},{1,0},{2,1},{3,2},{4,7},{5,4},{6,5},{7,6},{8,9},{9,10},{10,1... | collective-permute-start | bytes 1572872 | tf_op jit(solution)/shard_map/ppermute | solution.py:365
  54.7 3.5 %all-to-all-start.1 = ((bf16[8,16,2048]{2,1,0:T(8,128)(2,1)}), bf16[8,16,2048]{2,1,0:T(8,128)(2,1)S(1)}, u32[]{:S(2)}, u32[]{:S(2)}) async-start(bf16[8,16,2048]{2,1,0:T(8,128)(2,1)} %get-tuple-element.11), calls=%async_computation.1 | async-start | bytes 1048576 | tf_op jit(solution)/shard_map/all_to_all | solution.py:398
  58.2 1.9 %collective-permute-start.15 = (bf16[16,16,1024]{2,1,0:T(8,128)(2,1)S(1)}, bf16[16,16,1024]{2,1,0:T(8,128)(2,1)S(1)}, u32[]{:S(2)}, u32[]{:S(2)}) collective-permute-start(bf16[16,16,1024]{2,1,0:T(8,128)(2,1)S(1)} %all_to_all.10.refs_16_), channel_id=1, source_target_pairs={{0,1},{1,2},{2,3},{3,0},{4,5},{5,6},{6,7},{7,4},{8,11},{9,8},{10,9... | collective-permute-start | bytes 1572872 | tf_op jit(solution)/shard_map/ppermute | solution.py:365
  60.1 12.1 %all-to-all-done.1.refs_0_ = bf16[8,16,2048]{2,1,0:T(8,128)(2,1)S(1)} async-done(((bf16[8,16,2048]{2,1,0:T(8,128)(2,1)}), bf16[8,16,2048]{2,1,0:T(8,128)(2,1)S(1)}, u32[]{:S(2)}, u32[]{:S(2)}) %all-to-all-start.1) | async-done | bytes 524320 | tf_op jit(solution)/shard_map/all_to_all | solution.py:398
  72.2 0.7 collective-permute-start.1
  73.0 1.4 %collective-permute-start = (bf16[8,16,2048]{2,1,0:T(8,128)(2,1)S(1)}, bf16[8,16,2048]{2,1,0:T(8,128)(2,1)S(1)}, u32[]{:S(2)}, u32[]{:S(2)}) collective-permute-start(bf16[8,16,2048]{2,1,0:T(8,128)(2,1)S(1)} %all-to-all-done.1.refs_0_), channel_id=1, source_target_pairs={{0,32},{1,33},{2,34},{3,35},{4,36},{5,37},{6,38},{7,39},{8,104},{9... | collective-permute-start | bytes 1572872 | tf_op jit(solution)/shard_map/ppermute | solution.py:365
  74.4 3.6 %collective-permute-start.20 = (bf16[16,16,1024]{2,1,0:T(8,128)(2,1)S(1)}, bf16[16,16,1024]{2,1,0:T(8,128)(2,1)S(1)}, u32[]{:S(2)}, u32[]{:S(2)}) collective-permute-start(bf16[16,16,1024]{2,1,0:T(8,128)(2,1)S(1)} %collective-permute-done.18.refs_20_), channel_id=1, source_target_pairs={{0,3},{1,0},{2,1},{3,2},{4,7},{5,4},{6,5},{7,6},{8,9},{9,10},{10,1... | collective-permute-start | bytes 1572872 | tf_op jit(solution)/shard_map/ppermute | solution.py:365
  77.9 8.6 %collective-permute-done.3.refs_4_ = bf16[8,16,2048]{2,1,0:T(8,128)(2,1)S(1)} collective-permute-done((bf16[8,16,2048]{2,1,0:T(8,128)(2,1)S(1)}, bf16[8,16,2048]{2,1,0:T(8,128)(2,1)S(1)}, u32[]{:S(2)}, u32[]{:S(2)}) %collective-permute-start.3) | collective-permute-done | bytes 524320 | tf_op jit(solution)/shard_map/ppermute | solution.py:370
  86.7 2.9 %collective-permute-start.11 = (bf16[8,16,2048]{2,1,0:T(8,128)(2,1)S(1)}, bf16[8,16,2048]{2,1,0:T(8,128)(2,1)S(1)}, u32[]{:S(2)}, u32[]{:S(2)}) collective-permute-start(bf16[8,16,2048]{2,1,0:T(8,128)(2,1)S(1)} %collective-permute-done.3.refs_4_), channel_id=1, source_target_pairs={{0,8},{8,0},{16,24},{24,16},{32,40},{40,32},{48,56},{56,48},{64,72... | collective-permute-start | bytes 1572872 | tf_op jit(solution)/shard_map/ppermute | solution.py:370
  89.6 0.4 collective-permute-done.20.refs_22_
  90.1 2.8 %collective-permute-start.5 = (bf16[8,16,2048]{2,1,0:T(8,128)(2,1)S(1)}, bf16[8,16,2048]{2,1,0:T(8,128)(2,1)S(1)}, u32[]{:S(2)}, u32[]{:S(2)}) collective-permute-start(bf16[8,16,2048]{2,1,0:T(8,128)(2,1)S(1)} %collective-permute-done.3.refs_4_), channel_id=1, source_target_pairs={{0,96},{1,97},{2,98},{3,99},{4,100},{5,101},{6,102},{7,103},{8,40}... | collective-permute-start | bytes 1572872 | tf_op jit(solution)/shard_map/ppermute | solution.py:365
  92.9 4.5 %collective-permute-done.17.refs_19_ = bf16[16,16,1024]{2,1,0:T(8,128)(2,1)S(1)} collective-permute-done((bf16[16,16,1024]{2,1,0:T(8,128)(2,1)S(1)}, bf16[16,16,1024]{2,1,0:T(8,128)(2,1)S(1)}, u32[]{:S(2)}, u32[]{:S(2)}) %collective-permute-start.17) | collective-permute-done | bytes 524320 | tf_op jit(solution)/shard_map/ppermute | solution.py:365
  97.3 0.5 collective-permute-start.8
  97.8 7.3 %collective-permute-done.2.refs_3_ = bf16[8,16,2048]{2,1,0:T(8,128)(2,1)S(1)} collective-permute-done((bf16[8,16,2048]{2,1,0:T(8,128)(2,1)S(1)}, bf16[8,16,2048]{2,1,0:T(8,128)(2,1)S(1)}, u32[]{:S(2)}, u32[]{:S(2)}) %collective-permute-start.2) | collective-permute-done | bytes 524320 | tf_op jit(solution)/shard_map/ppermute | solution.py:365
  105.1 0.7 collective-permute-start.6
  105.8 4.9 %collective-permute-done.4.refs_5_ = bf16[8,16,2048]{2,1,0:T(8,128)(2,1)S(1)} collective-permute-done((bf16[8,16,2048]{2,1,0:T(8,128)(2,1)S(1)}, bf16[8,16,2048]{2,1,0:T(8,128)(2,1)S(1)}, u32[]{:S(2)}, u32[]{:S(2)}) %collective-permute-start.4) | collective-permute-done | bytes 524320 | tf_op jit(solution)/shard_map/ppermute | solution.py:365
  110.7 0.5 collective-permute-start.13
  111.3 4.8 %collective-permute-done.6.refs_7_ = bf16[8,16,2048]{2,1,0:T(8,128)(2,1)S(1)} collective-permute-done((bf16[8,16,2048]{2,1,0:T(8,128)(2,1)S(1)}, bf16[8,16,2048]{2,1,0:T(8,128)(2,1)S(1)}, u32[]{:S(2)}, u32[]{:S(2)}) %collective-permute-start.6) | collective-permute-done | bytes 524320 | tf_op jit(solution)/shard_map/ppermute | solution.py:370
  116.1 0.1 collective-permute-done.21.refs_23_
  116.2 1.8 %collective-permute-done.14.refs_15_ = bf16[8,16,2048]{2,1,0:T(8,128)(2,1)S(1)} collective-permute-done((bf16[8,16,2048]{2,1,0:T(8,128)(2,1)S(1)}, bf16[8,16,2048]{2,1,0:T(8,128)(2,1)S(1)}, u32[]{:S(2)}, u32[]{:S(2)}) %collective-permute-start.14) | collective-permute-done | bytes 524320 | tf_op jit(solution)/shard_map/ppermute | solution.py:370
  118.0 11.0 %product.1 = f32[2048,1024]{1,0:T(8,128)} custom-call(bf16[8,16,2048]{2,1,0:T(8,128)(2,1)S(1)} %all-to-all-done.1.refs_0_, bf16[8,16,2048]{2,1,0:T(8,128)(2,1)S(1)} %collective-permute-done.refs_1_, bf16[8,16,2048]{2,1,0:T(8,128)(2,1)S(1)} %collective-permute-done.1.refs_2_, bf16[8,16,2048]{2,1,0:T(8,128)(2,1)S(1)} %collective-permute-done.2.refs_3_, ...), custom_call_target="tpu_custom_call" | custom-call | tf_op jit(solution)/shard_map/product/pallas_call | solution.py:338
  (25 shorter events, 0.2 us)
Async XLA Ops:
  48.4 23.9 %collective-permute-start.18 = (bf16[16,16,1024]{2,1,0:T(8,128)(2,1)S(1)}, bf16[16,16,1024]{2,1,0:T(8,128)(2,1)S(1)}, u32[]{:S(2)}, u32[]{:S(2)}) collective-permute-start(bf16[16,16,1024]{2,1,0:T(8,128)(2,1)S(1)} %all_to_all.10.refs_16_), channel_id=1, source_target_pairs={{0,4},{1,5},{2,6},{3,7},{4,0},{5,1},{6,2},{7,3},{8,12},{9,13},{10,... | collective-permute-start | bytes 1572872 | tf_op jit(solution)/shard_map/ppermute | solution.py:370
  51.9 21.0 %collective-permute-start.16 = (bf16[16,16,1024]{2,1,0:T(8,128)(2,1)S(1)}, bf16[16,16,1024]{2,1,0:T(8,128)(2,1)S(1)}, u32[]{:S(2)}, u32[]{:S(2)}) collective-permute-start(bf16[16,16,1024]{2,1,0:T(8,128)(2,1)S(1)} %all_to_all.10.refs_16_), channel_id=1, source_target_pairs={{0,3},{1,0},{2,1},{3,2},{4,7},{5,4},{6,5},{7,6},{8,9},{9,10},{10,1... | collective-permute-start | bytes 1572872 | tf_op jit(solution)/shard_map/ppermute | solution.py:365
  54.7 17.5 %all-to-all-start.1 = ((bf16[8,16,2048]{2,1,0:T(8,128)(2,1)}), bf16[8,16,2048]{2,1,0:T(8,128)(2,1)S(1)}, u32[]{:S(2)}, u32[]{:S(2)}) async-start(bf16[8,16,2048]{2,1,0:T(8,128)(2,1)} %get-tuple-element.11), calls=%async_computation.1 | async-start | bytes 1048576 | tf_op jit(solution)/shard_map/all_to_all | solution.py:398
  58.2 16.1 %collective-permute-start.15 = (bf16[16,16,1024]{2,1,0:T(8,128)(2,1)S(1)}, bf16[16,16,1024]{2,1,0:T(8,128)(2,1)S(1)}, u32[]{:S(2)}, u32[]{:S(2)}) collective-permute-start(bf16[16,16,1024]{2,1,0:T(8,128)(2,1)S(1)} %all_to_all.10.refs_16_), channel_id=1, source_target_pairs={{0,1},{1,2},{2,3},{3,0},{4,5},{5,6},{6,7},{7,4},{8,11},{9,8},{10,9... | collective-permute-start | bytes 1572872 | tf_op jit(solution)/shard_map/ppermute | solution.py:365
  72.2 5.7 %collective-permute-start.7 = (bf16[8,16,2048]{2,1,0:T(8,128)(2,1)S(1)}, bf16[8,16,2048]{2,1,0:T(8,128)(2,1)S(1)}, u32[]{:S(2)}, u32[]{:S(2)}) collective-permute-start(bf16[8,16,2048]{2,1,0:T(8,128)(2,1)S(1)} %all-to-all-done.1.refs_0_), channel_id=1, source_target_pairs={{0,8},{8,0},{16,24},{24,16},{32,40},{40,32},{48,56},{56,48},{64,72... | collective-permute-start | bytes 1572872 | tf_op jit(solution)/shard_map/ppermute | solution.py:370
  72.2 14.3 %collective-permute-start.3 = (bf16[8,16,2048]{2,1,0:T(8,128)(2,1)S(1)}, bf16[8,16,2048]{2,1,0:T(8,128)(2,1)S(1)}, u32[]{:S(2)}, u32[]{:S(2)}) collective-permute-start(bf16[8,16,2048]{2,1,0:T(8,128)(2,1)S(1)} %all-to-all-done.1.refs_0_), channel_id=1, source_target_pairs={{0,16},{8,24},{16,0},{24,8},{32,48},{40,56},{48,32},{56,40},{64,80... | collective-permute-start | bytes 1572872 | tf_op jit(solution)/shard_map/ppermute | solution.py:370
  72.2 14.4 %collective-permute-start.1 = (bf16[8,16,2048]{2,1,0:T(8,128)(2,1)S(1)}, bf16[8,16,2048]{2,1,0:T(8,128)(2,1)S(1)}, u32[]{:S(2)}, u32[]{:S(2)}) collective-permute-start(bf16[8,16,2048]{2,1,0:T(8,128)(2,1)S(1)} %all-to-all-done.1.refs_0_), channel_id=1, source_target_pairs={{0,96},{1,97},{2,98},{3,99},{4,100},{5,101},{6,102},{7,103},{8,40}... | collective-permute-start | bytes 1572872 | tf_op jit(solution)/shard_map/ppermute | solution.py:365
  73.0 16.7 %collective-permute-start = (bf16[8,16,2048]{2,1,0:T(8,128)(2,1)S(1)}, bf16[8,16,2048]{2,1,0:T(8,128)(2,1)S(1)}, u32[]{:S(2)}, u32[]{:S(2)}) collective-permute-start(bf16[8,16,2048]{2,1,0:T(8,128)(2,1)S(1)} %all-to-all-done.1.refs_0_), channel_id=1, source_target_pairs={{0,32},{1,33},{2,34},{3,35},{4,36},{5,37},{6,38},{7,39},{8,104},{9... | collective-permute-start | bytes 1572872 | tf_op jit(solution)/shard_map/ppermute | solution.py:365
  74.4 15.7 %collective-permute-start.20 = (bf16[16,16,1024]{2,1,0:T(8,128)(2,1)S(1)}, bf16[16,16,1024]{2,1,0:T(8,128)(2,1)S(1)}, u32[]{:S(2)}, u32[]{:S(2)}) collective-permute-start(bf16[16,16,1024]{2,1,0:T(8,128)(2,1)S(1)} %collective-permute-done.18.refs_20_), channel_id=1, source_target_pairs={{0,3},{1,0},{2,1},{3,2},{4,7},{5,4},{6,5},{7,6},{8,9},{9,10},{10,1... | collective-permute-start | bytes 1572872 | tf_op jit(solution)/shard_map/ppermute | solution.py:365
  77.9 14.9 %collective-permute-start.19 = (bf16[16,16,1024]{2,1,0:T(8,128)(2,1)S(1)}, bf16[16,16,1024]{2,1,0:T(8,128)(2,1)S(1)}, u32[]{:S(2)}, u32[]{:S(2)}) collective-permute-start(bf16[16,16,1024]{2,1,0:T(8,128)(2,1)S(1)} %collective-permute-done.18.refs_20_), channel_id=1, source_target_pairs={{0,1},{1,2},{2,3},{3,0},{4,5},{5,6},{6,7},{7,4},{8,11},{9,8},{10,9... | collective-permute-start | bytes 1572872 | tf_op jit(solution)/shard_map/ppermute | solution.py:365
  86.6 10.7 %collective-permute-start.17 = (bf16[16,16,1024]{2,1,0:T(8,128)(2,1)S(1)}, bf16[16,16,1024]{2,1,0:T(8,128)(2,1)S(1)}, u32[]{:S(2)}, u32[]{:S(2)}) collective-permute-start(bf16[16,16,1024]{2,1,0:T(8,128)(2,1)S(1)} %collective-permute-done.15.refs_17_), channel_id=1, source_target_pairs={{0,1},{1,2},{2,3},{3,0},{4,5},{5,6},{6,7},{7,4},{8,11},{9,8},{10,9... | collective-permute-start | bytes 1572872 | tf_op jit(solution)/shard_map/ppermute | solution.py:365
  86.7 10.7 %collective-permute-start.11 = (bf16[8,16,2048]{2,1,0:T(8,128)(2,1)S(1)}, bf16[8,16,2048]{2,1,0:T(8,128)(2,1)S(1)}, u32[]{:S(2)}, u32[]{:S(2)}) collective-permute-start(bf16[8,16,2048]{2,1,0:T(8,128)(2,1)S(1)} %collective-permute-done.3.refs_4_), channel_id=1, source_target_pairs={{0,8},{8,0},{16,24},{24,16},{32,40},{40,32},{48,56},{56,48},{64,72... | collective-permute-start | bytes 1572872 | tf_op jit(solution)/shard_map/ppermute | solution.py:370
  89.6 15.5 %collective-permute-start.2 = (bf16[8,16,2048]{2,1,0:T(8,128)(2,1)S(1)}, bf16[8,16,2048]{2,1,0:T(8,128)(2,1)S(1)}, u32[]{:S(2)}, u32[]{:S(2)}) collective-permute-start(bf16[8,16,2048]{2,1,0:T(8,128)(2,1)S(1)} %collective-permute-done.refs_1_), channel_id=1, source_target_pairs={{0,32},{1,33},{2,34},{3,35},{4,36},{5,37},{6,38},{7,39},{8,104},{9... | collective-permute-start | bytes 1572872 | tf_op jit(solution)/shard_map/ppermute | solution.py:365
  90.1 15.7 %collective-permute-start.5 = (bf16[8,16,2048]{2,1,0:T(8,128)(2,1)S(1)}, bf16[8,16,2048]{2,1,0:T(8,128)(2,1)S(1)}, u32[]{:S(2)}, u32[]{:S(2)}) collective-permute-start(bf16[8,16,2048]{2,1,0:T(8,128)(2,1)S(1)} %collective-permute-done.3.refs_4_), channel_id=1, source_target_pairs={{0,96},{1,97},{2,98},{3,99},{4,100},{5,101},{6,102},{7,103},{8,40}... | collective-permute-start | bytes 1572872 | tf_op jit(solution)/shard_map/ppermute | solution.py:365
  92.9 17.9 %collective-permute-start.4 = (bf16[8,16,2048]{2,1,0:T(8,128)(2,1)S(1)}, bf16[8,16,2048]{2,1,0:T(8,128)(2,1)S(1)}, u32[]{:S(2)}, u32[]{:S(2)}) collective-permute-start(bf16[8,16,2048]{2,1,0:T(8,128)(2,1)S(1)} %collective-permute-done.3.refs_4_), channel_id=1, source_target_pairs={{0,32},{1,33},{2,34},{3,35},{4,36},{5,37},{6,38},{7,39},{8,104},{9... | collective-permute-start | bytes 1572872 | tf_op jit(solution)/shard_map/ppermute | solution.py:365
  97.3 13.4 %collective-permute-start.9 = (bf16[8,16,2048]{2,1,0:T(8,128)(2,1)S(1)}, bf16[8,16,2048]{2,1,0:T(8,128)(2,1)S(1)}, u32[]{:S(2)}, u32[]{:S(2)}) collective-permute-start(bf16[8,16,2048]{2,1,0:T(8,128)(2,1)S(1)} %collective-permute-done.1.refs_2_), channel_id=1, source_target_pairs={{0,8},{8,0},{16,24},{24,16},{32,40},{40,32},{48,56},{56,48},{64,72... | collective-permute-start | bytes 1572872 | tf_op jit(solution)/shard_map/ppermute | solution.py:370
  97.3 13.9 %collective-permute-start.8 = (bf16[8,16,2048]{2,1,0:T(8,128)(2,1)S(1)}, bf16[8,16,2048]{2,1,0:T(8,128)(2,1)S(1)}, u32[]{:S(2)}, u32[]{:S(2)}) collective-permute-start(bf16[8,16,2048]{2,1,0:T(8,128)(2,1)S(1)} %collective-permute-done.refs_1_), channel_id=1, source_target_pairs={{0,8},{8,0},{16,24},{24,16},{32,40},{40,32},{48,56},{56,48},{64,72... | collective-permute-start | bytes 1572872 | tf_op jit(solution)/shard_map/ppermute | solution.py:370
  105.1 11.0 %collective-permute-start.6 = (bf16[8,16,2048]{2,1,0:T(8,128)(2,1)S(1)}, bf16[8,16,2048]{2,1,0:T(8,128)(2,1)S(1)}, u32[]{:S(2)}, u32[]{:S(2)}) collective-permute-start(bf16[8,16,2048]{2,1,0:T(8,128)(2,1)S(1)} %collective-permute-done.2.refs_3_), channel_id=1, source_target_pairs={{0,16},{8,24},{16,0},{24,8},{32,48},{40,56},{48,32},{56,40},{64,80... | collective-permute-start | bytes 1572872 | tf_op jit(solution)/shard_map/ppermute | solution.py:370
  105.8 10.4 %collective-permute-start.21 = (bf16[16,16,1024]{2,1,0:T(8,128)(2,1)S(1)}, bf16[16,16,1024]{2,1,0:T(8,128)(2,1)S(1)}, u32[]{:S(2)}, u32[]{:S(2)}) collective-permute-start(bf16[16,16,1024]{2,1,0:T(8,128)(2,1)S(1)} %collective-permute-done.19.refs_21_), channel_id=1, source_target_pairs={{0,1},{1,2},{2,3},{3,0},{4,5},{5,6},{6,7},{7,4},{8,11},{9,8},{10,9... | collective-permute-start | bytes 1572872 | tf_op jit(solution)/shard_map/ppermute | solution.py:365
  110.7 5.5 %collective-permute-start.10 = (bf16[8,16,2048]{2,1,0:T(8,128)(2,1)S(1)}, bf16[8,16,2048]{2,1,0:T(8,128)(2,1)S(1)}, u32[]{:S(2)}, u32[]{:S(2)}) collective-permute-start(bf16[8,16,2048]{2,1,0:T(8,128)(2,1)S(1)} %collective-permute-done.2.refs_3_), channel_id=1, source_target_pairs={{0,8},{8,0},{16,24},{24,16},{32,40},{40,32},{48,56},{56,48},{64,72... | collective-permute-start | bytes 1572872 | tf_op jit(solution)/shard_map/ppermute | solution.py:370
  110.7 5.5 %collective-permute-start.13 = (bf16[8,16,2048]{2,1,0:T(8,128)(2,1)S(1)}, bf16[8,16,2048]{2,1,0:T(8,128)(2,1)S(1)}, u32[]{:S(2)}, u32[]{:S(2)}) collective-permute-start(bf16[8,16,2048]{2,1,0:T(8,128)(2,1)S(1)} %collective-permute-done.5.refs_6_), channel_id=1, source_target_pairs={{0,8},{8,0},{16,24},{24,16},{32,40},{40,32},{48,56},{56,48},{64,72... | collective-permute-start | bytes 1572872 | tf_op jit(solution)/shard_map/ppermute | solution.py:370
  111.2 5.0 %collective-permute-start.12 = (bf16[8,16,2048]{2,1,0:T(8,128)(2,1)S(1)}, bf16[8,16,2048]{2,1,0:T(8,128)(2,1)S(1)}, u32[]{:S(2)}, u32[]{:S(2)}) collective-permute-start(bf16[8,16,2048]{2,1,0:T(8,128)(2,1)S(1)} %collective-permute-done.4.refs_5_), channel_id=1, source_target_pairs={{0,8},{8,0},{16,24},{24,16},{32,40},{40,32},{48,56},{56,48},{64,72... | collective-permute-start | bytes 1572872 | tf_op jit(solution)/shard_map/ppermute | solution.py:370
  116.1 1.9 %collective-permute-start.14 = (bf16[8,16,2048]{2,1,0:T(8,128)(2,1)S(1)}, bf16[8,16,2048]{2,1,0:T(8,128)(2,1)S(1)}, u32[]{:S(2)}, u32[]{:S(2)}) collective-permute-start(bf16[8,16,2048]{2,1,0:T(8,128)(2,1)S(1)} %collective-permute-done.6.refs_7_), channel_id=1, source_target_pairs={{0,8},{8,0},{16,24},{24,16},{32,40},{40,32},{48,56},{56,48},{64,72... | collective-permute-start | bytes 1572872 | tf_op jit(solution)/shard_map/ppermute | solution.py:370
